TPU v7x, 128 devices: a whole 4x4x4 slice. The times are simulated.
128 devices in a mesh: group: 16 (over y, x), hidden: 8 (over z, core).
Axes of the slice: x: 4, y: 4, z: 4, core: 2. Of those that a mesh axis runs over, the one named last changes fastest.
Arguments:
- queries: bfloat16 [6144, 4096], P('group', 'hidden'), may hold values from -16 to 16, as said below
- key_rows: bfloat16 [6144, 512], P('group'), may hold values from -16 to 16
- value_rows: bfloat16 [6144, 512], P('group'), may hold values from -6 to 6
- out_proj: bfloat16 [4096, 2048], P('hidden'), may hold values from -0.09375 to 0.09375
- residual: bfloat16 [6144, 2048], P('group'), may hold values from -120 to 120
- norm_gain: float32 [2048], replicated, may hold values from 0.1 to 1.9
- w_gate: bfloat16 [128, 2048, 768], P('group', None, 'hidden'), may hold values from -0.125 to 0.125
- w_up: bfloat16 [128, 2048, 768], P('group', None, 'hidden'), may hold values from -0.125 to 0.125
- w_down: bfloat16 [128, 768, 2048], P('group', 'hidden'), may hold values from -0.21875 to 0.21875
- route_slot: int32 [6144, 8], P('group'), may hold values from 0 to 15, all different within a row; in each aligned block of 384 rows (0 to 383, 384 to 767, ...) at most 240 rows name the same one
- route_weight: float32 [6144, 8], P('group'), may hold values from 0.05 to 0.3
- fetch_list: int32 [16, 16], replicated, may hold values from 0 to 127, as said below
- cotangent: bfloat16 [6144, 2048], P('group'), may hold values from -6 to 6
Outputs:
- layer_out: bfloat16 [6144, 2048], P('group', 'hidden')
- grad_normed: bfloat16 [6144, 2048], P('group', 'hidden')
- grad_gate: bfloat16 [128, 2048, 768], P('group', None, 'hidden')
- grad_up: bfloat16 [128, 2048, 768], P('group', None, 'hidden')
- grad_down: bfloat16 [128, 768, 2048], P('group', 'hidden')
Inputs may be any that keep to these rules, and one draw needn't show every extreme that they name: `queries`: queries and keys lie within the range. `route_slot`: within each group's 384 tokens no entry is named by more than 240 tokens, a bound that some block reaches; a token's 8 entries differ. `fetch_list`: entry f of every group's list is an expert owned by owner group f, that is an id from (f) * 8 to (f) * 8 + 7; the ids of one group's list differ.
All inputs are finite; a program needn't handle non-finite values.
Results may differ from a plain program's by a relative error of at most 0.017.
Values may be sent and summed in bfloat16 or wider, within the bound.
No kernel may reach another device: no remote copies, remote signals or barrier semaphores. Data moves between devices by JAX's collectives and lax.ppermute only.
A program may use at most 256 MiB of HBM per device.

v0:
```python
import math

import jax
import jax.numpy as jnp
from jax import lax
from jax.sharding import PartitionSpec as P

D = 2048
HEADS = 32
KV_HEADS = 4
HEAD_DIM = 128
EXP_GROUP = 8
FETCH = 16
CAP = 240


epsilon = 1e-06


def attention_rows(query_in, key_block, value_block, heads_here):
    tokens_here = query_in.shape[0]
    block_count = tokens_here // tokens_here
    query_blocks = query_in.reshape(block_count, tokens_here, heads_here, HEAD_DIM)
    col_pos = jnp.arange(tokens_here, dtype=jnp.int32)[None, :]

    def one_block(inputs):
        query_blk, first_row = inputs
        scores = jnp.einsum(
            "thd,sd->hts", query_blk, key_block, preferred_element_type=jnp.float32
        ) / math.sqrt(HEAD_DIM)
        row_pos = first_row + jnp.arange(tokens_here, dtype=jnp.int32)[:, None]
        scores = jnp.where(row_pos >= col_pos, scores, -1e30)
        row_peak = jnp.max(scores, axis=-1, keepdims=True)
        weights = jnp.exp(scores - row_peak)
        probabilities = (weights / jnp.sum(weights, axis=-1, keepdims=True)).astype(jnp.bfloat16)
        mixed = jnp.einsum(
            "hts,sd->thd", probabilities, value_block, preferred_element_type=jnp.float32
        )
        return mixed.astype(jnp.bfloat16)

    starts = jnp.arange(block_count, dtype=jnp.int32) * tokens_here
    mixed = lax.map(one_block, (query_blocks, starts))
    return mixed.reshape(tokens_here, heads_here * HEAD_DIM)


def route_table(slots, weights, fetch_count, capacity):
    tokens_here = slots.shape[0]
    slot_ids = jnp.arange(fetch_count, dtype=jnp.int32)
    chosen = slots[:, :, None] == slot_ids[None, None, :]
    slot_weight = jnp.sum(jnp.where(chosen, weights[:, :, None], 0.0), axis=1)
    is_used = jnp.any(chosen, axis=1)
    position = jnp.cumsum(is_used.astype(jnp.int32), axis=0) - 1
    target = jnp.where(is_used, slot_ids[None, :] * capacity + position, fetch_count * capacity)
    token_ids = jnp.broadcast_to(
        jnp.arange(tokens_here, dtype=jnp.int32)[:, None], (tokens_here, fetch_count)
    )
    rows = (
        jnp.zeros((fetch_count * capacity + 1,), jnp.int32)
        .at[target.reshape(-1)]
        .set(token_ids.reshape(-1))
    )
    row_weight = (
        jnp.zeros((fetch_count * capacity + 1,), weights.dtype)
        .at[target.reshape(-1)]
        .set(slot_weight.reshape(-1))
    )
    return (
        rows[:-1].reshape(fetch_count, capacity),
        row_weight[:-1].reshape(fetch_count, capacity),
    )


def shards(
    queries,
    key_rows,
    value_rows,
    out_proj,
    residual,
    norm_gain,
    w_gate,
    w_up,
    w_down,
    route_slot,
    route_weight,
    fetch_list,
    cotangent,
):
    tokens_here = queries.shape[0]
    hidden_index = lax.axis_index("hidden")
    hidden_count = lax.axis_size("hidden")
    heads_here = queries.shape[1] // HEAD_DIM
    kv_index = hidden_index * heads_here // (HEADS // KV_HEADS)
    key_block = lax.dynamic_slice_in_dim(key_rows, kv_index * HEAD_DIM, HEAD_DIM, 1)
    value_block = lax.dynamic_slice_in_dim(value_rows, kv_index * HEAD_DIM, HEAD_DIM, 1)
    mixed = attention_rows(queries, key_block, value_block, heads_here)
    partial_value = jnp.dot(mixed, out_proj, preferred_element_type=jnp.float32)
    share_width = D // hidden_count
    first_col = hidden_index * share_width
    attn_out = lax.psum(partial_value.astype(jnp.bfloat16), "hidden").astype(jnp.float32)
    stream = residual.astype(jnp.float32) + attn_out
    mean_square = jnp.mean(stream * stream, axis=-1, keepdims=True)
    normed = (stream * lax.rsqrt(mean_square + epsilon) * norm_gain).astype(jnp.bfloat16)
    stream_share = lax.dynamic_slice_in_dim(stream, first_col, share_width, 1)
    rows, row_weight = route_table(route_slot, route_weight, FETCH, CAP)
    group_index = lax.axis_index("group")
    group_count = lax.axis_size("group")
    per_owner = FETCH // group_count
    own_cols = lax.dynamic_slice_in_dim(fetch_list, group_index * per_owner, per_owner, 1)
    local_ids = (own_cols - group_index * EXP_GROUP).reshape(-1)
    fetched_gate, fetched_up, fetched_down = (
        lax.all_to_all(
            jnp.take(w_gate, local_ids, axis=0), "group", split_axis=0, concat_axis=0, tiled=True
        ),
        lax.all_to_all(
            jnp.take(w_up, local_ids, axis=0), "group", split_axis=0, concat_axis=0, tiled=True
        ),
        lax.all_to_all(
            jnp.take(w_down, local_ids, axis=0), "group", split_axis=0, concat_axis=0, tiled=True
        ),
    )
    routed_rows = normed[rows]
    routed_grad = (cotangent[rows].astype(jnp.float32) * row_weight[..., None]).astype(jnp.bfloat16)
    pre_gate = jnp.einsum(
        "fcd,fdh->fch", routed_rows, fetched_gate, preferred_element_type=jnp.float32
    )
    pre_up = jnp.einsum("fcd,fdh->fch", routed_rows, fetched_up, preferred_element_type=jnp.float32)
    sigmoid_gate = jax.nn.sigmoid(pre_gate)
    swish = pre_gate * sigmoid_gate
    activated = (swish * pre_up).astype(jnp.bfloat16)
    expert_out = jnp.einsum(
        "fch,fhd->fcd", activated, fetched_down, preferred_element_type=jnp.float32
    )
    flat_rows = rows.reshape(-1)
    out_part = (
        jnp.zeros((tokens_here, D), jnp.float32)
        .at[flat_rows]
        .add((expert_out * row_weight[..., None]).reshape(-1, D))
    )
    grad_down_part = jnp.einsum(
        "fch,fcd->fhd", activated, routed_grad, preferred_element_type=jnp.float32
    ).astype(jnp.bfloat16)
    d_act = jnp.einsum(
        "fcd,fhd->fch", routed_grad, fetched_down, preferred_element_type=jnp.float32
    )
    d_gate = (d_act * pre_up * sigmoid_gate * (1.0 + pre_gate * (1.0 - sigmoid_gate))).astype(
        jnp.bfloat16
    )
    d_up = (d_act * swish).astype(jnp.bfloat16)
    grad_gate_part = jnp.einsum(
        "fcd,fch->fdh", routed_rows, d_gate, preferred_element_type=jnp.float32
    ).astype(jnp.bfloat16)
    grad_up_part = jnp.einsum(
        "fcd,fch->fdh", routed_rows, d_up, preferred_element_type=jnp.float32
    ).astype(jnp.bfloat16)
    back_gate, back_up, back_down = (
        lax.all_to_all(grad_gate_part, "group", split_axis=0, concat_axis=0, tiled=True),
        lax.all_to_all(grad_up_part, "group", split_axis=0, concat_axis=0, tiled=True),
        lax.all_to_all(grad_down_part, "group", split_axis=0, concat_axis=0, tiled=True),
    )
    d_rows = jnp.einsum("fch,fdh->fcd", d_gate, fetched_gate, preferred_element_type=jnp.float32)
    d_rows = d_rows + jnp.einsum(
        "fch,fdh->fcd", d_up, fetched_up, preferred_element_type=jnp.float32
    )
    input_part = jnp.zeros((tokens_here, D), jnp.float32).at[flat_rows].add(d_rows.reshape(-1, D))
    out_share, input_share = (
        lax.psum_scatter(
            out_part.astype(jnp.bfloat16), "hidden", scatter_dimension=1, tiled=True
        ).astype(jnp.float32),
        lax.psum_scatter(
            input_part.astype(jnp.bfloat16), "hidden", scatter_dimension=1, tiled=True
        ).astype(jnp.float32),
    )
    owner_map = (local_ids[None, :] == jnp.arange(EXP_GROUP, dtype=jnp.int32)[:, None]).astype(
        jnp.bfloat16
    )
    grad_gate = jnp.einsum(
        "ls,sdh->ldh", owner_map, back_gate, preferred_element_type=jnp.float32
    ).astype(jnp.bfloat16)
    grad_up = jnp.einsum(
        "ls,sdh->ldh", owner_map, back_up, preferred_element_type=jnp.float32
    ).astype(jnp.bfloat16)
    grad_down = jnp.einsum(
        "ls,shd->lhd", owner_map, back_down, preferred_element_type=jnp.float32
    ).astype(jnp.bfloat16)
    layer_out = (stream_share + out_share).astype(jnp.bfloat16)
    return (layer_out, input_share.astype(jnp.bfloat16), grad_gate, grad_up, grad_down)


def solution(mesh):
    return jax.shard_map(
        shards,
        mesh=mesh,
        in_specs=(
            P("group", "hidden"),
            P("group", None),
            P("group", None),
            P("hidden", None),
            P("group", None),
            P(),
            P("group", None, "hidden"),
            P("group", None, "hidden"),
            P("group", "hidden", None),
            P("group", None),
            P("group", None),
            P(),
            P("group", None),
        ),
        out_specs=(
            P("group", "hidden"),
            P("group", "hidden"),
            P("group", None, "hidden"),
            P("group", None, "hidden"),
            P("group", "hidden", None),
        ),
        check_vma=False,
    )
```

profile of v0, /device:TPU:6, one launch (start us, length us, event | category | flops | bytes accessed | tf_op | source)
XLA Modules:
  0.0 663.6 jit_solution(3105727596796394096)
XLA Ops:
  9.1 3.6 gather_fusion.4
  12.7 5.5 gather_fusion.3
  18.2 8.3 %broadcast_select_fusion.1 = (bf16[16,2048,96]{1,2,0:T(8,128)(2,1)S(1)}, bf16[16,2048,96]{1,2,0:T(8,128)(2,1)}) fusion(bf16[16,2048,96]{1,2,0:T(8,128)(2,1)} %gather_fusion.3, pred[16]{0:T(512)(128)(4,1)S(1)} %compare_and_fusion, bf16[16,2048,96]{1,2,0:T(8,128)(2,1)} %gather_fusion.4), kind=kLoop, calls=%fused_computation.23 | loop fusion | flops 6291456 | bytes 25165840 | tf_op jit(solution)/shard_map/jit(_take)/select_n | solution.py:112
  26.5 78.0 %all_to_all.30 = bf16[16,2048,96]{1,2,0:T(8,128)(2,1)} all-to-all(bf16[16,2048,96]{1,2,0:T(8,128)(2,1)S(1)} %get-tuple-element.53), channel_id=1, replica_groups=mesh['group'=16,'hidden'=8] {'group'}, dimensions={0} | all-to-all | bytes 12582912 | tf_op jit(solution)/shard_map/all_to_all | solution.py:111
  104.5 7.2 %all-to-all-start.1 = ((bf16[16,2048,96]{1,2,0:T(8,128)(2,1)}), bf16[16,2048,96]{1,2,0:T(8,128)(2,1)}, u32[]{:S(2)}, u32[]{:S(2)}) async-start(bf16[16,2048,96]{1,2,0:T(8,128)(2,1)} %get-tuple-element.54), calls=%async_computation.1 | async-start | bytes 12582912 | tf_op jit(solution)/shard_map/all_to_all | solution.py:114
  121.2 3.6 gather_fusion.1
  125.1 6.1 broadcast_select_fusion.2
  131.2 70.2 %all-to-all-done.1 = bf16[16,2048,96]{1,2,0:T(8,128)(2,1)} async-done(((bf16[16,2048,96]{1,2,0:T(8,128)(2,1)}), bf16[16,2048,96]{1,2,0:T(8,128)(2,1)}, u32[]{:S(2)}, u32[]{:S(2)}) %all-to-all-start.1) | async-done | bytes 6291488 | tf_op jit(solution)/shard_map/all_to_all | solution.py:114
  201.4 6.8 %all-to-all-start.2 = ((bf16[16,96,2048]{2,1,0:T(8,128)(2,1)}), bf16[16,96,2048]{2,1,0:T(8,128)(2,1)}, u32[]{:S(2)}, u32[]{:S(2)}) async-start(bf16[16,96,2048]{2,1,0:T(8,128)(2,1)} %broadcast_select_fusion.2), calls=%async_computation.2 | async-start | bytes 12582912 | tf_op jit(solution)/shard_map/all_to_all | solution.py:117
  208.6 23.0 %scatter_custom_fusion.1 = f32[3841]{0:T(1024)S(1)} fusion(s32[6144]{0:T(1024)S(1)} %bitcast.104, f32[6144]{0:T(1024)S(1)} %reshape.201, f32[]{:T(128)} %constant.66.clone.1), kind=kCustom, calls=%fused_computation.78 | custom fusion | bytes 15368 | tf_op jit(solution)/shard_map/scatter | solution.py:65
  231.8 23.2 %scatter_custom_fusion = s32[3841]{0:T(1024)S(1)} fusion(s32[6144]{0:T(1024)S(1)} %bitcast.105, s32[6144]{0:T(1024)S(1)} %reshape.193, s32[]{:T(128)} %constant.38.clone.1), kind=kCustom, calls=%fused_computation.81 | custom fusion | bytes 15368 | tf_op jit(solution)/shard_map/scatter | solution.py:60
  255.8 15.6 %gather_fusion.2 = bf16[3840,2048]{1,0:T(8,128)(2,1)} fusion(bf16[384,2048]{1,0:T(8,128)(2,1)S(1)} %copy-done.2, s32[4096]{0:T(1024)S(1)} %pad_clamp_fusion), kind=kCustom, calls=%fused_computation.4 | custom fusion | bytes 31472640 | tf_op jit(solution)/shard_map/gather | solution.py:122
  271.4 3.7 convert_add_fusion
  275.9 15.4 %gather_fusion = bf16[3840,2048]{1,0:T(8,128)(2,1)} fusion(bf16[384,2048]{1,0:T(8,128)(2,1)S(1)} %multiply_convert_fusion, s32[4096]{0:T(1024)S(1)} %pad_clamp_fusion), kind=kCustom, calls=%fused_computation.2 | custom fusion | bytes 31472640 | tf_op jit(solution)/shard_map/gather | solution.py:121
  291.3 9.8 %fusion.81 = f32[16,240,96]{1,2,0:T(8,128)S(1)} fusion(bf16[16,240,2048]{2,1,0:T(8,128)(2,1)} %bitcast.94, bf16[16,2048,96]{1,2,0:T(8,128)(2,1)} %all-to-all-done.1), kind=kOutput, calls=%fused_computation.105 | convolution fusion | flops 1509949440 | bytes 23494656 | tf_op jit(solution)/shard_map/fcd,fdh->fch/dot_general | solution.py:126
  301.2 11.0 %fusion.80 = f32[16,240,96]{1,2,0:T(8,128)} fusion(bf16[16,240,2048]{2,1,0:T(8,128)(2,1)} %bitcast.95, bf16[16,2048,96]{1,2,0:T(8,128)(2,1)} %all_to_all.30), kind=kOutput, calls=%fused_computation.104 | convolution fusion | flops 1509949440 | bytes 23494656 | tf_op jit(solution)/shard_map/fcd,fdh->fch/dot_general | solution.py:123
  312.1 12.7 %multiply_convert_fusion.1 = (bf16[16,240,96]{1,2,0:T(8,128)(2,1)}, bf16[16,240,96]{1,2,0:T(8,128)(2,1)S(1)}, bf16[16,240,96]{1,2,0:T(8,128)(2,1)S(1)}) fusion(f32[16,240,96]{1,2,0:T(8,128)} %fusion.80, f32[16,240,96]{1,2,0:T(8,128)S(1)} %fusion.81, bf16[16,96,2048]{2,1,0:T(8,128)(2,1)} %all-to-all-done.2, bf16[16,240,2048]{2,1,0:T(8,128)(2,1)} %bitcast.98, ...), kind=kOutput, calls=%fused_computation.39 | convolution fusion | flops 1539072000 | bytes 27196416 | tf_op jit(solution)/shard_map/fcd,fhd->fch/dot_general | solution.py:142
  324.8 9.4 %fusion.12 = bf16[16,96,2048]{2,1,0:T(8,128)(2,1)} fusion(bf16[16,240,96]{1,2,0:T(8,128)(2,1)S(1)} %get-tuple-element.48, bf16[16,240,2048]{2,1,0:T(8,128)(2,1)} %bitcast.99, f32[16,240]{1,0:T(8,128)S(1)} %mul.89), kind=kOutput, calls=%fused_computation.25 | convolution fusion | flops 1536688128 | bytes 22772736 | tf_op jit(solution)/shard_map/fch,fcd->fhd/dot_general | solution.py:139
  334.2 7.8 %all-to-all-start.5 = ((bf16[16,96,2048]{2,1,0:T(8,128)(2,1)}), bf16[16,96,2048]{2,1,0:T(8,128)(2,1)}, u32[]{:S(2)}, u32[]{:S(2)}) async-start(bf16[16,96,2048]{2,1,0:T(8,128)(2,1)} %fusion.12), calls=%async_computation.7 | async-start | bytes 12582912 | tf_op jit(solution)/shard_map/all_to_all | solution.py:158
  342.1 10.9 %convolution_convert_fusion.1 = bf16[16,2048,96]{1,2,0:T(8,128)(2,1)} fusion(bf16[16,240,96]{1,2,0:T(8,128)(2,1)S(1)} %get-tuple-element.47, bf16[16,240,2048]{2,1,0:T(8,128)(2,1)} %bitcast.96), kind=kOutput, calls=%fused_computation.27 | convolution fusion | flops 1513095168 | bytes 22757376 | tf_op jit(solution)/shard_map/fcd,fch->fdh/dot_general | solution.py:149
  353.0 73.0 %all-to-all-done.5 = bf16[16,96,2048]{2,1,0:T(8,128)(2,1)} async-done(((bf16[16,96,2048]{2,1,0:T(8,128)(2,1)}), bf16[16,96,2048]{2,1,0:T(8,128)(2,1)}, u32[]{:S(2)}, u32[]{:S(2)}) %all-to-all-start.5) | async-done | bytes 6291488 | tf_op jit(solution)/shard_map/all_to_all | solution.py:158
  426.0 8.4 %all-to-all-start.3 = ((bf16[16,2048,96]{1,2,0:T(8,128)(2,1)}), bf16[16,2048,96]{1,2,0:T(8,128)(2,1)}, u32[]{:S(2)}, u32[]{:S(2)}) async-start(bf16[16,2048,96]{1,2,0:T(8,128)(2,1)} %convolution_convert_fusion.1), calls=%async_computation.5 | async-start | bytes 12582912 | tf_op jit(solution)/shard_map/all_to_all | solution.py:156
  434.4 15.4 %convolution_multiply_fusion = f32[16,240,2048]{2,1,0:T(8,128)} fusion(bf16[16,240,96]{1,2,0:T(8,128)(2,1)S(1)} %get-tuple-element.48, bf16[16,96,2048]{2,1,0:T(8,128)(2,1)} %all-to-all-done.2, f32[16,240]{1,0:T(8,128)S(1)} %mul.89), kind=kOutput, calls=%fused_computation.13 | convolution fusion | flops 1517813760 | bytes 38501376 | tf_op jit(solution)/shard_map/fch,fhd->fcd/dot_general | solution.py:130
  449.8 53.0 %scatter_custom_fusion.2 = f32[384,2048]{1,0:T(8,128)S(1)} fusion(s32[3840]{0:T(1024)} %get-tuple-element.52, f32[3840,2048]{1,0:T(8,128)} %bitcast.100, f32[]{:T(128)} %constant.66.clone.1), kind=kCustom, calls=%fused_computation.46 | custom fusion | flops 7864320 | bytes 3146240 | tf_op jit(solution)/shard_map/scatter-add | solution.py:137
  504.3 11.1 %convolution_convert_fusion = bf16[16,2048,96]{1,2,0:T(8,128)(2,1)} fusion(bf16[16,240,96]{1,2,0:T(8,128)(2,1)} %get-tuple-element.46, bf16[16,240,2048]{2,1,0:T(8,128)(2,1)} %bitcast.97), kind=kOutput, calls=%fused_computation.26 | convolution fusion | flops 1513095168 | bytes 22757376 | tf_op jit(solution)/shard_map/fcd,fch->fdh/dot_general | solution.py:152
  515.4 15.5 %fusion.82 = f32[16,240,2048]{2,1,0:T(8,128)} fusion(bf16[16,240,96]{1,2,0:T(8,128)(2,1)S(1)} %copy-done.5, bf16[16,2048,96]{1,2,0:T(8,128)(2,1)} %all_to_all.30), kind=kOutput, calls=%fused_computation.106 | convolution fusion | flops 1509949440 | bytes 38486016 | tf_op jit(solution)/shard_map/fch,fdh->fcd/dot_general | solution.py:160
  530.9 7.4 %all-to-all-start.4 = ((bf16[16,2048,96]{1,2,0:T(8,128)(2,1)}), bf16[16,2048,96]{1,2,0:T(8,128)(2,1)}, u32[]{:S(2)}, u32[]{:S(2)}) async-start(bf16[16,2048,96]{1,2,0:T(8,128)(2,1)} %convolution_convert_fusion), calls=%async_computation.6 | async-start | bytes 12582912 | tf_op jit(solution)/shard_map/all_to_all | solution.py:157
  538.3 22.4 %convolution_add_fusion = f32[16,240,2048]{2,1,0:T(8,128)} fusion(f32[16,240,2048]{2,1,0:T(8,128)} %fusion.82, bf16[16,240,96]{1,2,0:T(8,128)(2,1)S(1)} %copy-done.8, bf16[16,2048,96]{1,2,0:T(8,128)(2,1)} %all-to-all-done.1), kind=kOutput, calls=%fused_computation.12 | convolution fusion | flops 1517813760 | bytes 69943296 | tf_op jit(solution)/shard_map/fch,fdh->fcd/dot_general | solution.py:161
  560.7 53.3 %scatter_custom_fusion.3 = f32[384,2048]{1,0:T(8,128)S(1)} fusion(s32[3840]{0:T(1024)} %get-tuple-element.52, f32[3840,2048]{1,0:T(8,128)} %bitcast.101, f32[]{:T(128)} %constant.66.clone.1), kind=kCustom, calls=%fused_computation.44 | custom fusion | flops 7864320 | bytes 3146240 | tf_op jit(solution)/shard_map/scatter-add | solution.py:164
  617.2 9.6 %fusion.21 = bf16[8,96,2048]{2,0,1:T(8,128)(2,1)S(1)} fusion(bf16[16,96,2048]{2,1,0:T(8,128)(2,1)} %all-to-all-done.5, s32[16]{0:T(128)S(1)} %copy-done.15), kind=kOutput, calls=%fused_computation.30 | convolution fusion | flops 51904640 | bytes 9437248 | tf_op jit(solution)/shard_map/ls,shd->lhd/dot_general | solution.py:182
  630.2 9.9 %fusion.15 = bf16[8,2048,96]{1,0,2:T(8,128)(2,1)S(1)} fusion(bf16[16,2048,96]{1,2,0:T(8,128)(2,1)} %all-to-all-done.3, s32[16]{0:T(128)S(1)} %copy-done.15), kind=kOutput, calls=%fused_computation.28 | convolution fusion | flops 51904640 | bytes 9437248 | tf_op jit(solution)/shard_map/ls,sdh->ldh/dot_general | solution.py:176
  643.5 9.9 %fusion.18 = bf16[8,2048,96]{1,0,2:T(8,128)(2,1)S(1)} fusion(bf16[16,2048,96]{1,2,0:T(8,128)(2,1)} %all-to-all-done.4, s32[16]{0:T(128)S(1)} %copy-done.15), kind=kOutput, calls=%fused_computation.29 | convolution fusion | flops 51904640 | bytes 9437248 | tf_op jit(solution)/shard_map/ls,sdh->ldh/dot_general | solution.py:179
  (85 shorter events, 28.4 us)
Async XLA Ops:
  7.2 1.9 copy-start
  8.2 0.6 copy-start.14
  104.5 7.4 %copy-start.16 = (bf16[384,512]{1,0:T(8,128)(2,1)S(1)}, bf16[384,512]{1,0:T(8,128)(2,1)}, u32[]{:S(2)}) copy-start(bf16[384,512]{1,0:T(8,128)(2,1)} %param.15) | copy-start | bytes 1179652
  104.5 96.8 %all-to-all-start.1 = ((bf16[16,2048,96]{1,2,0:T(8,128)(2,1)}), bf16[16,2048,96]{1,2,0:T(8,128)(2,1)}, u32[]{:S(2)}, u32[]{:S(2)}) async-start(bf16[16,2048,96]{1,2,0:T(8,128)(2,1)} %get-tuple-element.54), calls=%async_computation.1 | async-start | bytes 12582912 | tf_op jit(solution)/shard_map/all_to_all | solution.py:114
  111.8 159.6 %all-reduce.2.cloned.1.call-start = ((), (), s32[]{:S(2)}) async-start(), calls=%async_computation.8 | async-start | bytes 3145728 | tf_op jit(solution)/shard_map/psum | solution.py:99
  115.1 2.4 copy-start.9
  115.1 4.5 copy-start.10
  115.1 6.1 copy-start.3
  121.2 3.6 copy-start.11
  131.2 77.1 %copy-start.12 = (f32[384,8]{0,1:T(8,128)S(1)}, f32[384,8]{0,1:T(8,128)}, u32[]{:S(2)}) copy-start(f32[384,8]{0,1:T(8,128)} %param.25) | copy-start | bytes 36868
  131.2 124.6 %copy-start.2 = (bf16[384,2048]{1,0:T(8,128)(2,1)S(1)}, bf16[384,2048]{1,0:T(8,128)(2,1)}, u32[]{:S(2)}) copy-start(bf16[384,2048]{1,0:T(8,128)(2,1)} %param.27) | copy-start | bytes 4718596
  201.4 110.8 %all-to-all-start.2 = ((bf16[16,96,2048]{2,1,0:T(8,128)(2,1)}), bf16[16,96,2048]{2,1,0:T(8,128)(2,1)}, u32[]{:S(2)}, u32[]{:S(2)}) async-start(bf16[16,96,2048]{2,1,0:T(8,128)(2,1)} %broadcast_select_fusion.2), calls=%async_computation.2 | async-start | bytes 12582912 | tf_op jit(solution)/shard_map/all_to_all | solution.py:117
  255.8 15.6 %copy-start.6 = (bf16[384,2048]{1,0:T(8,128)(2,1)S(1)}, bf16[384,2048]{1,0:T(8,128)(2,1)}, u32[]{:S(2)}) copy-start(bf16[384,2048]{1,0:T(8,128)(2,1)} %param.19) | copy-start | bytes 4718596
  271.4 3.7 copy-start.13
  271.4 3.7 copy-start.7
  324.8 17.3 %copy-start.4 = (bf16[16,240,96]{1,2,0:T(8,128)(2,1)}, bf16[16,240,96]{1,2,0:T(8,128)(2,1)S(1)}, u32[]{:S(2)}) copy-start(bf16[16,240,96]{1,2,0:T(8,128)(2,1)S(1)} %get-tuple-element.47) | copy-start | bytes 2211844
  334.2 91.7 %all-to-all-start.5 = ((bf16[16,96,2048]{2,1,0:T(8,128)(2,1)}), bf16[16,96,2048]{2,1,0:T(8,128)(2,1)}, u32[]{:S(2)}, u32[]{:S(2)}) async-start(bf16[16,96,2048]{2,1,0:T(8,128)(2,1)} %fusion.12), calls=%async_computation.7 | async-start | bytes 12582912 | tf_op jit(solution)/shard_map/all_to_all | solution.py:158
  426.0 104.9 %all-to-all-start.3 = ((bf16[16,2048,96]{1,2,0:T(8,128)(2,1)}), bf16[16,2048,96]{1,2,0:T(8,128)(2,1)}, u32[]{:S(2)}, u32[]{:S(2)}) async-start(bf16[16,2048,96]{1,2,0:T(8,128)(2,1)} %convolution_convert_fusion.1), calls=%async_computation.5 | async-start | bytes 12582912 | tf_op jit(solution)/shard_map/all_to_all | solution.py:156
  434.4 181.0 %reduce-scatter.3.cloned.1.call-start = ((), (), s32[]{:S(2)}) async-start(), calls=%async_computation.9 | async-start | bytes 1769472 | tf_op jit(solution)/shard_map/reduce_scatter | solution.py:166
  504.3 11.1 %copy-start.5 = (bf16[16,240,96]{1,2,0:T(8,128)(2,1)S(1)}, bf16[16,240,96]{1,2,0:T(8,128)(2,1)}, u32[]{:S(2)}) copy-start(bf16[16,240,96]{1,2,0:T(8,128)(2,1)} %copy-done.4) | copy-start | bytes 2211844
  530.8 7.4 %copy-start.8 = (bf16[16,240,96]{1,2,0:T(8,128)(2,1)S(1)}, bf16[16,240,96]{1,2,0:T(8,128)(2,1)}, u32[]{:S(2)}) copy-start(bf16[16,240,96]{1,2,0:T(8,128)(2,1)} %get-tuple-element.46) | copy-start | bytes 2211844
  530.9 112.7 %all-to-all-start.4 = ((bf16[16,2048,96]{1,2,0:T(8,128)(2,1)}), bf16[16,2048,96]{1,2,0:T(8,128)(2,1)}, u32[]{:S(2)}, u32[]{:S(2)}) async-start(bf16[16,2048,96]{1,2,0:T(8,128)(2,1)} %convolution_convert_fusion), calls=%async_computation.6 | async-start | bytes 12582912 | tf_op jit(solution)/shard_map/all_to_all | solution.py:157
  538.2 118.6 %reduce-scatter.5.cloned.1.call-start = ((), (), s32[]{:S(2)}) async-start(), calls=%async_computation.10 | async-start | bytes 1769472 | tf_op jit(solution)/shard_map/reduce_scatter | solution.py:169
  560.7 56.5 %copy-start.15 = (s32[16]{0:T(128)S(1)}, s32[16]{0:T(128)}, u32[]{:S(2)}) copy-start(s32[16]{0:T(128)} %copy-done.14) | copy-start | bytes 196
  640.1 16.7 %copy-start.1 = (bf16[8,2048,96]{1,2,0:T(8,128)(2,1)S(1)}, bf16[8,2048,96]{1,2,0:T(8,128)(2,1)}, u32[]{:S(2)}) copy-start(bf16[8,2048,96]{1,2,0:T(8,128)(2,1)} %param.22) | copy-start | bytes 9437188
Sparse Core Ops, SparseCore 0:
  119.8 67.9 all-reduce.1
  504.4 35.0 reduce-scatter.2
  615.5 35.0 reduce-scatter.4
where the time goes:
time: 671 us; the launch traced here: 664 us
  matrix products  155 us (23%)
  waiting for transfers between devices  143 us (21%)
  other arithmetic  133 us (20%)
  local copies, waits for them, and re-layouts  102 us (15%)
  blocking collectives  78 us (12%)
  starting transfers between devices  37.8 us (6%)
  between operations  14.3 us (2%)
    all_to_all x1, blocking collectives, shards(): lax.all_to_all(jnp.take(w_gate, local_ids, axis=0), 'group', split_axis=0...  78 us
    all_to_all x1, waiting for transfers between devices, shards(): lax.all_to_all(grad_down_part, 'group', split_axis=0, concat_axis=0, tile...  73 us
    all_to_all x1, waiting for transfers between devices, shards(): lax.all_to_all(jnp.take(w_up, local_ids, axis=0), 'group', split_axis=0,...  70.2 us
    scatter-add x1, other arithmetic, shards(): jnp.zeros((tokens_here, D), jnp.float32).at[flat_rows]  53.3 us
    scatter-add x1, other arithmetic, shards(): out_part = jnp.zeros((tokens_here, D), jnp.float32).at[flat_rows].add((ex...  53 us
    scatter x1, local copies, waits for them, and re-layouts, route_table(): rows = jnp.zeros((fetch_count * capacity + 1,), jnp.int32).at[target.resh...  23.2 us
    scatter x1, local copies, waits for them, and re-layouts, route_table(): row_weight = jnp.zeros((fetch_count * capacity + 1,), weights.dtype).at[t...  23 us
    dot_general x1, matrix products, shards(): jnp.einsum('fch,fdh->fcd', d_up, fetched_up, preferred_element_type=jnp.f...  22.4 us
  transfers between devices with their start and end apart: 8, of which 2 were waited for; matrix products, arithmetic and copies ran while one was open for 53% of the time, Pallas kernels for 0%

commit v1 on v0

v1 whole, which is shorter than its diff:
```python
import math

import jax
import jax.numpy as jnp
from jax import lax
from jax.experimental import pallas as pl
from jax.experimental.pallas import tpu as pltpu
from jax.sharding import PartitionSpec as P

D = 2048
HEADS = 32
KV_HEADS = 4
HEAD_DIM = 128
EXP_GROUP = 8
FETCH = 16
CAP = 240
UNITS = 96
PAD = 128
COLS = 256
HALF = 1024
STEPS = FETCH + EXP_GROUP

epsilon = 1e-06
bf16 = jnp.bfloat16
f32 = jnp.float32

NT = (((1,), (1,)), ((), ()))
NN = (((1,), (0,)), ((), ()))
TN = (((0,), (0,)), ((), ()))


def mm(a, b, dims):
    return lax.dot_general(a, b, dims, preferred_element_type=f32)


def attention(queries, key_block, value_block):
    tokens = queries.shape[0]
    heads = queries.shape[1] // HEAD_DIM
    query = queries.reshape(tokens, heads, HEAD_DIM)
    scores = jnp.einsum("thd,sd->hts", query, key_block, preferred_element_type=f32)
    scores = scores / math.sqrt(HEAD_DIM)
    row_pos = lax.broadcasted_iota(jnp.int32, (tokens, tokens), 0)
    col_pos = lax.broadcasted_iota(jnp.int32, (tokens, tokens), 1)
    scores = jnp.where(row_pos >= col_pos, scores, -1e30)
    weights = jnp.exp(scores - jnp.max(scores, axis=-1, keepdims=True))
    probs = (weights / jnp.sum(weights, axis=-1, keepdims=True)).astype(bf16)
    mixed = jnp.einsum("hts,sd->thd", probs, value_block, preferred_element_type=f32)
    return mixed.astype(bf16).reshape(tokens, heads * HEAD_DIM)


def rows_kernel(
    expert_ref, core_ref, x_ref, g_own_ref, g_oth_ref, wg_ref, wu_ref, wd_ref,
    out_ref, d_own_ref, d_oth_ref, act_ref, dgu_ref, wgu, wdp,
):
    core = core_ref[0]

    @pl.when(pl.program_id(0) == 0)
    def _():
        zeros = jnp.zeros((PAD - UNITS, D), bf16)
        wgu[UNITS:PAD, :] = zeros
        wgu[PAD + UNITS :, :] = zeros
        wdp[UNITS:, :] = zeros

    wgu[:UNITS, :] = wg_ref[0]
    wgu[PAD : PAD + UNITS, :] = wu_ref[0]
    wdp[:UNITS, :] = wd_ref[0]

    pre = jnp.zeros((CAP, 2 * PAD), f32)
    for block in range(D // COLS):
        pre = pre + mm(x_ref[block, 0], wgu[:, block * COLS : (block + 1) * COLS], NT)
    own = pl.multiple_of(core * HALF, HALF)
    oth = pl.multiple_of(HALF - core * HALF, HALF)
    d_act = mm(g_own_ref[0], wdp[:, pl.ds(own, HALF)], NT) + mm(
        g_oth_ref[0], wdp[:, pl.ds(oth, HALF)], NT
    )
    gate, up = pre[:, :PAD], pre[:, PAD:]
    sig = jax.nn.sigmoid(gate)
    swish = gate * sig
    act = (swish * up).astype(bf16)
    d_gate = (d_act * up * sig * (1.0 + gate * (1.0 - sig))).astype(bf16)
    d_up = (d_act * swish).astype(bf16)
    act_ref[0] = act
    dgu_ref[0, :, :PAD] = d_gate
    dgu_ref[0, :, PAD:] = d_up
    for block in range(D // COLS):
        out_ref[block, 0] = mm(act, wdp[:, block * COLS : (block + 1) * COLS], NN).astype(bf16)
    d_gu = dgu_ref[0]
    for block in range(4):
        place = slice(block * COLS, (block + 1) * COLS)
        col = pl.multiple_of((2 * block + core) * COLS, COLS)
        d_own_ref[0, :, place] = mm(d_gu, wgu[:, pl.ds(col, COLS)], NN).astype(bf16)
        col = pl.multiple_of((2 * block + 1 - core) * COLS, COLS)
        d_oth_ref[0, :, place] = mm(d_gu, wgu[:, pl.ds(col, COLS)], NN).astype(bf16)


def rows_call(experts, core, x_rows, g_own, g_oth, wg, wu, wd):
    weight = pl.BlockSpec((1, UNITS, D), lambda i, e, c: (e[i], 0, 0))
    cols8 = pl.BlockSpec((8, 1, CAP, COLS), lambda i, e, c: (0, i, 0, 0))
    half = pl.BlockSpec((1, CAP, HALF), lambda i, e, c: (i, 0, 0))
    return pl.pallas_call(
        rows_kernel,
        grid_spec=pltpu.PrefetchScalarGridSpec(
            num_scalar_prefetch=2,
            grid=(FETCH,),
            in_specs=[cols8, half, half, weight, weight, weight],
            out_specs=[
                cols8,
                half,
                half,
                pl.BlockSpec((1, CAP, PAD), lambda i, e, c: (i, 0, 0)),
                pl.BlockSpec((1, CAP, 2 * PAD), lambda i, e, c: (i, 0, 0)),
            ],
            scratch_shapes=[pltpu.VMEM((2 * PAD, D), bf16), pltpu.VMEM((PAD, D), bf16)],
        ),
        out_shape=[
            jax.ShapeDtypeStruct((8, FETCH, CAP, COLS), bf16),
            jax.ShapeDtypeStruct((FETCH, CAP, HALF), bf16),
            jax.ShapeDtypeStruct((FETCH, CAP, HALF), bf16),
            jax.ShapeDtypeStruct((FETCH, CAP, PAD), bf16),
            jax.ShapeDtypeStruct((FETCH, CAP, 2 * PAD), bf16),
        ],
        compiler_params=pltpu.CompilerParams(vmem_limit_bytes=48 << 20),
        cost_estimate=pl.CostEstimate(
            flops=2 * 6 * FETCH * CAP * D * PAD, bytes_accessed=85 << 20, transcendentals=0
        ),
        name="expert_rows",
    )(experts, core, x_rows, g_own, g_oth, wg, wu, wd)


def grads_kernel(
    chunk_ref, expert_ref, real_ref, last_ref, core_ref, x_ref, g_own_ref, g_oth_ref,
    act_ref, dgu_ref, gg_ref, gu_ref, gd_ref, acc_gu, acc_d,
):
    step = pl.program_id(0)
    core = core_ref[0]

    @pl.when(real_ref[step] == 0)
    def _():
        acc_gu[...] = jnp.zeros_like(acc_gu)
        acc_d[...] = jnp.zeros_like(acc_d)

    @pl.when(real_ref[step] == 1)
    def _():
        d_gu, act = dgu_ref[0], act_ref[0]
        for block in range(D // COLS):
            place = slice(block * COLS, (block + 1) * COLS)
            acc_gu[:, place] += mm(d_gu, x_ref[block, 0], TN)
        for block in range(HALF // COLS):
            place = slice(block * COLS, (block + 1) * COLS)
            col = pl.multiple_of(core * HALF + block * COLS, COLS)
            acc_d[:, pl.ds(col, COLS)] += mm(act, g_own_ref[0, :, place], TN)
            col = pl.multiple_of(HALF - core * HALF + block * COLS, COLS)
            acc_d[:, pl.ds(col, COLS)] += mm(act, g_oth_ref[0, :, place], TN)

    @pl.when(last_ref[step] == 1)
    def _():
        gg_ref[0] = acc_gu[:UNITS, :].astype(bf16)
        gu_ref[0] = acc_gu[PAD : PAD + UNITS, :].astype(bf16)
        gd_ref[0] = acc_d[:UNITS, :].astype(bf16)


def grads_call(chunk, expert, real, last, core, x_rows, g_own, g_oth, act, dgu):
    weight = pl.BlockSpec((1, UNITS, D), lambda i, k, e, r, l, c: (e[i], 0, 0))
    half = pl.BlockSpec((1, CAP, HALF), lambda i, k, e, r, l, c: (k[i], 0, 0))
    return pl.pallas_call(
        grads_kernel,
        grid_spec=pltpu.PrefetchScalarGridSpec(
            num_scalar_prefetch=5,
            grid=(STEPS,),
            in_specs=[
                pl.BlockSpec((8, 1, CAP, COLS), lambda i, k, e, r, l, c: (0, k[i], 0, 0)),
                half,
                half,
                pl.BlockSpec((1, CAP, PAD), lambda i, k, e, r, l, c: (k[i], 0, 0)),
                pl.BlockSpec((1, CAP, 2 * PAD), lambda i, k, e, r, l, c: (k[i], 0, 0)),
            ],
            out_specs=[weight, weight, weight],
            scratch_shapes=[pltpu.VMEM((2 * PAD, D), f32), pltpu.VMEM((PAD, D), f32)],
        ),
        out_shape=[jax.ShapeDtypeStruct((EXP_GROUP, UNITS, D), bf16)] * 3,
        compiler_params=pltpu.CompilerParams(vmem_limit_bytes=48 << 20),
        cost_estimate=pl.CostEstimate(
            flops=2 * 3 * FETCH * CAP * D * PAD, bytes_accessed=45 << 20, transcendentals=0
        ),
        name="weight_grads",
    )(chunk, expert, real, last, core, x_rows, g_own, g_oth, act, dgu)


def grad_order(experts):
    ids = jnp.arange(FETCH, dtype=jnp.int32)
    own = jnp.arange(EXP_GROUP, dtype=jnp.int32)
    listed = experts[None, :] == own[:, None]
    first = jnp.min(jnp.where(listed, ids[None, :], FETCH), axis=1)
    first = jnp.where(first == FETCH, 0, first)
    key = jnp.concatenate([own * 32, experts * 32 + 1 + ids])
    chunk = jnp.concatenate([first, ids])
    owner = jnp.concatenate([own, experts])
    rank = jnp.sum((key[None, :] < key[:, None]).astype(jnp.int32), axis=1)
    place = rank[:, None] == jnp.arange(STEPS, dtype=jnp.int32)[None, :]

    def ordered(values):
        return jnp.sum(jnp.where(place, values[:, None], 0), axis=0)

    count = jnp.sum((owner[None, :] == owner[:, None]) & (key[None, :] > key[:, None]), axis=1)
    real = (jnp.arange(STEPS) >= EXP_GROUP).astype(jnp.int32)
    last = (count == 0).astype(jnp.int32)
    return ordered(chunk), ordered(owner), ordered(real), ordered(last)


Z_GROUPS = [[0, 2, 4, 6], [1, 3, 5, 7]]
PAIRS = [(i, i ^ 1) for i in range(8)]


def shards(
    queries, key_rows, value_rows, out_proj, residual, norm_gain, w_gate, w_up, w_down,
    route_slot, route_weight, fetch_list, cotangent,
):
    tokens = queries.shape[0]
    hidden = lax.axis_index("hidden")
    group = lax.axis_index("group")
    core = hidden % 2
    core_arr = core.reshape(1).astype(jnp.int32)

    slot_ids = jnp.arange(FETCH, dtype=jnp.int32)
    chosen = route_slot[:, :, None] == slot_ids[None, None, :]
    slot_weight = jnp.sum(jnp.where(chosen, route_weight[:, :, None], 0.0), axis=1)
    used = jnp.any(chosen, axis=1)
    lower = (
        lax.broadcasted_iota(jnp.int32, (tokens, tokens), 0)
        >= lax.broadcasted_iota(jnp.int32, (tokens, tokens), 1)
    ).astype(bf16)
    position = mm(lower, used.astype(bf16), NN).astype(jnp.int32) - 1
    position = jnp.where(used, position, -1)
    pos_t, weight_t = position.T, slot_weight.T
    caps = jnp.arange(CAP, dtype=jnp.int32)
    hit = pos_t[:, None, :] == caps[None, :, None]
    pick = hit.astype(bf16).reshape(FETCH * CAP, tokens)
    row_weight = jnp.sum(jnp.where(hit, weight_t[:, None, :], 0.0), axis=2).reshape(-1, 1)

    cot_half = lax.dynamic_slice_in_dim(cotangent, core * HALF, HALF, 1)
    grad_rows = (mm(pick, cot_half, NN) * row_weight).astype(bf16)
    g_own = lax.all_to_all(
        grad_rows.reshape(FETCH, CAP, HALF), "group", split_axis=0, concat_axis=0, tiled=True
    )
    g_oth = lax.ppermute(g_own, "hidden", PAIRS)

    kv = hidden * (queries.shape[1] // HEAD_DIM) // (HEADS // KV_HEADS)
    key_block = lax.dynamic_slice_in_dim(key_rows, kv * HEAD_DIM, HEAD_DIM, 1)
    value_block = lax.dynamic_slice_in_dim(value_rows, kv * HEAD_DIM, HEAD_DIM, 1)
    mixed = attention(queries, key_block, value_block)
    proj = out_proj.reshape(out_proj.shape[0], 8, COLS)
    part = jnp.einsum("tk,khc->htc", mixed, proj, preferred_element_type=f32).astype(bf16)
    parts = lax.all_to_all(part, "hidden", split_axis=0, concat_axis=0, tiled=True)
    first_col = hidden * COLS
    res_share = lax.dynamic_slice_in_dim(residual, first_col, COLS, 1)
    gain = lax.dynamic_slice_in_dim(norm_gain, first_col, COLS, 0)
    stream = res_share.astype(f32) + jnp.sum(parts.astype(f32), axis=0)
    square = lax.psum(jnp.sum(stream * stream, axis=1), "hidden") / D
    normed = (stream * lax.rsqrt(square + epsilon)[:, None] * gain[None, :]).astype(bf16)

    x_part = mm(pick, normed, NN).astype(bf16).reshape(FETCH, CAP, COLS)
    x_part = lax.all_to_all(x_part, "group", split_axis=0, concat_axis=0, tiled=True)
    x_rows = lax.all_gather(x_part, "hidden", axis=0, tiled=False)

    own_col = lax.dynamic_slice_in_dim(fetch_list, group, 1, 1)[:, 0]
    experts = own_col - group * EXP_GROUP
    wg, wu = w_gate.transpose(0, 2, 1), w_up.transpose(0, 2, 1)
    out_rows, d_own, d_oth, act, dgu = rows_call(
        experts, core_arr, x_rows, g_own, g_oth, wg, wu, w_down
    )

    out_share = lax.psum_scatter(
        out_rows, "hidden", scatter_dimension=0, tiled=True
    ).reshape(FETCH, CAP, COLS)
    out_back = lax.all_to_all(out_share, "group", split_axis=0, concat_axis=0, tiled=True)
    d_in = lax.ppermute(d_oth, "hidden", PAIRS)
    d_sum = (d_own.astype(f32) + d_in.astype(f32)).astype(bf16)
    d_back = lax.all_to_all(d_sum, "group", split_axis=0, concat_axis=0, tiled=True)

    chunk, expert, real, last = grad_order(experts)
    grad_gate, grad_up, grad_down = grads_call(
        chunk, expert, real, last, core_arr, x_rows, g_own, g_oth, act, dgu
    )

    d_tok = mm(pick, d_back.reshape(FETCH * CAP, HALF), TN).astype(bf16)
    d_tok = d_tok.reshape(tokens, 4, COLS).transpose(1, 0, 2)
    d_parts = lax.all_to_all(
        d_tok, "hidden", split_axis=0, concat_axis=0, tiled=True, axis_index_groups=Z_GROUPS
    )
    grad_normed = jnp.sum(d_parts.astype(f32), axis=0).astype(bf16)

    high = row_weight.astype(bf16)
    low = (row_weight - high.astype(f32)).astype(bf16)
    out_flat = out_back.reshape(FETCH * CAP, COLS)
    moe = mm(pick * high, out_flat, TN) + mm(pick * low, out_flat, TN)
    layer_out = (stream + moe).astype(bf16)
    return (
        layer_out,
        grad_normed,
        grad_gate.transpose(0, 2, 1),
        grad_up.transpose(0, 2, 1),
        grad_down,
    )


def solution(mesh):
    return jax.shard_map(
        shards,
        mesh=mesh,
        in_specs=(
            P("group", "hidden"),
            P("group", None),
            P("group", None),
            P("hidden", None),
            P("group", None),
            P(),
            P("group", None, "hidden"),
            P("group", None, "hidden"),
            P("group", "hidden", None),
            P("group", None),
            P("group", None),
            P(),
            P("group", None),
        ),
        out_specs=(
            P("group", "hidden"),
            P("group", "hidden"),
            P("group", None, "hidden"),
            P("group", None, "hidden"),
            P("group", "hidden", None),
        ),
        check_vma=False,
    )
```

time: 671 us -> 435 us (0.65)
  blocking collectives: 78 us -> 234 us
  matrix products: 155 us -> 25.9 us
  other arithmetic: 133 us -> 20.8 us
  local copies, waits for them, and re-layouts: 102 us -> 4.49 us
  waiting for transfers between devices: 143 us -> 54.6 us
  Pallas kernels: 0 us -> 60.3 us
  starting transfers between devices: 37.8 us -> 17.8 us
    all_to_all x1 -> x3, blocking collectives: 78 us -> 221 us  [the longest x1 95.8 us: shards(): lax.all_to_all(d_sum, 'group', split_axis=0, concat_axis=0, tiled=True)]
    dot_general x14 -> x8, matrix products: 152 us -> 22.5 us  [the longest x6 18.1 us: mm(): return lax.dot_general(a, b, dims, preferred_element_type=f32)]
    all_to_all x5 -> x3, waiting for transfers between devices: 143 us -> 29.3 us  [the longest x1 17.9 us: shards(): lax.all_to_all(part, 'hidden', split_axis=0, concat_axis=0, tiled=True)]
    scatter-add x2 -> x0, other arithmetic: 106 us -> none  [the longest x1 53.3 us: shards(): jnp.zeros((tokens_here, D), jnp.float32).at[flat_rows]]
    pallas_call x0 -> x2, Pallas kernels: none -> 60.3 us  [the longest x1 34 us: rows_call(): pl.pallas_call(rows_kernel, grid_spec=pltpu.PrefetchScalarGridSpec(num_sc...]
    scatter x2 -> x0, local copies, waits for them, and re-layouts: 46.2 us -> none  [the longest x1 23.2 us: route_table(): rows = jnp.zeros((fetch_count * capacity + 1,), jnp.int32).at[target.resh...]
    gather x5 -> x0, local copies, waits for them, and re-layouts: 43.7 us -> none  [the longest x1 15.6 us: shards(): cotangent[rows].astype(jnp.float32) * row_weight[..., None]]
    ppermute x0 -> x2, waiting for transfers between devices: none -> 25.2 us  [the longest x1 12.6 us: shards(): d_in = lax.ppermute(d_oth, 'hidden', PAIRS)]
  transfers between devices with their start and end apart: 8 -> 7, of which waited for: 2 -> 4; matrix products, arithmetic and copies ran while one was open for 53% -> 7% of each run, Pallas kernels for 0% -> 6%
where the time goes in v1:
time: 435 us; the launch traced here: 432 us
  blocking collectives  234 us (54%)
  Pallas kernels  60.3 us (14%)
  waiting for transfers between devices  54.6 us (13%)
  matrix products  25.9 us (6%)
  other arithmetic  20.8 us (5%)
  starting transfers between devices  17.8 us (4%)
  between operations  14.4 us (3%)
  local copies, waits for them, and re-layouts  4.49 us (1%)
    all_to_all x1, blocking collectives, shards(): lax.all_to_all(d_sum, 'group', split_axis=0, concat_axis=0, tiled=True)  95.8 us
    all_to_all x1, blocking collectives, shards(): lax.all_to_all(grad_rows.reshape(FETCH, CAP, HALF), 'group', split_axis=0...  93.7 us
    pallas_call x1, Pallas kernels, rows_call(): pl.pallas_call(rows_kernel, grid_spec=pltpu.PrefetchScalarGridSpec(num_sc...  34 us
    all_to_all x1, blocking collectives, shards(): lax.all_to_all(x_part, 'group', split_axis=0, concat_axis=0, tiled=True)  31.4 us
    pallas_call x1, Pallas kernels, grads_call(): pl.pallas_call(grads_kernel, grid_spec=pltpu.PrefetchScalarGridSpec(num_s...  26.3 us
    dot_general x6, matrix products, mm(): return lax.dot_general(a, b, dims, preferred_element_type=f32)  18.1 us
    all_to_all x1, waiting for transfers between devices, shards(): lax.all_to_all(part, 'hidden', split_axis=0, concat_axis=0, tiled=True)  17.9 us
    convert_element_type x1, other arithmetic, shards(): d_sum = (d_own.astype(f32) + d_in.astype(f32)).astype(bf16)  13.2 us
  transfers between devices with their start and end apart: 7, of which 4 were waited for; matrix products, arithmetic and copies ran while one was open for 7% of the time, Pallas kernels for 6%

profile of v1, /device:TPU:6, one launch (start us, length us, event | category | flops | bytes accessed | tf_op | source)
XLA Modules:
  0.0 432.0 jit_solution(12591284464147390078)
XLA Ops:
  7.3 3.5 fusion.78
  10.7 2.3 convolution_convert_fusion.1
  13.1 2.2 fusion.18
  15.2 5.4 %all-to-all-start = ((bf16[8,384,256]{2,1,0:T(8,128)(2,1)}), bf16[8,384,256]{2,1,0:T(8,128)(2,1)S(1)}, u32[]{:S(2)}, u32[]{:S(2)}) async-start(bf16[8,384,256]{2,1,0:T(8,128)(2,1)} %fusion.18), calls=%async_computation | async-start | bytes 3145728 | tf_op jit(solution)/shard_map/all_to_all | solution.py:253
  21.1 0.6 copy-done.6
  21.7 2.0 bitcast_compare_fusion
  23.6 0.8 dynamic_slice.22
  24.4 17.9 %all-to-all-done = bf16[8,384,256]{2,1,0:T(8,128)(2,1)S(1)} async-done(((bf16[8,384,256]{2,1,0:T(8,128)(2,1)}), bf16[8,384,256]{2,1,0:T(8,128)(2,1)S(1)}, u32[]{:S(2)}, u32[]{:S(2)}) %all-to-all-start) | async-done | bytes 1572896 | tf_op jit(solution)/shard_map/all_to_all | solution.py:253
  42.5 1.2 multiply_reduce_fusion
  43.7 12.8 %psum.7 = f32[384]{0:T(512)S(1)} all-reduce(f32[384]{0:T(512)S(1)} %multiply_reduce_fusion), channel_id=1, replica_groups=mesh['group'=16,'hidden'=8] {'hidden'}, use_global_device_ids=true, to_apply=%region_7.8 | all-reduce | flops 384 | bytes 3072 | tf_op jit(solution)/shard_map/psum | solution.py:258
  56.5 2.6 convolution_convert_fusion
  59.2 31.4 %all_to_all.30 = bf16[16,240,256]{2,1,0:T(8,128)(2,1)} all-to-all(bf16[16,240,256]{2,1,0:T(8,128)(2,1)S(1)} %bitcast.98), channel_id=1, replica_groups=mesh['group'=16,'hidden'=8] {'group'}, dimensions={0} | all-to-all | bytes 3932160 | tf_op jit(solution)/shard_map/all_to_all | solution.py:262
  90.8 0.7 select_reduce_fusion
  91.6 4.7 %multiply_convert_fusion = bf16[3840,1024]{1,0:T(8,128)(2,1)S(1)} fusion(pred[3840,384]{1,0:T(32,128)(4,1)S(1)} %copy-done.5, f32[3840]{0:T(1024)S(1)} %mul.81, bf16[384,2048]{1,0:T(8,128)(2,1)S(1)} %copy-done, s32[]{:T(128)S(6)} %select_n.72), kind=kOutput, calls=%fused_computation.2 | convolution fusion | flops 3027763200 | bytes 10141700 | tf_op jit(solution)/shard_map/dot_general | solution.py:33
  96.4 93.7 %all_to_all.31.g_own_ref = bf16[16,240,1024]{2,1,0:T(8,128)(2,1)} all-to-all(bf16[16,240,1024]{2,1,0:T(8,128)(2,1)S(1)} %bitcast.95), channel_id=1, replica_groups=mesh['group'=16,'hidden'=8] {'group'}, dimensions={0} | all-to-all | bytes 15728640 | tf_op jit(solution)/shard_map/all_to_all | solution.py:242
  190.2 12.6 %collective-permute-done.g_oth_ref = bf16[16,240,1024]{2,1,0:T(8,128)(2,1)} collective-permute-done((bf16[16,240,1024]{2,1,0:T(8,128)(2,1)}, bf16[16,240,1024]{2,1,0:T(8,128)(2,1)}, u32[]{:S(2)}, u32[]{:S(2)}) %collective-permute-start) | collective-permute-done | bytes 7864352 | tf_op jit(solution)/shard_map/ppermute | solution.py:245
  202.8 1.9 copy-done.2
  204.7 34.0 %expert_rows.1 = (bf16[8,16,240,256]{3,2,1,0:T(8,128)(2,1)}, bf16[16,240,1024]{2,1,0:T(8,128)(2,1)}, bf16[16,240,1024]{2,1,0:T(8,128)(2,1)}, bf16[16,240,128]{2,1,0:T(8,128)(2,1)S(1)}, bf16[16,240,256]{2,1,0:T(8,128)(2,1)S(1)}) custom-call(s32[16]{0:T(128)S(1)} %subtract_reduce_fusion.expert_ref, s32[1]{0:T(128)} %bitcast.9.core_ref, ...), custom_call_target="tpu_custom_call" | custom-call | flops 12079595520 | bytes 89128960 | tf_op jit(solution)/shard_map/expert_rows/pallas_call | solution.py:100
  238.7 0.4 collective-permute-start.1
  239.1 12.6 %collective-permute-done.1 = bf16[16,240,1024]{2,1,0:T(8,128)(2,1)} collective-permute-done((bf16[16,240,1024]{2,1,0:T(8,128)(2,1)}, bf16[16,240,1024]{2,1,0:T(8,128)(2,1)}, u32[]{:S(2)}, u32[]{:S(2)}) %collective-permute-start.1) | collective-permute-done | bytes 7864352 | tf_op jit(solution)/shard_map/ppermute | solution.py:276
  251.7 13.2 %add_convert_fusion = bf16[16,240,1024]{2,1,0:T(8,128)(2,1)} fusion(bf16[16,240,1024]{2,1,0:T(8,128)(2,1)} %collective-permute-done.1, bf16[16,240,1024]{2,1,0:T(8,128)(2,1)} %get-tuple-element.14), kind=kLoop, calls=%fused_computation.1 | loop fusion | flops 15728640 | bytes 23592960 | tf_op jit(solution)/shard_map/convert_element_type | solution.py:277
  264.9 95.8 %all_to_all.32 = bf16[16,240,1024]{2,1,0:T(8,128)(2,1)S(1)} all-to-all(bf16[16,240,1024]{2,1,0:T(8,128)(2,1)} %add_convert_fusion), channel_id=1, replica_groups=mesh['group'=16,'hidden'=8] {'group'}, dimensions={0} | all-to-all | bytes 15728640 | tf_op jit(solution)/shard_map/all_to_all | solution.py:278
  360.7 3.3 bitcast_convert_fusion
  363.9 0.9 copy.74
  364.9 4.2 all-to-all-start.5
  369.1 11.5 %all-to-all-done.5 = bf16[4,384,256]{2,1,0:T(8,128)(2,1)} async-done(((bf16[4,384,256]{2,1,0:T(8,128)(2,1)}), bf16[4,384,256]{2,1,0:T(8,128)(2,1)}, u32[]{:S(2)}, u32[]{:S(2)}) %all-to-all-start.5) | async-done | bytes 786464 | tf_op jit(solution)/shard_map/all_to_all | solution.py:287
  380.5 7.7 %all-to-all-start.3 = ((bf16[16,240,256]{2,1,0:T(8,128)(2,1)}), bf16[16,240,256]{2,1,0:T(8,128)(2,1)}, u32[]{:S(2)}, u32[]{:S(2)}) async-start(bf16[16,240,256]{2,1,0:T(8,128)(2,1)} %bitcast.97), calls=%async_computation.4 | async-start | bytes 3932160 | tf_op jit(solution)/shard_map/all_to_all | solution.py:275
  388.9 0.6 subtract_convert_fusion
  389.5 26.3 %weight_grads.1 = (bf16[8,96,2048]{2,1,0:T(8,128)(2,1)}, bf16[8,96,2048]{2,1,0:T(8,128)(2,1)}, bf16[8,96,2048]{2,1,0:T(8,128)(2,1)}) custom-call(s32[24]{0:T(128)S(1)} %get-tuple-element.24.chunk_ref, s32[24]{0:T(128)S(1)} %get-tuple-element.23.expert_ref, s32[24]{0:T(128)S(1)} %get-tuple-element.22.real_ref, s32[24]{0:T(128)S(1)} %get-tuple-element.21.last_ref, ...), custom_call_target="tpu_custom_call" | custom-call | flops 6039797760 | bytes 47185920 | tf_op jit(solution)/shard_map/weight_grads/pallas_call | solution.py:165
  415.8 2.0 reduce_sum.116
  417.8 3.3 fusion.25
  421.1 4.0 fusion.40
  (58 shorter events, 1.7 us)
Async XLA Ops:
  7.2 84.4 %copy-start = (bf16[384,2048]{1,0:T(8,128)(2,1)S(1)}, bf16[384,2048]{1,0:T(8,128)(2,1)}, u32[]{:S(2)}) copy-start(bf16[384,2048]{1,0:T(8,128)(2,1)} %param.25) | copy-start | bytes 4718596
  10.7 2.4 copy-start.14
  15.2 5.6 %copy-start.10 = (s32[384,8]{0,1:T(8,128)S(1)}, s32[384,8]{0,1:T(8,128)}, u32[]{:S(2)}) copy-start(s32[384,8]{0,1:T(8,128)} %param.22) | copy-start | bytes 36868
  15.2 27.0 %all-to-all-start = ((bf16[8,384,256]{2,1,0:T(8,128)(2,1)}), bf16[8,384,256]{2,1,0:T(8,128)(2,1)S(1)}, u32[]{:S(2)}, u32[]{:S(2)}) async-start(bf16[8,384,256]{2,1,0:T(8,128)(2,1)} %fusion.18), calls=%async_computation | async-start | bytes 3145728 | tf_op jit(solution)/shard_map/all_to_all | solution.py:253
  20.7 182.1 %all-gather.3.cloned.1.call-start = ((), (), s32[]{:S(2)}) async-start(), calls=%async_computation.8 | async-start | bytes 17694720 | tf_op jit(solution)/shard_map/all_gather | solution.py:263
  21.0 0.6 copy-start.6
  42.5 16.7 %copy-start.3 = (f32[384,256]{1,0:T(8,128)}, f32[384,256]{1,0:T(8,128)S(1)}, u32[]{:S(2)}) copy-start(f32[384,256]{1,0:T(8,128)S(1)} %convert_reduce_fusion) | copy-start | bytes 1179652
  59.2 31.6 %copy-start.11 = (f32[384,8]{0,1:T(8,128)S(1)}, f32[384,8]{0,1:T(8,128)}, u32[]{:S(2)}) copy-start(f32[384,8]{0,1:T(8,128)} %param.23) | copy-start | bytes 36868
  59.2 31.6 %copy-start.7 = (s32[16,384]{1,0:T(8,128)S(1)}, s32[16,384]{1,0:T(8,128)}, u32[]{:S(2)}) copy-start(s32[16,384]{1,0:T(8,128)} %copy-done.6) | copy-start | bytes 73732
  59.2 32.4 %copy-start.5 = (pred[3840,384]{1,0:T(32,128)(4,1)S(1)}, pred[3840,384]{1,0:T(32,128)(4,1)}, u32[]{:S(2)}) copy-start(pred[3840,384]{1,0:T(32,128)(4,1)} %bitcast_compare_fusion) | copy-start | bytes 4423684
  90.7 289.8 %reduce-scatter.2.cloned.1.call-start = ((), (), s32[]{:S(2)}) async-start(), calls=%async_computation.7 | async-start | bytes 17694720 | tf_op jit(solution)/shard_map/reduce_scatter | solution.py:272
  96.4 93.7 %copy-start.12 = (s32[16,16]{1,0:T(8,128)S(1)}, s32[16,16]{1,0:T(8,128)}, u32[]{:S(2)}) copy-start(s32[16,16]{1,0:T(8,128)} %param.24) | copy-start | bytes 3076
  190.0 12.8 %collective-permute-start = (bf16[16,240,1024]{2,1,0:T(8,128)(2,1)}, bf16[16,240,1024]{2,1,0:T(8,128)(2,1)}, u32[]{:S(2)}, u32[]{:S(2)}) collective-permute-start(bf16[16,240,1024]{2,1,0:T(8,128)(2,1)} %all_to_all.31.g_own_ref), channel_id=1, source_target_pairs={{0,1},{1,0},{2,3},{3,2},{4,5},{5,4},{6,7},{7,6},{8,9},{9,8},{10,11... | collective-permute-start | bytes 23592968 | tf_op jit(solution)/shard_map/ppermute | solution.py:245
  202.8 1.9 copy-start.2
  238.7 13.0 %collective-permute-start.1 = (bf16[16,240,1024]{2,1,0:T(8,128)(2,1)}, bf16[16,240,1024]{2,1,0:T(8,128)(2,1)}, u32[]{:S(2)}, u32[]{:S(2)}) collective-permute-start(bf16[16,240,1024]{2,1,0:T(8,128)(2,1)} %get-tuple-element.15), channel_id=1, source_target_pairs={{0,1},{1,0},{2,3},{3,2},{4,5},{5,4},{6,7},{7,6},{8,9},{9,8},{10,11... | collective-permute-start | bytes 23592968 | tf_op jit(solution)/shard_map/ppermute | solution.py:276
  264.9 95.8 %copy-start.8 = (s32[16,384]{1,0:T(8,128)S(1)}, s32[16,384]{1,0:T(8,128)}, u32[]{:S(2)}) copy-start(s32[16,384]{1,0:T(8,128)} %copy-done.6) | copy-start | bytes 73732
  364.9 15.7 %all-to-all-start.5 = ((bf16[4,384,256]{2,1,0:T(8,128)(2,1)}), bf16[4,384,256]{2,1,0:T(8,128)(2,1)}, u32[]{:S(2)}, u32[]{:S(2)}) async-start(bf16[4,384,256]{2,1,0:T(8,128)(2,1)} %bitcast.96), calls=%async_computation.6 | async-start | bytes 1572864 | tf_op jit(solution)/shard_map/all_to_all | solution.py:287
  380.5 37.3 %all-to-all-start.3 = ((bf16[16,240,256]{2,1,0:T(8,128)(2,1)}), bf16[16,240,256]{2,1,0:T(8,128)(2,1)}, u32[]{:S(2)}, u32[]{:S(2)}) async-start(bf16[16,240,256]{2,1,0:T(8,128)(2,1)} %bitcast.97), calls=%async_computation.4 | async-start | bytes 3932160 | tf_op jit(solution)/shard_map/all_to_all | solution.py:275
  417.8 3.3 copy-start.4
  417.8 3.3 copy-start.9
  417.8 3.3 copy-start.13
  421.1 4.0 copy-start.1
Sparse Core Ops, SparseCore 0:
  90.8 78.1 all-gather.2
  238.8 85.5 reduce-scatter.1

commit v2 on v1

v2 whole, which is shorter than its diff:
```python
import math

import jax
import jax.numpy as jnp
from jax import lax
from jax.experimental import pallas as pl
from jax.experimental.pallas import tpu as pltpu
from jax.sharding import PartitionSpec as P

D = 2048
HEADS = 32
KV_HEADS = 4
HEAD_DIM = 128
EXP_GROUP = 8
FETCH = 16
CAP = 240
UNITS = 96
PAD = 128
COLS = 256
HALF = 1024
STEPS = FETCH + EXP_GROUP
SPLIT = (96, 144)

epsilon = 1e-06
bf16 = jnp.bfloat16
f32 = jnp.float32

NT = (((1,), (1,)), ((), ()))
NN = (((1,), (0,)), ((), ()))
TN = (((0,), (0,)), ((), ()))


def mm(a, b, dims):
    return lax.dot_general(a, b, dims, preferred_element_type=f32)


def attention(queries, key_block, value_block):
    tokens = queries.shape[0]
    heads = queries.shape[1] // HEAD_DIM
    query = queries.reshape(tokens, heads, HEAD_DIM)
    scores = jnp.einsum("thd,sd->hts", query, key_block, preferred_element_type=f32)
    scores = scores / math.sqrt(HEAD_DIM)
    row_pos = lax.broadcasted_iota(jnp.int32, (tokens, tokens), 0)
    col_pos = lax.broadcasted_iota(jnp.int32, (tokens, tokens), 1)
    scores = jnp.where(row_pos >= col_pos, scores, -1e30)
    weights = jnp.exp(scores - jnp.max(scores, axis=-1, keepdims=True))
    probs = (weights / jnp.sum(weights, axis=-1, keepdims=True)).astype(bf16)
    mixed = jnp.einsum("hts,sd->thd", probs, value_block, preferred_element_type=f32)
    return mixed.astype(bf16).reshape(tokens, heads * HEAD_DIM)


def rows_kernel(expert_ref, core_ref, x_ref, *refs):
    g_refs = refs[: 2 * len(SPLIT)]
    wg_ref, wu_ref, wd_ref, out_ref, act_ref, dgu_ref, wgu, wdp = refs[2 * len(SPLIT) :]
    core = core_ref[0]

    @pl.when(pl.program_id(0) == 0)
    def _():
        zeros = jnp.zeros((PAD - UNITS, D), bf16)
        wgu[UNITS:PAD, :] = zeros
        wgu[PAD + UNITS :, :] = zeros
        wdp[UNITS:, :] = zeros

    wgu[:UNITS, :] = wg_ref[0]
    wgu[PAD : PAD + UNITS, :] = wu_ref[0]
    wdp[:UNITS, :] = wd_ref[0]

    pre = mm(x_ref[0, 0], wgu[:, :COLS], NT)
    for block in range(1, D // COLS):
        pre = pre + mm(x_ref[block, 0], wgu[:, block * COLS : (block + 1) * COLS], NT)
    gate, up = pre[:, :PAD], pre[:, PAD:]
    sig = jax.nn.sigmoid(gate)
    swish = gate * sig
    act = (swish * up).astype(bf16)
    act_ref[0] = act
    for block in range(D // COLS):
        out_ref[block, 0] = mm(act, wdp[:, block * COLS : (block + 1) * COLS], NN).astype(bf16)
    own = pl.multiple_of(core * HALF, HALF)
    oth = pl.multiple_of(HALF - core * HALF, HALF)
    start = 0
    for i, size in enumerate(SPLIT):
        d_act = mm(g_refs[2 * i][0], wdp[:, pl.ds(own, HALF)], NT)
        d_act = d_act + mm(g_refs[2 * i + 1][0], wdp[:, pl.ds(oth, HALF)], NT)
        rows = slice(start, start + size)
        gate_i, up_i, sig_i, swish_i = gate[rows], up[rows], sig[rows], swish[rows]
        dgu_ref[0, rows, :PAD] = (
            d_act * up_i * sig_i * (1.0 + gate_i * (1.0 - sig_i))
        ).astype(bf16)
        dgu_ref[0, rows, PAD:] = (d_act * swish_i).astype(bf16)
        start += size


def rows_call(experts, core, x_rows, g_parts, wg, wu, wd):
    weight = pl.BlockSpec((1, UNITS, D), lambda i, e, c: (e[i], 0, 0))
    cols8 = pl.BlockSpec((8, 1, CAP, COLS), lambda i, e, c: (0, i, 0, 0))

    def flat(size, width):
        return pl.BlockSpec((1, size, width), lambda i, e, c: (i, 0, 0))

    halves = [flat(size, HALF) for size in SPLIT for _ in range(2)]
    return pl.pallas_call(
        rows_kernel,
        grid_spec=pltpu.PrefetchScalarGridSpec(
            num_scalar_prefetch=2,
            grid=(FETCH,),
            in_specs=[cols8, *halves, weight, weight, weight],
            out_specs=[cols8, flat(CAP, PAD), flat(CAP, 2 * PAD)],
            scratch_shapes=[pltpu.VMEM((2 * PAD, D), bf16), pltpu.VMEM((PAD, D), bf16)],
        ),
        out_shape=[
            jax.ShapeDtypeStruct((8, FETCH, CAP, COLS), bf16),
            jax.ShapeDtypeStruct((FETCH, CAP, PAD), bf16),
            jax.ShapeDtypeStruct((FETCH, CAP, 2 * PAD), bf16),
        ],
        compiler_params=pltpu.CompilerParams(vmem_limit_bytes=32 << 20),
        cost_estimate=pl.CostEstimate(
            flops=2 * 4 * FETCH * CAP * D * PAD, bytes_accessed=65 << 20, transcendentals=0
        ),
        name="expert_rows",
    )(experts, core, x_rows, *g_parts, wg, wu, wd)


def input_kernel(
    expert_ref, core_ref, own_ref, oth_ref, wg_ref, wu_ref, wg_oth_ref, wu_oth_ref,
    d_ref, w_own, w_oth,
):
    core = core_ref[0]

    @pl.when(pl.program_id(0) == 0)
    def _():
        zeros = jnp.zeros((PAD - UNITS, HALF), bf16)
        for ref in (w_own, w_oth):
            ref[UNITS:PAD, :] = zeros
            ref[PAD + UNITS :, :] = zeros

    own, oth = own_ref[0], oth_ref[0]
    for block in range(HALF // COLS):
        place = slice(block * COLS, (block + 1) * COLS)
        col = pl.ds(pl.multiple_of((2 * block + core) * COLS, COLS), COLS)
        w_own[:UNITS, place] = wg_ref[0, :, col]
        w_own[PAD : PAD + UNITS, place] = wu_ref[0, :, col]
        w_oth[:UNITS, place] = wg_oth_ref[0, :, col]
        w_oth[PAD : PAD + UNITS, place] = wu_oth_ref[0, :, col]
        d_ref[0, :, place] = (mm(own, w_own[:, place], NN) + mm(oth, w_oth[:, place], NN)).astype(
            bf16
        )


def input_call(experts, core, dgu, dgu_oth, wg, wu, wg_oth, wu_oth):
    weight = pl.BlockSpec((1, UNITS, D), lambda i, e, c: (e[i], 0, 0))
    flat = pl.BlockSpec((1, CAP, 2 * PAD), lambda i, e, c: (i, 0, 0))
    return pl.pallas_call(
        input_kernel,
        grid_spec=pltpu.PrefetchScalarGridSpec(
            num_scalar_prefetch=2,
            grid=(FETCH,),
            in_specs=[flat, flat, weight, weight, weight, weight],
            out_specs=pl.BlockSpec((1, CAP, HALF), lambda i, e, c: (i, 0, 0)),
            scratch_shapes=[pltpu.VMEM((2 * PAD, HALF), bf16)] * 2,
        ),
        out_shape=jax.ShapeDtypeStruct((FETCH, CAP, HALF), bf16),
        compiler_params=pltpu.CompilerParams(vmem_limit_bytes=32 << 20),
        cost_estimate=pl.CostEstimate(
            flops=2 * 2 * FETCH * CAP * D * PAD, bytes_accessed=40 << 20, transcendentals=0
        ),
        name="input_rows",
    )(experts, core, dgu, dgu_oth, wg, wu, wg_oth, wu_oth)


def grads_kernel(chunk_ref, expert_ref, real_ref, last_ref, core_ref, x_ref, *refs):
    g_refs = refs[: 2 * len(SPLIT)]
    act_ref, dgu_ref, gg_ref, gu_ref, gd_ref, acc_gu, acc_d = refs[2 * len(SPLIT) :]
    step = pl.program_id(0)
    core = core_ref[0]

    @pl.when(real_ref[step] == 0)
    def _():
        acc_gu[...] = jnp.zeros_like(acc_gu)
        acc_d[...] = jnp.zeros_like(acc_d)

    @pl.when(real_ref[step] == 1)
    def _():
        d_gu, act = dgu_ref[0], act_ref[0]
        for block in range(D // COLS):
            place = slice(block * COLS, (block + 1) * COLS)
            acc_gu[:, place] += mm(d_gu, x_ref[block, 0], TN)
        start = 0
        for i, size in enumerate(SPLIT):
            act_i = act[start : start + size]
            start += size
            for block in range(HALF // COLS):
                place = slice(block * COLS, (block + 1) * COLS)
                for half, base in ((0, core * HALF), (1, HALF - core * HALF)):
                    col = pl.ds(pl.multiple_of(base + block * COLS, COLS), COLS)
                    acc_d[:, col] += mm(act_i, g_refs[2 * i + half][0, :, place], TN)

    @pl.when(last_ref[step] == 1)
    def _():
        gg_ref[0] = acc_gu[:UNITS, :].astype(bf16)
        gu_ref[0] = acc_gu[PAD : PAD + UNITS, :].astype(bf16)
        gd_ref[0] = acc_d[:UNITS, :].astype(bf16)


def grads_call(chunk, expert, real, last, core, x_rows, g_parts, act, dgu):
    weight = pl.BlockSpec((1, UNITS, D), lambda i, k, e, r, l, c: (e[i], 0, 0))

    def flat(size, width):
        return pl.BlockSpec((1, size, width), lambda i, k, e, r, l, c: (k[i], 0, 0))

    halves = [flat(size, HALF) for size in SPLIT for _ in range(2)]
    return pl.pallas_call(
        grads_kernel,
        grid_spec=pltpu.PrefetchScalarGridSpec(
            num_scalar_prefetch=5,
            grid=(STEPS,),
            in_specs=[
                pl.BlockSpec((8, 1, CAP, COLS), lambda i, k, e, r, l, c: (0, k[i], 0, 0)),
                *halves,
                flat(CAP, PAD),
                flat(CAP, 2 * PAD),
            ],
            out_specs=[weight, weight, weight],
            scratch_shapes=[pltpu.VMEM((2 * PAD, D), f32), pltpu.VMEM((PAD, D), f32)],
        ),
        out_shape=[jax.ShapeDtypeStruct((EXP_GROUP, UNITS, D), bf16)] * 3,
        compiler_params=pltpu.CompilerParams(vmem_limit_bytes=32 << 20),
        cost_estimate=pl.CostEstimate(
            flops=2 * 3 * FETCH * CAP * D * PAD, bytes_accessed=45 << 20, transcendentals=0
        ),
        name="weight_grads",
    )(chunk, expert, real, last, core, x_rows, *g_parts, act, dgu)


def grad_order(experts):
    ids = jnp.arange(FETCH, dtype=jnp.int32)
    own = jnp.arange(EXP_GROUP, dtype=jnp.int32)
    listed = experts[None, :] == own[:, None]
    first = jnp.min(jnp.where(listed, ids[None, :], FETCH), axis=1)
    first = jnp.where(first == FETCH, 0, first)
    key = jnp.concatenate([own * 32, experts * 32 + 1 + ids])
    chunk = jnp.concatenate([first, ids])
    owner = jnp.concatenate([own, experts])
    rank = jnp.sum((key[None, :] < key[:, None]).astype(jnp.int32), axis=1)
    place = rank[:, None] == jnp.arange(STEPS, dtype=jnp.int32)[None, :]

    def ordered(values):
        return jnp.sum(jnp.where(place, values[:, None], 0), axis=0)

    count = jnp.sum((owner[None, :] == owner[:, None]) & (key[None, :] > key[:, None]), axis=1)
    real = (jnp.arange(STEPS) >= EXP_GROUP).astype(jnp.int32)
    last = (count == 0).astype(jnp.int32)
    return ordered(chunk), ordered(owner), ordered(real), ordered(last)


Z_GROUPS = [[0, 2, 4, 6], [1, 3, 5, 7]]
PAIRS = [(i, i ^ 1) for i in range(8)]


def after(value, *others):
    return lax.optimization_barrier((value,) + others)[0]


def exchange(value, axis="group"):
    return lax.all_to_all(value, axis, split_axis=0, concat_axis=0, tiled=True)


def swap(value):
    return lax.ppermute(value, "hidden", PAIRS)


def shards(
    queries, key_rows, value_rows, out_proj, residual, norm_gain, w_gate, w_up, w_down,
    route_slot, route_weight, fetch_list, cotangent,
):
    tokens = queries.shape[0]
    hidden = lax.axis_index("hidden")
    group = lax.axis_index("group")
    core = hidden % 2
    core_arr = core.reshape(1).astype(jnp.int32)
    wg, wu = w_gate.transpose(0, 2, 1), w_up.transpose(0, 2, 1)
    wg_oth, wu_oth = swap(wg), swap(wu)

    kv = hidden * (queries.shape[1] // HEAD_DIM) // (HEADS // KV_HEADS)
    key_block = lax.dynamic_slice_in_dim(key_rows, kv * HEAD_DIM, HEAD_DIM, 1)
    value_block = lax.dynamic_slice_in_dim(value_rows, kv * HEAD_DIM, HEAD_DIM, 1)
    mixed = attention(queries, key_block, value_block)
    proj = out_proj.reshape(out_proj.shape[0], 8, COLS)
    part = jnp.einsum("tk,khc->htc", mixed, proj, preferred_element_type=f32).astype(bf16)
    attn = lax.psum_scatter(part, "hidden", scatter_dimension=0, tiled=True)[0]

    route_slot = after(route_slot, part)
    slot_ids = jnp.arange(FETCH, dtype=jnp.int32)
    chosen = route_slot[:, :, None] == slot_ids[None, None, :]
    slot_weight = jnp.sum(jnp.where(chosen, route_weight[:, :, None], 0.0), axis=1)
    used = jnp.any(chosen, axis=1)
    lower = (
        lax.broadcasted_iota(jnp.int32, (tokens, tokens), 0)
        >= lax.broadcasted_iota(jnp.int32, (tokens, tokens), 1)
    ).astype(bf16)
    position = mm(lower, used.astype(bf16), NN).astype(jnp.int32) - 1
    position = jnp.where(used, position, -1)
    pos_t, weight_t = position.T, slot_weight.T

    def one_hot(start, size):
        caps = start + jnp.arange(size, dtype=jnp.int32)
        hit = pos_t[:, None, :] == caps[None, :, None]
        weight = jnp.sum(jnp.where(hit, weight_t[:, None, :], 0.0), axis=2)
        return hit.astype(bf16).reshape(FETCH * size, tokens), weight.reshape(-1, 1)

    cot_half = lax.dynamic_slice_in_dim(cotangent, core * HALF, HALF, 1)

    def grad_rows(start, size):
        pick, weight = one_hot(start, size)
        return (mm(pick, cot_half, NN) * weight).astype(bf16).reshape(FETCH, size, HALF)

    g_first = exchange(after(grad_rows(0, SPLIT[0]), wg_oth, wu_oth))

    first_col = hidden * COLS
    res_share = lax.dynamic_slice_in_dim(residual, first_col, COLS, 1)
    gain = lax.dynamic_slice_in_dim(norm_gain, first_col, COLS, 0)
    stream = res_share.astype(f32) + attn.astype(f32)
    square = lax.psum(jnp.sum(stream * stream, axis=1), "hidden") / D
    normed = (stream * lax.rsqrt(square + epsilon)[:, None] * gain[None, :]).astype(bf16)

    pick, row_weight = one_hot(0, CAP)
    x_part = mm(pick, normed, NN).astype(bf16).reshape(FETCH, CAP, COLS)
    x_part = exchange(after(x_part, g_first))
    x_rows = lax.all_gather(x_part, "hidden", axis=0, tiled=False)
    g_second = exchange(after(grad_rows(SPLIT[0], SPLIT[1]), x_part))
    g_parts = [g_first, swap(g_first), g_second, swap(g_second)]

    own_col = lax.dynamic_slice_in_dim(fetch_list, group, 1, 1)[:, 0]
    experts = own_col - group * EXP_GROUP
    out_rows, act, dgu = rows_call(experts, core_arr, x_rows, g_parts, wg, wu, w_down)
    d_half = input_call(experts, core_arr, dgu, swap(dgu), wg, wu, wg_oth, wu_oth)

    out_share = lax.psum_scatter(out_rows, "hidden", scatter_dimension=0, tiled=True)[0]
    d_back = exchange(d_half)
    chunk, expert, real, last = grad_order(experts)
    grad_gate, grad_up, grad_down = grads_call(
        chunk, expert, real, last, core_arr, x_rows, g_parts, act, dgu
    )
    out_back = exchange(after(out_share, d_back))

    d_tok = mm(pick, d_back.reshape(-1, HALF), TN).astype(bf16)
    d_tok = d_tok.reshape(tokens, 4, COLS).transpose(1, 0, 2)
    grad_normed = lax.psum_scatter(
        d_tok, "hidden", scatter_dimension=0, tiled=True, axis_index_groups=Z_GROUPS
    )[0]

    high = row_weight.astype(bf16)
    low = (row_weight - high.astype(f32)).astype(bf16)
    out_back = out_back.reshape(-1, COLS)
    moe = mm(pick * high, out_back, TN) + mm(pick * low, out_back, TN)
    layer_out = (stream + moe).astype(bf16)
    return (
        layer_out,
        grad_normed,
        grad_gate.transpose(0, 2, 1),
        grad_up.transpose(0, 2, 1),
        grad_down,
    )


def solution(mesh):
    return jax.shard_map(
        shards,
        mesh=mesh,
        in_specs=(
            P("group", "hidden"),
            P("group", None),
            P("group", None),
            P("hidden", None),
            P("group", None),
            P(),
            P("group", None, "hidden"),
            P("group", None, "hidden"),
            P("group", "hidden", None),
            P("group", None),
            P("group", None),
            P(),
            P("group", None),
        ),
        out_specs=(
            P("group", "hidden"),
            P("group", "hidden"),
            P("group", None, "hidden"),
            P("group", None, "hidden"),
            P("group", "hidden", None),
        ),
        check_vma=False,
    )
```

time: 435 us -> 432 us (level)
  blocking collectives: 234 us -> 102 us
  waiting for transfers between devices: 54.6 us -> 162 us
  Pallas kernels: 60.3 us -> 76.2 us
  other arithmetic: 20.8 us -> 7.41 us
  local copies, waits for them, and re-layouts: 4.49 us -> 13.5 us
  starting transfers between devices: 17.8 us -> 23.4 us
  matrix products: 25.9 us -> 30.8 us
    all_to_all x3 -> x2, blocking collectives: 221 us -> 88.6 us  [exchange(): return lax.all_to_all(value, axis, split_axis=0, concat_axis=0, tiled=True)]
    all_to_all x3, waiting for transfers between devices: 29.3 us -> 120 us  [exchange(): return lax.all_to_all(value, axis, split_axis=0, concat_axis=0, tiled=True)]
    reduce_scatter x1 -> x3, waiting for transfers between devices: 0.01 us -> 20.7 us  [the longest x1 20.7 us: shards(): attn = lax.psum_scatter(part, 'hidden', scatter_dimension=0, tiled=True)[0]]
    pallas_call x0 -> x1, Pallas kernels: none -> 16.4 us  [input_call(): pl.pallas_call(input_kernel, grid_spec=pltpu.PrefetchScalarGridSpec(num_s...]
    convert_element_type x1, other arithmetic: 13.2 us -> 0.01 us  [grad_order(): real = (jnp.arange(STEPS) >= EXP_GROUP).astype(jnp.int32)]
    unnamed x30 -> x42, local copies, waits for them, and re-layouts: 2.64 us -> 11.4 us
    ppermute x2 -> x5, waiting for transfers between devices: 25.2 us -> 16.9 us  [swap(): return lax.ppermute(value, 'hidden', PAIRS)]
    dot_general x6 -> x7, matrix products: 18.1 us -> 23 us  [mm(): return lax.dot_general(a, b, dims, preferred_element_type=f32)]
  transfers between devices with their start and end apart: 7 -> 12, of which waited for: 4 -> 6; matrix products, arithmetic and copies ran while one was open for 7% -> 9% of each run, Pallas kernels for 6% -> 11%
where the time goes in v2:
time: 432 us; the launch traced here: 429 us
  waiting for transfers between devices  162 us (38%)
  blocking collectives  102 us (24%)
  Pallas kernels  76.2 us (18%)
  matrix products  30.8 us (7%)
  starting transfers between devices  23.4 us (5%)
  between operations  14.1 us (3%)
  local copies, waits for them, and re-layouts  13.5 us (3%)
  other arithmetic  7.41 us (2%)
    all_to_all x3, waiting for transfers between devices, exchange(): return lax.all_to_all(value, axis, split_axis=0, concat_axis=0, tiled=True)  120 us
    all_to_all x2, blocking collectives, exchange(): return lax.all_to_all(value, axis, split_axis=0, concat_axis=0, tiled=True)  88.6 us
    pallas_call x1, Pallas kernels, rows_call(): pl.pallas_call(rows_kernel, grid_spec=pltpu.PrefetchScalarGridSpec(num_sc...  30.8 us
    pallas_call x1, Pallas kernels, grads_call(): pl.pallas_call(grads_kernel, grid_spec=pltpu.PrefetchScalarGridSpec(num_s...  29.1 us
    dot_general x7, matrix products, mm(): return lax.dot_general(a, b, dims, preferred_element_type=f32)  23 us
    all_to_all x3, starting transfers between devices, exchange(): return lax.all_to_all(value, axis, split_axis=0, concat_axis=0, tiled=True)  21.9 us
    reduce_scatter x1, waiting for transfers between devices, shards(): attn = lax.psum_scatter(part, 'hidden', scatter_dimension=0, tiled=True)[0]  20.7 us
    ppermute x5, waiting for transfers between devices, swap(): return lax.ppermute(value, 'hidden', PAIRS)  16.9 us
  transfers between devices with their start and end apart: 12, of which 6 were waited for; matrix products, arithmetic and copies ran while one was open for 9% of the time, Pallas kernels for 11%

profile of v2, /device:TPU:6, one launch (start us, length us, event | category | flops | bytes accessed | tf_op | source)
XLA Modules:
  0.0 429.0 jit_solution(7879583840163571038)
XLA Ops:
  7.9 3.4 fusion.82
  11.2 2.3 convolution_convert_fusion.1
  13.6 2.2 fusion.18
  17.6 3.5 multiply_convert_fusion.1
  21.0 7.4 %all-to-all-start = ((bf16[16,96,1024]{2,1,0:T(8,128)(2,1)}), bf16[16,96,1024]{2,1,0:T(8,128)(2,1)}, u32[]{:S(2)}, u32[]{:S(2)}) async-start(bf16[16,96,1024]{2,1,0:T(8,128)(2,1)} %bitcast.116), calls=%async_computation.1 | async-start | bytes 6291456 | tf_op jit(solution)/shard_map/all_to_all | solution.py:264
  28.6 2.0 bitcast_compare_fusion
  31.3 20.7 %reduce-scatter.4.cloned.1.call-done = bf16[1,384,256]{2,1,0:T(8,128)(2,1)} async-done(((bf16[8,384,256]{2,1,0:T(8,128)(2,1)}), bf16[1,384,256]{2,1,0:T(8,128)(2,1)}) %reduce-scatter.4.cloned.1.call-update) | async-done | bytes 196624 | tf_op jit(solution)/shard_map/reduce_scatter | solution.py:289
  52.1 1.2 multiply_reduce_fusion
  53.2 13.4 %psum.7 = f32[384]{0:T(512)S(1)} all-reduce(f32[384]{0:T(512)S(1)} %multiply_reduce_fusion), channel_id=1, replica_groups=mesh['group'=16,'hidden'=8] {'hidden'}, use_global_device_ids=true, to_apply=%region_7.8 | all-reduce | flops 384 | bytes 3072 | tf_op jit(solution)/shard_map/psum | solution.py:322
  66.6 2.8 convolution_convert_fusion
  69.4 5.1 %all-to-all-done.refs_0_ = bf16[16,96,1024]{2,1,0:T(8,128)(2,1)} async-done(((bf16[16,96,1024]{2,1,0:T(8,128)(2,1)}), bf16[16,96,1024]{2,1,0:T(8,128)(2,1)}, u32[]{:S(2)}, u32[]{:S(2)}) %all-to-all-start) | async-done | bytes 3145760 | tf_op jit(solution)/shard_map/all_to_all | solution.py:264
  74.5 30.2 %all_to_all.25 = bf16[16,240,256]{2,1,0:T(8,128)(2,1)} all-to-all(bf16[16,240,256]{2,1,0:T(8,128)(2,1)S(1)} %bitcast.119), channel_id=1, replica_groups=mesh['group'=16,'hidden'=8] {'group'}, dimensions={0} | all-to-all | bytes 3932160 | tf_op jit(solution)/shard_map/all_to_all | solution.py:264
  104.9 1.3 bitcast_compare_fusion.1
  107.0 2.9 multiply_convert_fusion
  109.9 58.5 %all_to_all.26.refs_2_ = bf16[16,144,1024]{2,1,0:T(8,128)(2,1)} all-to-all(bf16[16,144,1024]{2,1,0:T(8,128)(2,1)S(1)} %bitcast.115), channel_id=1, replica_groups=mesh['group'=16,'hidden'=8] {'group'}, dimensions={0} | all-to-all | bytes 9437184 | tf_op jit(solution)/shard_map/all_to_all | solution.py:264
  169.1 13.2 %collective-permute-done.2.refs_1_ = bf16[16,96,1024]{2,1,0:T(8,128)(2,1)} collective-permute-done((bf16[16,96,1024]{2,1,0:T(8,128)(2,1)}, bf16[16,96,1024]{2,1,0:T(8,128)(2,1)}, u32[]{:S(2)}, u32[]{:S(2)}) %collective-permute-start.2) | collective-permute-done | bytes 3145760 | tf_op jit(solution)/shard_map/ppermute | solution.py:268
  182.2 4.1 all-gather.3.cloned.1.call-done
  186.4 1.9 copy-done.2
  188.2 1.9 copy-done.4
  190.1 1.9 copy-done.6
  192.0 30.8 %expert_rows.1 = (bf16[8,16,240,256]{3,2,1,0:T(8,128)(2,1)}, bf16[16,240,128]{2,1,0:T(8,128)(2,1)S(1)}, bf16[16,240,256]{2,1,0:T(8,128)(2,1)S(1)}) custom-call(s32[16]{0:T(128)S(1)} %subtract_reduce_fusion.expert_ref, s32[1]{0:T(128)} %bitcast.10.core_ref, bf16[8,16,240,256]{3,2,1,0:T(8,128)(2,1)} %bitcast.113, bf16[16,96,1024]{2,1,0:T(8,128)(2,1)} %all-to-all-done.refs_0_, ...), custom_call_target="tpu_custom_call" | custom-call | flops 8053063680 | bytes 68157440 | tf_op jit(solution)/shard_map/expert_rows/pallas_call | solution.py:101
  224.0 3.7 collective-permute-done.4.oth_ref
  227.7 1.9 copy-done.3
  229.6 1.9 copy-done.5
  231.5 16.4 %input_rows.1 = bf16[16,240,1024]{2,1,0:T(8,128)(2,1)} custom-call(s32[16]{0:T(128)S(1)} %subtract_reduce_fusion.expert_ref, s32[1]{0:T(128)} %bitcast.10.core_ref, bf16[16,240,256]{2,1,0:T(8,128)(2,1)S(1)} %get-tuple-element.21.own_ref.refs_5_, bf16[16,240,256]{2,1,0:T(8,128)(2,1)S(1)} %collective-permute-done.4.oth_ref, ...), custom_call_target="tpu_custom_call" | custom-call | flops 4026531840 | bytes 41943040 | tf_op jit(solution)/shard_map/input_rows/pallas_call | solution.py:152
  247.9 7.4 %all-to-all-start.3 = ((bf16[16,240,1024]{2,1,0:T(8,128)(2,1)}), bf16[16,240,1024]{2,1,0:T(8,128)(2,1)}, u32[]{:S(2)}, u32[]{:S(2)}) async-start(bf16[16,240,1024]{2,1,0:T(8,128)(2,1)} %input_rows.1), calls=%async_computation.5 | async-start | bytes 15728640 | tf_op jit(solution)/shard_map/all_to_all | solution.py:264
  256.4 114.6 %all-to-all-done.3 = bf16[16,240,1024]{2,1,0:T(8,128)(2,1)} async-done(((bf16[16,240,1024]{2,1,0:T(8,128)(2,1)}), bf16[16,240,1024]{2,1,0:T(8,128)(2,1)}, u32[]{:S(2)}, u32[]{:S(2)}) %all-to-all-start.3) | async-done | bytes 7864352 | tf_op jit(solution)/shard_map/all_to_all | solution.py:264
  371.0 7.0 %all-to-all-start.4 = ((bf16[16,240,256]{2,1,0:T(8,128)(2,1)}), bf16[16,240,256]{2,1,0:T(8,128)(2,1)}, u32[]{:S(2)}, u32[]{:S(2)}) async-start(bf16[16,240,256]{2,1,0:T(8,128)(2,1)} %bitcast.118), calls=%async_computation.6 | async-start | bytes 3932160 | tf_op jit(solution)/shard_map/all_to_all | solution.py:264
  378.1 6.5 %bitcast_convert_fusion = bf16[384,1024]{1,0:T(8,128)(2,1)S(1)} fusion(bf16[16,240,1024]{2,1,0:T(8,128)(2,1)} %all-to-all-done.3, s32[16,384]{1,0:T(8,128)S(1)} %copy-done.11), kind=kOutput, calls=%fused_computation.28 | convolution fusion | flops 3021766656 | bytes 8675328 | tf_op jit(solution)/shard_map/dot_general | solution.py:34
  386.1 29.1 %weight_grads.1 = (bf16[8,96,2048]{2,1,0:T(8,128)(2,1)}, bf16[8,96,2048]{2,1,0:T(8,128)(2,1)}, bf16[8,96,2048]{2,1,0:T(8,128)(2,1)}) custom-call(s32[24]{0:T(128)S(1)} %get-tuple-element.30.chunk_ref, s32[24]{0:T(128)S(1)} %get-tuple-element.29.expert_ref, s32[24]{0:T(128)S(1)} %get-tuple-element.28.real_ref, s32[24]{0:T(128)S(1)} %get-tuple-element.27.last_ref, ...), custom_call_target="tpu_custom_call" | custom-call | flops 6039797760 | bytes 47185920 | tf_op jit(solution)/shard_map/weight_grads/pallas_call | solution.py:211
  415.2 3.2 fusion.25
  418.5 4.0 fusion.40
  (90 shorter events, 8.8 us)
Async XLA Ops:
  7.2 10.4 %copy-start = (bf16[384,2048]{1,0:T(8,128)(2,1)S(1)}, bf16[384,2048]{1,0:T(8,128)(2,1)}, u32[]{:S(2)}) copy-start(bf16[384,2048]{1,0:T(8,128)(2,1)} %param.25) | copy-start | bytes 4718596
  7.2 44.9 %reduce-scatter.4.cloned.1.call-start = ((), (), s32[]{:S(2)}) async-start(), calls=%async_computation.8 | async-start | bytes 1769472 | tf_op jit(solution)/shard_map/reduce_scatter | solution.py:289
  7.2 13.8 %collective-permute-start = (bf16[8,96,2048]{2,1,0:T(8,128)(2,1)}, bf16[8,96,2048]{2,1,0:T(8,128)(2,1)}, u32[]{:S(2)}, u32[]{:S(2)}) collective-permute-start(bf16[8,96,2048]{2,1,0:T(8,128)(2,1)} %bitcast.107), channel_id=1, source_target_pairs={{0,1},{1,0},{2,3},{3,2},{4,5},{5,4},{6,7},{7,6},{8,9},{9,8},{10,11... | collective-permute-start | bytes 9437192 | tf_op jit(solution)/shard_map/ppermute | solution.py:268
  7.3 13.7 %collective-permute-start.1 = (bf16[8,96,2048]{2,1,0:T(8,128)(2,1)}, bf16[8,96,2048]{2,1,0:T(8,128)(2,1)}, u32[]{:S(2)}, u32[]{:S(2)}) collective-permute-start(bf16[8,96,2048]{2,1,0:T(8,128)(2,1)} %bitcast.110), channel_id=1, source_target_pairs={{0,1},{1,0},{2,3},{3,2},{4,5},{5,4},{6,7},{7,6},{8,9},{9,8},{10,11... | collective-permute-start | bytes 9437192 | tf_op jit(solution)/shard_map/ppermute | solution.py:268
  11.2 2.4 copy-start.20
  13.6 2.2 copy-start.17
  15.8 0.7 copy-start.18
  16.1 12.5 %copy-start.9 = (s32[16,384]{1,0:T(8,128)}, s32[16,384]{1,0:T(8,128)S(1)}, u32[]{:S(2)}) copy-start(s32[16,384]{1,0:T(8,128)S(1)} %fusion.44) | copy-start | bytes 73732
  21.0 53.5 %all-to-all-start = ((bf16[16,96,1024]{2,1,0:T(8,128)(2,1)}), bf16[16,96,1024]{2,1,0:T(8,128)(2,1)}, u32[]{:S(2)}, u32[]{:S(2)}) async-start(bf16[16,96,1024]{2,1,0:T(8,128)(2,1)} %bitcast.116), calls=%async_computation.1 | async-start | bytes 6291456 | tf_op jit(solution)/shard_map/all_to_all | solution.py:264
  28.5 157.9 %all-gather.3.cloned.1.call-start = ((), (), s32[]{:S(2)}) async-start(), calls=%async_computation.11 | async-start | bytes 17694720 | tf_op jit(solution)/shard_map/all_gather | solution.py:328
  104.7 1.5 copy-start.10
  104.7 1.5 copy-start.14
  104.7 266.3 %reduce-scatter.6.cloned.1.call-start = ((), (), s32[]{:S(2)}) async-start(), calls=%async_computation.9 | async-start | bytes 17694720 | tf_op jit(solution)/shard_map/reduce_scatter | solution.py:337
  109.9 59.0 %copy-start.19 = (s32[16,16]{1,0:T(8,128)S(1)}, s32[16,16]{1,0:T(8,128)}, u32[]{:S(2)}) copy-start(s32[16,16]{1,0:T(8,128)} %param.24) | copy-start | bytes 3076
  168.4 13.9 %collective-permute-start.3 = (bf16[16,144,1024]{2,1,0:T(8,128)(2,1)}, bf16[16,144,1024]{2,1,0:T(8,128)(2,1)}, u32[]{:S(2)}, u32[]{:S(2)}) collective-permute-start(bf16[16,144,1024]{2,1,0:T(8,128)(2,1)} %all_to_all.26.refs_2_), channel_id=1, source_target_pairs={{0,1},{1,0},{2,3},{3,2},{4,5},{5,4},{6,7},{7,6},{8,9},{9,8},{10,11... | collective-permute-start | bytes 14155784 | tf_op jit(solution)/shard_map/ppermute | solution.py:268
  168.4 13.9 %collective-permute-start.2 = (bf16[16,96,1024]{2,1,0:T(8,128)(2,1)}, bf16[16,96,1024]{2,1,0:T(8,128)(2,1)}, u32[]{:S(2)}, u32[]{:S(2)}) collective-permute-start(bf16[16,96,1024]{2,1,0:T(8,128)(2,1)} %all-to-all-done.refs_0_), channel_id=1, source_target_pairs={{0,1},{1,0},{2,3},{3,2},{4,5},{5,4},{6,7},{7,6},{8,9},{9,8},{10,11... | collective-permute-start | bytes 9437192 | tf_op jit(solution)/shard_map/ppermute | solution.py:268
  186.4 1.9 copy-start.2
  188.2 1.9 copy-start.4
  190.1 1.9 copy-start.6
  222.8 0.9 copy-start.7
  223.7 4.0 collective-permute-start.4
  227.7 1.9 copy-start.3
  229.6 1.9 copy-start.5
  247.9 7.8 %copy-start.11 = (s32[16,384]{1,0:T(8,128)S(1)}, s32[16,384]{1,0:T(8,128)}, u32[]{:S(2)}) copy-start(s32[16,384]{1,0:T(8,128)} %copy-done.9) | copy-start | bytes 73732
  247.9 7.8 %copy-start.15 = (f32[384,16]{0,1:T(8,128)S(1)}, f32[384,16]{0,1:T(8,128)}, u32[]{:S(2)}) copy-start(f32[384,16]{0,1:T(8,128)} %copy-done.13) | copy-start | bytes 73732
  247.9 123.1 %all-to-all-start.3 = ((bf16[16,240,1024]{2,1,0:T(8,128)(2,1)}), bf16[16,240,1024]{2,1,0:T(8,128)(2,1)}, u32[]{:S(2)}, u32[]{:S(2)}) async-start(bf16[16,240,1024]{2,1,0:T(8,128)(2,1)} %input_rows.1), calls=%async_computation.5 | async-start | bytes 15728640 | tf_op jit(solution)/shard_map/all_to_all | solution.py:264
  371.0 44.2 %all-to-all-start.4 = ((bf16[16,240,256]{2,1,0:T(8,128)(2,1)}), bf16[16,240,256]{2,1,0:T(8,128)(2,1)}, u32[]{:S(2)}, u32[]{:S(2)}) async-start(bf16[16,240,256]{2,1,0:T(8,128)(2,1)} %bitcast.118), calls=%async_computation.6 | async-start | bytes 3932160 | tf_op jit(solution)/shard_map/all_to_all | solution.py:264
  378.0 44.4 %reduce-scatter.8.cloned.1.call-start = ((), (), s32[]{:S(2)}) async-start(), calls=%async_computation.10 | async-start | bytes 983040 | tf_op jit(solution)/shard_map/reduce_scatter | solution.py:347
  384.6 1.5 copy-start.8
  415.2 3.3 copy-start.12
  415.2 3.3 copy-start.16
  418.4 4.0 copy-start.1
  (1 other events, 0.6 us)
Sparse Core Ops, SparseCore 0:
  15.9 36.1 reduce-scatter.3
  104.8 81.4 all-gather.2
  222.9 87.9 reduce-scatter.5
  385.7 23.0 reduce-scatter.7

commit v3 on v2

--- a/solution.py
+++ b/solution.py
@@ -19,7 +19,7 @@
 COLS = 256
 HALF = 1024
 STEPS = FETCH + EXP_GROUP
-SPLIT = (96, 144)
+SPLIT = (64, 176)
 
 epsilon = 1e-06
 bf16 = jnp.bfloat16
@@ -49,7 +49,7 @@
     return mixed.astype(bf16).reshape(tokens, heads * HEAD_DIM)
 
 
-def rows_kernel(expert_ref, core_ref, x_ref, *refs):
+def rows_kernel(order_ref, expert_ref, fresh_ref, core_ref, x_ref, *refs):
     g_refs = refs[: 2 * len(SPLIT)]
     wg_ref, wu_ref, wd_ref, out_ref, act_ref, dgu_ref, wgu, wdp = refs[2 * len(SPLIT) :]
     core = core_ref[0]
@@ -61,9 +61,11 @@
         wgu[PAD + UNITS :, :] = zeros
         wdp[UNITS:, :] = zeros
 
-    wgu[:UNITS, :] = wg_ref[0]
-    wgu[PAD : PAD + UNITS, :] = wu_ref[0]
-    wdp[:UNITS, :] = wd_ref[0]
+    @pl.when(fresh_ref[pl.program_id(0)] == 1)
+    def _():
+        wgu[:UNITS, :] = wg_ref[0]
+        wgu[PAD : PAD + UNITS, :] = wu_ref[0]
+        wdp[:UNITS, :] = wd_ref[0]
 
     pre = mm(x_ref[0, 0], wgu[:, :COLS], NT)
     for block in range(1, D // COLS):
@@ -90,18 +92,18 @@
         start += size
 
 
-def rows_call(experts, core, x_rows, g_parts, wg, wu, wd):
-    weight = pl.BlockSpec((1, UNITS, D), lambda i, e, c: (e[i], 0, 0))
-    cols8 = pl.BlockSpec((8, 1, CAP, COLS), lambda i, e, c: (0, i, 0, 0))
+def rows_call(scalars, x_rows, g_parts, wg, wu, wd):
+    weight = pl.BlockSpec((1, UNITS, D), lambda i, o, e, n, c: (e[i], 0, 0))
+    cols8 = pl.BlockSpec((8, 1, CAP, COLS), lambda i, o, e, n, c: (0, o[i], 0, 0))
 
     def flat(size, width):
-        return pl.BlockSpec((1, size, width), lambda i, e, c: (i, 0, 0))
+        return pl.BlockSpec((1, size, width), lambda i, o, e, n, c: (o[i], 0, 0))
 
     halves = [flat(size, HALF) for size in SPLIT for _ in range(2)]
     return pl.pallas_call(
         rows_kernel,
         grid_spec=pltpu.PrefetchScalarGridSpec(
-            num_scalar_prefetch=2,
+            num_scalar_prefetch=4,
             grid=(FETCH,),
             in_specs=[cols8, *halves, weight, weight, weight],
             out_specs=[cols8, flat(CAP, PAD), flat(CAP, 2 * PAD)],
@@ -112,16 +114,16 @@
             jax.ShapeDtypeStruct((FETCH, CAP, PAD), bf16),
             jax.ShapeDtypeStruct((FETCH, CAP, 2 * PAD), bf16),
         ],
-        compiler_params=pltpu.CompilerParams(vmem_limit_bytes=32 << 20),
+        compiler_params=pltpu.CompilerParams(vmem_limit_bytes=56 << 20),
         cost_estimate=pl.CostEstimate(
             flops=2 * 4 * FETCH * CAP * D * PAD, bytes_accessed=65 << 20, transcendentals=0
         ),
         name="expert_rows",
-    )(experts, core, x_rows, *g_parts, wg, wu, wd)
+    )(*scalars, x_rows, *g_parts, wg, wu, wd)
 
 
 def input_kernel(
-    expert_ref, core_ref, own_ref, oth_ref, wg_ref, wu_ref, wg_oth_ref, wu_oth_ref,
+    order_ref, expert_ref, fresh_ref, core_ref, own_ref, oth_ref, wg_ref, wu_ref, wg_oth_ref, wu_oth_ref,
     d_ref, w_own, w_oth,
 ):
     core = core_ref[0]
@@ -133,38 +135,43 @@
             ref[UNITS:PAD, :] = zeros
             ref[PAD + UNITS :, :] = zeros
 
+    @pl.when(fresh_ref[pl.program_id(0)] == 1)
+    def _():
+        for block in range(HALF // COLS):
+            place = slice(block * COLS, (block + 1) * COLS)
+            col = pl.ds(pl.multiple_of((2 * block + core) * COLS, COLS), COLS)
+            w_own[:UNITS, place] = wg_ref[0, :, col]
+            w_own[PAD : PAD + UNITS, place] = wu_ref[0, :, col]
+            w_oth[:UNITS, place] = wg_oth_ref[0, :, col]
+            w_oth[PAD : PAD + UNITS, place] = wu_oth_ref[0, :, col]
+
     own, oth = own_ref[0], oth_ref[0]
     for block in range(HALF // COLS):
         place = slice(block * COLS, (block + 1) * COLS)
-        col = pl.ds(pl.multiple_of((2 * block + core) * COLS, COLS), COLS)
-        w_own[:UNITS, place] = wg_ref[0, :, col]
-        w_own[PAD : PAD + UNITS, place] = wu_ref[0, :, col]
-        w_oth[:UNITS, place] = wg_oth_ref[0, :, col]
-        w_oth[PAD : PAD + UNITS, place] = wu_oth_ref[0, :, col]
         d_ref[0, :, place] = (mm(own, w_own[:, place], NN) + mm(oth, w_oth[:, place], NN)).astype(
             bf16
         )
 
 
-def input_call(experts, core, dgu, dgu_oth, wg, wu, wg_oth, wu_oth):
-    weight = pl.BlockSpec((1, UNITS, D), lambda i, e, c: (e[i], 0, 0))
-    flat = pl.BlockSpec((1, CAP, 2 * PAD), lambda i, e, c: (i, 0, 0))
+def input_call(scalars, dgu, dgu_oth, wg, wu, wg_oth, wu_oth):
+    weight = pl.BlockSpec((1, UNITS, D), lambda i, o, e, n, c: (e[i], 0, 0))
+    flat = pl.BlockSpec((1, CAP, 2 * PAD), lambda i, o, e, n, c: (o[i], 0, 0))
     return pl.pallas_call(
         input_kernel,
         grid_spec=pltpu.PrefetchScalarGridSpec(
-            num_scalar_prefetch=2,
+            num_scalar_prefetch=4,
             grid=(FETCH,),
             in_specs=[flat, flat, weight, weight, weight, weight],
-            out_specs=pl.BlockSpec((1, CAP, HALF), lambda i, e, c: (i, 0, 0)),
+            out_specs=pl.BlockSpec((1, CAP, HALF), lambda i, o, e, n, c: (o[i], 0, 0)),
             scratch_shapes=[pltpu.VMEM((2 * PAD, HALF), bf16)] * 2,
         ),
         out_shape=jax.ShapeDtypeStruct((FETCH, CAP, HALF), bf16),
-        compiler_params=pltpu.CompilerParams(vmem_limit_bytes=32 << 20),
+        compiler_params=pltpu.CompilerParams(vmem_limit_bytes=56 << 20),
         cost_estimate=pl.CostEstimate(
             flops=2 * 2 * FETCH * CAP * D * PAD, bytes_accessed=40 << 20, transcendentals=0
         ),
         name="input_rows",
-    )(experts, core, dgu, dgu_oth, wg, wu, wg_oth, wu_oth)
+    )(*scalars, dgu, dgu_oth, wg, wu, wg_oth, wu_oth)
 
 
 def grads_kernel(chunk_ref, expert_ref, real_ref, last_ref, core_ref, x_ref, *refs):
@@ -223,7 +230,7 @@
             scratch_shapes=[pltpu.VMEM((2 * PAD, D), f32), pltpu.VMEM((PAD, D), f32)],
         ),
         out_shape=[jax.ShapeDtypeStruct((EXP_GROUP, UNITS, D), bf16)] * 3,
-        compiler_params=pltpu.CompilerParams(vmem_limit_bytes=32 << 20),
+        compiler_params=pltpu.CompilerParams(vmem_limit_bytes=56 << 20),
         cost_estimate=pl.CostEstimate(
             flops=2 * 3 * FETCH * CAP * D * PAD, bytes_accessed=45 << 20, transcendentals=0
         ),
@@ -250,6 +257,19 @@
     real = (jnp.arange(STEPS) >= EXP_GROUP).astype(jnp.int32)
     last = (count == 0).astype(jnp.int32)
     return ordered(chunk), ordered(owner), ordered(real), ordered(last)
+
+
+def rows_order(experts):
+    ids = jnp.arange(FETCH, dtype=jnp.int32)
+    key = experts * FETCH + ids
+    rank = jnp.sum((key[None, :] < key[:, None]).astype(jnp.int32), axis=1)
+    place = rank[:, None] == ids[None, :]
+    order = jnp.sum(jnp.where(place, ids[:, None], 0), axis=0)
+    expert = jnp.sum(jnp.where(place, experts[:, None], 0), axis=0)
+    earlier = (experts[None, :] == experts[:, None]) & (ids[None, :] < ids[:, None])
+    new = 1 - jnp.any(earlier, axis=1).astype(jnp.int32)
+    fresh = jnp.sum(jnp.where(place, new[:, None], 0), axis=0)
+    return order, expert, fresh
 
 
 Z_GROUPS = [[0, 2, 4, 6], [1, 3, 5, 7]]
@@ -313,7 +333,9 @@
         pick, weight = one_hot(start, size)
         return (mm(pick, cot_half, NN) * weight).astype(bf16).reshape(FETCH, size, HALF)
 
-    g_first = exchange(after(grad_rows(0, SPLIT[0]), wg_oth, wu_oth))
+    pick, row_weight = one_hot(0, CAP)
+    g_first = exchange(after(grad_rows(0, SPLIT[0]), wg_oth, wu_oth, pick, row_weight))
+    g_first_oth = swap(g_first)
 
     first_col = hidden * COLS
     res_share = lax.dynamic_slice_in_dim(residual, first_col, COLS, 1)
@@ -322,23 +344,26 @@
     square = lax.psum(jnp.sum(stream * stream, axis=1), "hidden") / D
     normed = (stream * lax.rsqrt(square + epsilon)[:, None] * gain[None, :]).astype(bf16)
 
-    pick, row_weight = one_hot(0, CAP)
     x_part = mm(pick, normed, NN).astype(bf16).reshape(FETCH, CAP, COLS)
-    x_part = exchange(after(x_part, g_first))
+    x_part = exchange(after(x_part, g_first_oth))
     x_rows = lax.all_gather(x_part, "hidden", axis=0, tiled=False)
     g_second = exchange(after(grad_rows(SPLIT[0], SPLIT[1]), x_part))
-    g_parts = [g_first, swap(g_first), g_second, swap(g_second)]
+    g_parts = [g_first, g_first_oth, g_second, swap(g_second)]
 
     own_col = lax.dynamic_slice_in_dim(fetch_list, group, 1, 1)[:, 0]
     experts = own_col - group * EXP_GROUP
-    out_rows, act, dgu = rows_call(experts, core_arr, x_rows, g_parts, wg, wu, w_down)
-    d_half = input_call(experts, core_arr, dgu, swap(dgu), wg, wu, wg_oth, wu_oth)
+    scalars = (*rows_order(experts), core_arr)
+    tables = grad_order(experts)
+    high = row_weight.astype(bf16)
+    low = (row_weight - high.astype(f32)).astype(bf16)
+    x_rows, high, low, *tables = lax.optimization_barrier((x_rows, high, low, *tables))
+    out_rows, act, dgu = rows_call(scalars, x_rows, g_parts, wg, wu, w_down)
+    d_half = input_call(scalars, dgu, swap(dgu), wg, wu, wg_oth, wu_oth)
 
     out_share = lax.psum_scatter(out_rows, "hidden", scatter_dimension=0, tiled=True)[0]
     d_back = exchange(d_half)
-    chunk, expert, real, last = grad_order(experts)
     grad_gate, grad_up, grad_down = grads_call(
-        chunk, expert, real, last, core_arr, x_rows, g_parts, act, dgu
+        *tables, core_arr, x_rows, g_parts, after(act, d_back), dgu
     )
     out_back = exchange(after(out_share, d_back))
 
@@ -348,8 +373,6 @@
         d_tok, "hidden", scatter_dimension=0, tiled=True, axis_index_groups=Z_GROUPS
     )[0]
 
-    high = row_weight.astype(bf16)
-    low = (row_weight - high.astype(f32)).astype(bf16)
     out_back = out_back.reshape(-1, COLS)
     moe = mm(pick * high, out_back, TN) + mm(pick * low, out_back, TN)
     layer_out = (stream + moe).astype(bf16)

time: 432 us -> 413 us (0.956)
  waiting for transfers between devices: 162 us -> 48.8 us
  blocking collectives: 102 us -> 209 us
  starting transfers between devices: 23.4 us -> 15.1 us
  local copies, waits for them, and re-layouts: 13.5 us -> 5.34 us
  Pallas kernels: 76.2 us -> 82.5 us
    all_to_all x2 -> x3, blocking collectives: 88.6 us -> 196 us  [exchange(): return lax.all_to_all(value, axis, split_axis=0, concat_axis=0, tiled=True)]
    all_to_all x3 -> x2, waiting for transfers between devices: 120 us -> 28.9 us  [exchange(): return lax.all_to_all(value, axis, split_axis=0, concat_axis=0, tiled=True)]
    reduce_scatter x1, waiting for transfers between devices: 20.7 us -> 8.07 us  [shards(): attn = lax.psum_scatter(part, 'hidden', scatter_dimension=0, tiled=True)[0]]
    ppermute x5, waiting for transfers between devices: 16.9 us -> 4.29 us  [swap(): return lax.ppermute(value, 'hidden', PAIRS)]
    unnamed x42 -> x24, local copies, waits for them, and re-layouts: 11.4 us -> 2.92 us
    all_to_all x3 -> x2, starting transfers between devices: 21.9 us -> 14.2 us  [exchange(): return lax.all_to_all(value, axis, split_axis=0, concat_axis=0, tiled=True)]
  transfers between devices with their start and end apart: 12 -> 11, of which waited for: 6 -> 5; matrix products, arithmetic and copies ran while one was open for 9% -> 9% of each run, Pallas kernels for 11% -> 12%
where the time goes in v3:
time: 413 us; the launch traced here: 411 us
  blocking collectives  209 us (51%)
  Pallas kernels  82.5 us (20%)
  waiting for transfers between devices  48.8 us (12%)
  matrix products  28.6 us (7%)
  starting transfers between devices  15.1 us (4%)
  between operations  14.1 us (3%)
  other arithmetic  7.11 us (2%)
  local copies, waits for them, and re-layouts  5.34 us (1%)
    all_to_all x3, blocking collectives, exchange(): return lax.all_to_all(value, axis, split_axis=0, concat_axis=0, tiled=True)  196 us
    pallas_call x1, Pallas kernels, rows_call(): pl.pallas_call(rows_kernel, grid_spec=pltpu.PrefetchScalarGridSpec(num_sc...  33 us
    pallas_call x1, Pallas kernels, grads_call(): pl.pallas_call(grads_kernel, grid_spec=pltpu.PrefetchScalarGridSpec(num_s...  30.2 us
    all_to_all x2, waiting for transfers between devices, exchange(): return lax.all_to_all(value, axis, split_axis=0, concat_axis=0, tiled=True)  28.9 us
    dot_general x7, matrix products, mm(): return lax.dot_general(a, b, dims, preferred_element_type=f32)  20.8 us
    pallas_call x1, Pallas kernels, input_call(): pl.pallas_call(input_kernel, grid_spec=pltpu.PrefetchScalarGridSpec(num_s...  19.3 us
    all_to_all x2, starting transfers between devices, exchange(): return lax.all_to_all(value, axis, split_axis=0, concat_axis=0, tiled=True)  14.2 us
    psum x1, blocking collectives, shards(): square = lax.psum(jnp.sum(stream * stream, axis=1), 'hidden') / D  13.1 us
  transfers between devices with their start and end apart: 11, of which 5 were waited for; matrix products, arithmetic and copies ran while one was open for 9% of the time, Pallas kernels for 12%

profile of v3, /device:TPU:6, one launch (start us, length us, event | category | flops | bytes accessed | tf_op | source)
XLA Modules:
  0.0 410.7 jit_solution(4167299971822943291)
XLA Ops:
  7.9 3.4 fusion.85
  11.3 2.3 convolution_convert_fusion.1
  13.6 2.2 fusion.18
  16.6 2.6 multiply_convert_fusion.1
  19.2 7.4 %all-to-all-start = ((bf16[16,64,1024]{2,1,0:T(8,128)(2,1)}), bf16[16,64,1024]{2,1,0:T(8,128)(2,1)}, u32[]{:S(2)}, u32[]{:S(2)}) async-start(bf16[16,64,1024]{2,1,0:T(8,128)(2,1)} %bitcast.117), calls=%async_computation.1 | async-start | bytes 4194304 | tf_op jit(solution)/shard_map/all_to_all | solution.py:284
  26.7 0.7 reduce-scatter.4.cloned.1.call-update
  27.4 28.9 %all-to-all-done.refs_0_ = bf16[16,64,1024]{2,1,0:T(8,128)(2,1)} async-done(((bf16[16,64,1024]{2,1,0:T(8,128)(2,1)}), bf16[16,64,1024]{2,1,0:T(8,128)(2,1)}, u32[]{:S(2)}, u32[]{:S(2)}) %all-to-all-start) | async-done | bytes 2097184 | tf_op jit(solution)/shard_map/all_to_all | solution.py:284
  56.4 0.9 bitcast_compare_fusion
  57.3 0.8 dynamic_slice.21
  58.1 8.1 %reduce-scatter.4.cloned.1.call-done = bf16[1,384,256]{2,1,0:T(8,128)(2,1)} async-done(((bf16[8,384,256]{2,1,0:T(8,128)(2,1)}), bf16[1,384,256]{2,1,0:T(8,128)(2,1)}) %reduce-scatter.4.cloned.1.call-update) | async-done | bytes 196624 | tf_op jit(solution)/shard_map/reduce_scatter | solution.py:309
  66.1 1.2 multiply_reduce_fusion
  67.3 13.1 %psum.7 = f32[384]{0:T(512)S(1)} all-reduce(f32[384]{0:T(512)S(1)} %multiply_reduce_fusion), channel_id=1, replica_groups=mesh['group'=16,'hidden'=8] {'hidden'}, use_global_device_ids=true, to_apply=%region_5.6 | all-reduce | flops 384 | bytes 3072 | tf_op jit(solution)/shard_map/psum | solution.py:344
  80.4 2.3 convolution_convert_fusion
  82.7 30.8 %all_to_all.25 = bf16[16,240,256]{2,1,0:T(8,128)(2,1)} all-to-all(bf16[16,240,256]{2,1,0:T(8,128)(2,1)S(1)} %bitcast.119), channel_id=1, replica_groups=mesh['group'=16,'hidden'=8] {'group'}, dimensions={0} | all-to-all | bytes 3932160 | tf_op jit(solution)/shard_map/all_to_all | solution.py:284
  113.7 0.7 select_reduce_fusion.1
  115.1 3.5 multiply_convert_fusion
  118.6 70.5 %all_to_all.26.refs_2_ = bf16[16,176,1024]{2,1,0:T(8,128)(2,1)} all-to-all(bf16[16,176,1024]{2,1,0:T(8,128)(2,1)S(1)} %bitcast.115), channel_id=1, replica_groups=mesh['group'=16,'hidden'=8] {'group'}, dimensions={0} | all-to-all | bytes 11534336 | tf_op jit(solution)/shard_map/all_to_all | solution.py:284
  189.1 0.7 select_reduce_fusion
  191.6 0.7 select_reduce_fusion.4
  192.3 6.8 %all-gather.3.cloned.1.call-done = bf16[128,240,256]{2,1,0:T(8,128)(2,1)} async-done(((bf16[16,240,256]{2,1,0:T(8,128)(2,1)}), bf16[128,240,256]{2,1,0:T(8,128)(2,1)}) %all-gather.3.cloned.1.call-update) | async-done | bytes 15728656 | tf_op jit(solution)/shard_map/all_gather | solution.py:349
  199.6 33.0 %expert_rows.1 = (bf16[8,16,240,256]{3,2,1,0:T(8,128)(2,1)}, bf16[16,240,128]{2,1,0:T(8,128)(2,1)}, bf16[16,240,256]{2,1,0:T(8,128)(2,1)}) custom-call(s32[16]{0:T(128)} %get-tuple-element.53.order_ref, s32[16]{0:T(128)} %get-tuple-element.52.expert_ref, s32[16]{0:T(128)} %get-tuple-element.51.fresh_ref, s32[1]{0:T(128)} %bitcast.17.core_ref, ...), custom_call_target="tpu_custom_call" | custom-call | flops 8053063680 | bytes 68157440 | tf_op jit(solution)/shard_map/expert_rows/pallas_call | solution.py:103
  232.6 1.5 copy-done.2
  234.3 3.8 collective-permute-done.4.oth_ref
  238.1 1.3 copy-done.3
  239.4 19.3 %input_rows.1 = bf16[16,240,1024]{2,1,0:T(8,128)(2,1)} custom-call(s32[16]{0:T(128)} %get-tuple-element.53.order_ref, s32[16]{0:T(128)} %get-tuple-element.52.expert_ref, s32[16]{0:T(128)} %get-tuple-element.51.fresh_ref, s32[1]{0:T(128)} %bitcast.17.core_ref, bf16[16,240,256]{2,1,0:T(8,128)(2,1)} %get-tuple-element.31.own_ref.refs_5_, ...), custom_call_target="tpu_custom_call" | custom-call | flops 4026531840 | bytes 41943040 | tf_op jit(solution)/shard_map/input_rows/pallas_call | solution.py:159
  258.6 94.8 %all_to_all.27 = bf16[16,240,1024]{2,1,0:T(8,128)(2,1)} all-to-all(bf16[16,240,1024]{2,1,0:T(8,128)(2,1)} %input_rows.1), channel_id=1, replica_groups=mesh['group'=16,'hidden'=8] {'group'}, dimensions={0} | all-to-all | bytes 15728640 | tf_op jit(solution)/shard_map/all_to_all | solution.py:284
  353.4 6.8 %all-to-all-start.4 = ((bf16[16,240,256]{2,1,0:T(8,128)(2,1)}), bf16[16,240,256]{2,1,0:T(8,128)(2,1)S(1)}, u32[]{:S(2)}, u32[]{:S(2)}) async-start(bf16[16,240,256]{2,1,0:T(8,128)(2,1)} %bitcast.118), calls=%async_computation.6 | async-start | bytes 3932160 | tf_op jit(solution)/shard_map/all_to_all | solution.py:284
  360.3 6.5 %bitcast_convert_fusion = bf16[384,1024]{1,0:T(8,128)(2,1)S(1)} fusion(bf16[16,240,1024]{2,1,0:T(8,128)(2,1)} %all_to_all.27, s32[16,384]{1,0:T(8,128)S(1)} %copy-done.5), kind=kOutput, calls=%fused_computation.25 | convolution fusion | flops 3021766656 | bytes 8675328 | tf_op jit(solution)/shard_map/dot_general | solution.py:34
  366.7 1.0 copy.76
  368.0 30.2 %weight_grads.1 = (bf16[8,96,2048]{2,1,0:T(8,128)(2,1)}, bf16[8,96,2048]{2,1,0:T(8,128)(2,1)}, bf16[8,96,2048]{2,1,0:T(8,128)(2,1)}) custom-call(s32[24]{0:T(128)} %get-tuple-element.34.chunk_ref, s32[24]{0:T(128)} %get-tuple-element.35.expert_ref, s32[24]{0:T(128)} %get-tuple-element.36.real_ref, s32[24]{0:T(128)} %get-tuple-element.37.last_ref, ...), custom_call_target="tpu_custom_call" | custom-call | flops 6039797760 | bytes 47185920 | tf_op jit(solution)/shard_map/weight_grads/pallas_call | solution.py:218
  398.3 2.5 fusion.25
  400.9 3.3 fusion.40
  (80 shorter events, 5.4 us)
Async XLA Ops:
  7.2 9.5 %copy-start = (bf16[384,2048]{1,0:T(8,128)(2,1)S(1)}, bf16[384,2048]{1,0:T(8,128)(2,1)}, u32[]{:S(2)}) copy-start(bf16[384,2048]{1,0:T(8,128)(2,1)} %param.25) | copy-start | bytes 4718596
  7.2 12.0 %collective-permute-start = (bf16[8,96,2048]{2,1,0:T(8,128)(2,1)}, bf16[8,96,2048]{2,1,0:T(8,128)(2,1)}, u32[]{:S(2)}, u32[]{:S(2)}) collective-permute-start(bf16[8,96,2048]{2,1,0:T(8,128)(2,1)} %bitcast.109), channel_id=1, source_target_pairs={{0,1},{1,0},{2,3},{3,2},{4,5},{5,4},{6,7},{7,6},{8,9},{9,8},{10,11... | collective-permute-start | bytes 9437192 | tf_op jit(solution)/shard_map/ppermute | solution.py:288
  7.3 12.0 %collective-permute-start.1 = (bf16[8,96,2048]{2,1,0:T(8,128)(2,1)}, bf16[8,96,2048]{2,1,0:T(8,128)(2,1)}, u32[]{:S(2)}, u32[]{:S(2)}) collective-permute-start(bf16[8,96,2048]{2,1,0:T(8,128)(2,1)} %bitcast.112), channel_id=1, source_target_pairs={{0,1},{1,0},{2,3},{3,2},{4,5},{5,4},{6,7},{7,6},{8,9},{9,8},{10,11... | collective-permute-start | bytes 9437192 | tf_op jit(solution)/shard_map/ppermute | solution.py:288
  11.3 2.4 copy-start.11
  13.6 2.2 copy-start.8
  13.6 2.2 copy-start.9
  16.0 173.1 %copy-start.4 = (s32[16,384]{1,0:T(8,128)}, s32[16,384]{1,0:T(8,128)S(1)}, u32[]{:S(2)}) copy-start(s32[16,384]{1,0:T(8,128)S(1)} %fusion.44) | copy-start | bytes 73732
  19.2 37.1 %all-to-all-start = ((bf16[16,64,1024]{2,1,0:T(8,128)(2,1)}), bf16[16,64,1024]{2,1,0:T(8,128)(2,1)}, u32[]{:S(2)}, u32[]{:S(2)}) async-start(bf16[16,64,1024]{2,1,0:T(8,128)(2,1)} %bitcast.117), calls=%async_computation.1 | async-start | bytes 4194304 | tf_op jit(solution)/shard_map/all_to_all | solution.py:284
  26.7 39.5 %reduce-scatter.4.cloned.1.call-start = ((), (), s32[]{:S(2)}) async-start(), calls=%async_computation.8 | async-start | bytes 1769472 | tf_op jit(solution)/shard_map/reduce_scatter | solution.py:309
  27.4 171.7 %all-gather.3.cloned.1.call-start = ((), (), s32[]{:S(2)}) async-start(), calls=%async_computation.11 | async-start | bytes 17694720 | tf_op jit(solution)/shard_map/all_gather | solution.py:349
  56.3 26.3 %collective-permute-start.2 = (bf16[16,64,1024]{2,1,0:T(8,128)(2,1)}, bf16[16,64,1024]{2,1,0:T(8,128)(2,1)}, u32[]{:S(2)}, u32[]{:S(2)}) collective-permute-start(bf16[16,64,1024]{2,1,0:T(8,128)(2,1)} %all-to-all-done.refs_0_), channel_id=1, source_target_pairs={{0,1},{1,0},{2,3},{3,2},{4,5},{5,4},{6,7},{7,6},{8,9},{9,8},{10,11... | collective-permute-start | bytes 6291464 | tf_op jit(solution)/shard_map/ppermute | solution.py:288
  113.5 239.9 %reduce-scatter.6.cloned.1.call-start = ((), (), s32[]{:S(2)}) async-start(), calls=%async_computation.9 | async-start | bytes 17694720 | tf_op jit(solution)/shard_map/reduce_scatter | solution.py:363
  118.6 71.3 %copy-start.10 = (s32[16,16]{1,0:T(8,128)S(1)}, s32[16,16]{1,0:T(8,128)}, u32[]{:S(2)}) copy-start(s32[16,16]{1,0:T(8,128)} %param.24) | copy-start | bytes 3076
  189.1 10.5 %collective-permute-start.3 = (bf16[16,176,1024]{2,1,0:T(8,128)(2,1)}, bf16[16,176,1024]{2,1,0:T(8,128)(2,1)}, u32[]{:S(2)}, u32[]{:S(2)}) collective-permute-start(bf16[16,176,1024]{2,1,0:T(8,128)(2,1)} %all_to_all.26.refs_2_), channel_id=1, source_target_pairs={{0,1},{1,0},{2,3},{3,2},{4,5},{5,4},{6,7},{7,6},{8,9},{9,8},{10,11... | collective-permute-start | bytes 17301512 | tf_op jit(solution)/shard_map/ppermute | solution.py:288
  232.6 1.5 copy-start.2
  234.1 4.0 collective-permute-start.4
  238.1 1.3 copy-start.3
  353.4 6.8 %copy-start.5 = (s32[16,384]{1,0:T(8,128)S(1)}, s32[16,384]{1,0:T(8,128)}, u32[]{:S(2)}) copy-start(s32[16,384]{1,0:T(8,128)} %copy-done.4) | copy-start | bytes 73732
  353.4 44.8 %all-to-all-start.4 = ((bf16[16,240,256]{2,1,0:T(8,128)(2,1)}), bf16[16,240,256]{2,1,0:T(8,128)(2,1)S(1)}, u32[]{:S(2)}, u32[]{:S(2)}) async-start(bf16[16,240,256]{2,1,0:T(8,128)(2,1)} %bitcast.118), calls=%async_computation.6 | async-start | bytes 3932160 | tf_op jit(solution)/shard_map/all_to_all | solution.py:284
  360.2 43.9 %reduce-scatter.8.cloned.1.call-start = ((), (), s32[]{:S(2)}) async-start(), calls=%async_computation.10 | async-start | bytes 983040 | tf_op jit(solution)/shard_map/reduce_scatter | solution.py:372
  398.3 2.6 copy-start.6
  398.3 2.5 copy-start.7
  398.3 5.8 %copy-start.1 = (bf16[384,2048]{1,0:T(8,128)(2,1)S(1)}, bf16[384,2048]{1,0:T(8,128)(2,1)}, u32[]{:S(2)}) copy-start(bf16[384,2048]{1,0:T(8,128)(2,1)} %param.25) | copy-start | bytes 4718596
Sparse Core Ops, SparseCore 0:
  30.5 35.6 reduce-scatter.3
  113.6 85.4 all-gather.2
  232.7 85.1 reduce-scatter.5
  367.8 21.3 reduce-scatter.7

commit v4 on v3

--- a/solution.py
+++ b/solution.py
@@ -51,48 +51,64 @@
 
 def rows_kernel(order_ref, expert_ref, fresh_ref, core_ref, x_ref, *refs):
     g_refs = refs[: 2 * len(SPLIT)]
-    wg_ref, wu_ref, wd_ref, out_ref, act_ref, dgu_ref, wgu, wdp = refs[2 * len(SPLIT) :]
+    (
+        wg_ref, wu_ref, wd_ref, wg_oth_ref, wu_oth_ref, wd_oth_ref,
+        out_ref, act_ref, dgu_ref, d_ref, wgu, wdp,
+    ) = refs[2 * len(SPLIT) :]
+    step = pl.program_id(0)
     core = core_ref[0]
 
-    @pl.when(pl.program_id(0) == 0)
-    def _():
-        zeros = jnp.zeros((PAD - UNITS, D), bf16)
-        wgu[UNITS:PAD, :] = zeros
-        wgu[PAD + UNITS :, :] = zeros
-        wdp[UNITS:, :] = zeros
-
-    @pl.when(fresh_ref[pl.program_id(0)] == 1)
-    def _():
-        wgu[:UNITS, :] = wg_ref[0]
-        wgu[PAD : PAD + UNITS, :] = wu_ref[0]
-        wdp[:UNITS, :] = wd_ref[0]
-
-    pre = mm(x_ref[0, 0], wgu[:, :COLS], NT)
-    for block in range(1, D // COLS):
-        pre = pre + mm(x_ref[block, 0], wgu[:, block * COLS : (block + 1) * COLS], NT)
-    gate, up = pre[:, :PAD], pre[:, PAD:]
-    sig = jax.nn.sigmoid(gate)
-    swish = gate * sig
-    act = (swish * up).astype(bf16)
+    @pl.when(step == 0)
+    def _():
+        for ref in (wgu, wdp):
+            for start in range(0, ref.shape[0], PAD):
+                ref[start + UNITS : start + PAD, :] = jnp.zeros((PAD - UNITS, D), bf16)
+
+    @pl.when(fresh_ref[step] == 1)
+    def _():
+        for i, ref in enumerate((wg_ref, wu_ref, wg_oth_ref, wu_oth_ref)):
+            wgu[i * PAD : i * PAD + UNITS, :] = ref[0]
+        own = pl.ds(pl.multiple_of(core * HALF, HALF), HALF)
+        oth = pl.ds(pl.multiple_of(HALF - core * HALF, HALF), HALF)
+        for i, ref in enumerate((wd_ref, wd_oth_ref)):
+            wdp[i * PAD : i * PAD + UNITS, :HALF] = ref[0, :, own]
+            wdp[i * PAD : i * PAD + UNITS, HALF:] = ref[0, :, oth]
+
+    x = jnp.concatenate([x_ref[block, 0] for block in range(D // COLS)], axis=1)
+    pre = mm(x, wgu[...], NT)
+    g = jnp.concatenate(
+        [
+            jnp.concatenate([g_refs[2 * i][0], g_refs[2 * i + 1][0]], axis=1)
+            for i in range(len(SPLIT))
+        ],
+        axis=0,
+    )
+    d_act = mm(g, wdp[...], NT)
+    hidden = []
+    for i in range(2):
+        gate = pre[:, 2 * i * PAD : (2 * i + 1) * PAD]
+        up = pre[:, (2 * i + 1) * PAD : (2 * i + 2) * PAD]
+        d_part = d_act[:, i * PAD : (i + 1) * PAD]
+        sig = jax.nn.sigmoid(gate)
+        swish = gate * sig
+        if i == 0:
+            act = (swish * up).astype(bf16)
+        hidden.append((d_part * up * sig * (1.0 + gate * (1.0 - sig))).astype(bf16))
+        hidden.append((d_part * swish).astype(bf16))
     act_ref[0] = act
-    for block in range(D // COLS):
-        out_ref[block, 0] = mm(act, wdp[:, block * COLS : (block + 1) * COLS], NN).astype(bf16)
-    own = pl.multiple_of(core * HALF, HALF)
-    oth = pl.multiple_of(HALF - core * HALF, HALF)
-    start = 0
-    for i, size in enumerate(SPLIT):
-        d_act = mm(g_refs[2 * i][0], wdp[:, pl.ds(own, HALF)], NT)
-        d_act = d_act + mm(g_refs[2 * i + 1][0], wdp[:, pl.ds(oth, HALF)], NT)
-        rows = slice(start, start + size)
-        gate_i, up_i, sig_i, swish_i = gate[rows], up[rows], sig[rows], swish[rows]
-        dgu_ref[0, rows, :PAD] = (
-            d_act * up_i * sig_i * (1.0 + gate_i * (1.0 - sig_i))
-        ).astype(bf16)
-        dgu_ref[0, rows, PAD:] = (d_act * swish_i).astype(bf16)
-        start += size
-
-
-def rows_call(scalars, x_rows, g_parts, wg, wu, wd):
+    dgu_ref[0, :, :PAD] = hidden[0]
+    dgu_ref[0, :, PAD:] = hidden[1]
+    for half, base in enumerate((core * 4, 4 - core * 4)):
+        for block in range(4):
+            col = half * HALF + block * COLS
+            out_ref[base + block, 0] = mm(act, wdp[:PAD, col : col + COLS], NN).astype(bf16)
+    both = jnp.concatenate(hidden, axis=1)
+    for block in range(4):
+        col = pl.ds(pl.multiple_of((2 * block + core) * COLS, COLS), COLS)
+        d_ref[0, :, block * COLS : (block + 1) * COLS] = mm(both, wgu[:, col], NN).astype(bf16)
+
+
+def rows_call(scalars, x_rows, g_parts, weights):
     weight = pl.BlockSpec((1, UNITS, D), lambda i, o, e, n, c: (e[i], 0, 0))
     cols8 = pl.BlockSpec((8, 1, CAP, COLS), lambda i, o, e, n, c: (0, o[i], 0, 0))
 
@@ -105,73 +121,22 @@
         grid_spec=pltpu.PrefetchScalarGridSpec(
             num_scalar_prefetch=4,
             grid=(FETCH,),
-            in_specs=[cols8, *halves, weight, weight, weight],
-            out_specs=[cols8, flat(CAP, PAD), flat(CAP, 2 * PAD)],
-            scratch_shapes=[pltpu.VMEM((2 * PAD, D), bf16), pltpu.VMEM((PAD, D), bf16)],
+            in_specs=[cols8, *halves, *[weight] * 6],
+            out_specs=[cols8, flat(CAP, PAD), flat(CAP, 2 * PAD), flat(CAP, HALF)],
+            scratch_shapes=[pltpu.VMEM((4 * PAD, D), bf16), pltpu.VMEM((2 * PAD, D), bf16)],
         ),
         out_shape=[
             jax.ShapeDtypeStruct((8, FETCH, CAP, COLS), bf16),
             jax.ShapeDtypeStruct((FETCH, CAP, PAD), bf16),
             jax.ShapeDtypeStruct((FETCH, CAP, 2 * PAD), bf16),
+            jax.ShapeDtypeStruct((FETCH, CAP, HALF), bf16),
         ],
         compiler_params=pltpu.CompilerParams(vmem_limit_bytes=56 << 20),
         cost_estimate=pl.CostEstimate(
-            flops=2 * 4 * FETCH * CAP * D * PAD, bytes_accessed=65 << 20, transcendentals=0
+            flops=2 * 9 * FETCH * CAP * D * PAD, bytes_accessed=80 << 20, transcendentals=0
         ),
         name="expert_rows",
-    )(*scalars, x_rows, *g_parts, wg, wu, wd)
-
-
-def input_kernel(
-    order_ref, expert_ref, fresh_ref, core_ref, own_ref, oth_ref, wg_ref, wu_ref, wg_oth_ref, wu_oth_ref,
-    d_ref, w_own, w_oth,
-):
-    core = core_ref[0]
-
-    @pl.when(pl.program_id(0) == 0)
-    def _():
-        zeros = jnp.zeros((PAD - UNITS, HALF), bf16)
-        for ref in (w_own, w_oth):
-            ref[UNITS:PAD, :] = zeros
-            ref[PAD + UNITS :, :] = zeros
-
-    @pl.when(fresh_ref[pl.program_id(0)] == 1)
-    def _():
-        for block in range(HALF // COLS):
-            place = slice(block * COLS, (block + 1) * COLS)
-            col = pl.ds(pl.multiple_of((2 * block + core) * COLS, COLS), COLS)
-            w_own[:UNITS, place] = wg_ref[0, :, col]
-            w_own[PAD : PAD + UNITS, place] = wu_ref[0, :, col]
-            w_oth[:UNITS, place] = wg_oth_ref[0, :, col]
-            w_oth[PAD : PAD + UNITS, place] = wu_oth_ref[0, :, col]
-
-    own, oth = own_ref[0], oth_ref[0]
-    for block in range(HALF // COLS):
-        place = slice(block * COLS, (block + 1) * COLS)
-        d_ref[0, :, place] = (mm(own, w_own[:, place], NN) + mm(oth, w_oth[:, place], NN)).astype(
-            bf16
-        )
-
-
-def input_call(scalars, dgu, dgu_oth, wg, wu, wg_oth, wu_oth):
-    weight = pl.BlockSpec((1, UNITS, D), lambda i, o, e, n, c: (e[i], 0, 0))
-    flat = pl.BlockSpec((1, CAP, 2 * PAD), lambda i, o, e, n, c: (o[i], 0, 0))
-    return pl.pallas_call(
-        input_kernel,
-        grid_spec=pltpu.PrefetchScalarGridSpec(
-            num_scalar_prefetch=4,
-            grid=(FETCH,),
-            in_specs=[flat, flat, weight, weight, weight, weight],
-            out_specs=pl.BlockSpec((1, CAP, HALF), lambda i, o, e, n, c: (o[i], 0, 0)),
-            scratch_shapes=[pltpu.VMEM((2 * PAD, HALF), bf16)] * 2,
-        ),
-        out_shape=jax.ShapeDtypeStruct((FETCH, CAP, HALF), bf16),
-        compiler_params=pltpu.CompilerParams(vmem_limit_bytes=56 << 20),
-        cost_estimate=pl.CostEstimate(
-            flops=2 * 2 * FETCH * CAP * D * PAD, bytes_accessed=40 << 20, transcendentals=0
-        ),
-        name="input_rows",
-    )(*scalars, dgu, dgu_oth, wg, wu, wg_oth, wu_oth)
+    )(*scalars, x_rows, *g_parts, *weights)
 
 
 def grads_kernel(chunk_ref, expert_ref, real_ref, last_ref, core_ref, x_ref, *refs):
@@ -187,25 +152,26 @@
 
     @pl.when(real_ref[step] == 1)
     def _():
-        d_gu, act = dgu_ref[0], act_ref[0]
+        d_gu, act = dgu_ref[0].T, act_ref[0].T
         for block in range(D // COLS):
             place = slice(block * COLS, (block + 1) * COLS)
-            acc_gu[:, place] += mm(d_gu, x_ref[block, 0], TN)
-        start = 0
-        for i, size in enumerate(SPLIT):
-            act_i = act[start : start + size]
-            start += size
+            acc_gu[:, place] += mm(d_gu, x_ref[block, 0], NN)
+        for half in range(2):
             for block in range(HALF // COLS):
                 place = slice(block * COLS, (block + 1) * COLS)
-                for half, base in ((0, core * HALF), (1, HALF - core * HALF)):
-                    col = pl.ds(pl.multiple_of(base + block * COLS, COLS), COLS)
-                    acc_d[:, col] += mm(act_i, g_refs[2 * i + half][0, :, place], TN)
+                g = jnp.concatenate(
+                    [g_refs[2 * i + half][0, :, place] for i in range(len(SPLIT))], axis=0
+                )
+                col = half * HALF + block * COLS
+                acc_d[:, col : col + COLS] += mm(act, g, NN)
 
     @pl.when(last_ref[step] == 1)
     def _():
         gg_ref[0] = acc_gu[:UNITS, :].astype(bf16)
         gu_ref[0] = acc_gu[PAD : PAD + UNITS, :].astype(bf16)
-        gd_ref[0] = acc_d[:UNITS, :].astype(bf16)
+        for half, base in enumerate((core * HALF, HALF - core * HALF)):
+            col = pl.ds(pl.multiple_of(base, HALF), HALF)
+            gd_ref[0, :, col] = acc_d[:UNITS, half * HALF : (half + 1) * HALF].astype(bf16)
 
 
 def grads_call(chunk, expert, real, last, core, x_rows, g_parts, act, dgu):
@@ -298,7 +264,7 @@
     core = hidden % 2
     core_arr = core.reshape(1).astype(jnp.int32)
     wg, wu = w_gate.transpose(0, 2, 1), w_up.transpose(0, 2, 1)
-    wg_oth, wu_oth = swap(wg), swap(wu)
+    weights = [wg, wu, w_down, swap(wg), swap(wu), swap(w_down)]
 
     kv = hidden * (queries.shape[1] // HEAD_DIM) // (HEADS // KV_HEADS)
     key_block = lax.dynamic_slice_in_dim(key_rows, kv * HEAD_DIM, HEAD_DIM, 1)
@@ -334,7 +300,7 @@
         return (mm(pick, cot_half, NN) * weight).astype(bf16).reshape(FETCH, size, HALF)
 
     pick, row_weight = one_hot(0, CAP)
-    g_first = exchange(after(grad_rows(0, SPLIT[0]), wg_oth, wu_oth, pick, row_weight))
+    g_first = exchange(after(grad_rows(0, SPLIT[0]), pick, row_weight))
     g_first_oth = swap(g_first)
 
     first_col = hidden * COLS
@@ -345,9 +311,9 @@
     normed = (stream * lax.rsqrt(square + epsilon)[:, None] * gain[None, :]).astype(bf16)
 
     x_part = mm(pick, normed, NN).astype(bf16).reshape(FETCH, CAP, COLS)
-    x_part = exchange(after(x_part, g_first_oth))
+    x_part = exchange(after(x_part, g_first, *weights))
     x_rows = lax.all_gather(x_part, "hidden", axis=0, tiled=False)
-    g_second = exchange(after(grad_rows(SPLIT[0], SPLIT[1]), x_part))
+    g_second = exchange(after(grad_rows(SPLIT[0], SPLIT[1]), x_part, g_first_oth))
     g_parts = [g_first, g_first_oth, g_second, swap(g_second)]
 
     own_col = lax.dynamic_slice_in_dim(fetch_list, group, 1, 1)[:, 0]
@@ -357,8 +323,7 @@
     high = row_weight.astype(bf16)
     low = (row_weight - high.astype(f32)).astype(bf16)
     x_rows, high, low, *tables = lax.optimization_barrier((x_rows, high, low, *tables))
-    out_rows, act, dgu = rows_call(scalars, x_rows, g_parts, wg, wu, w_down)
-    d_half = input_call(scalars, dgu, swap(dgu), wg, wu, wg_oth, wu_oth)
+    out_rows, act, dgu, d_half = rows_call(scalars, x_rows, g_parts, weights)
 
     out_share = lax.psum_scatter(out_rows, "hidden", scatter_dimension=0, tiled=True)[0]
     d_back = exchange(d_half)

time: 413 us -> 380 us (0.920)
  waiting for transfers between devices: 48.8 us -> 29.3 us
  Pallas kernels: 82.5 us -> 67.5 us
    all_to_all x2, waiting for transfers between devices: 28.9 us -> 0.01 us  [exchange(): return lax.all_to_all(value, axis, split_axis=0, concat_axis=0, tiled=True)]
    pallas_call x1 -> x0, Pallas kernels: 19.3 us -> none  [input_call(): pl.pallas_call(input_kernel, grid_spec=pltpu.PrefetchScalarGridSpec(num_s...]
    reduce_scatter x1, waiting for transfers between devices: 8.07 us -> 22.1 us  [shards(): attn = lax.psum_scatter(part, 'hidden', scatter_dimension=0, tiled=True)[0]]
    pallas_call x1, Pallas kernels: 33 us -> 39.1 us  [rows_call(): pl.pallas_call(rows_kernel, grid_spec=pltpu.PrefetchScalarGridSpec(num_sc...]
  transfers between devices with their start and end apart: 11 -> 11, of which waited for: 5 -> 3; matrix products, arithmetic and copies ran while one was open for 9% -> 9% of each run, Pallas kernels for 12% -> 8%
where the time goes in v4:
time: 380 us; the launch traced here: 378 us
  blocking collectives  210 us (55%)
  Pallas kernels  67.5 us (18%)
  waiting for transfers between devices  29.3 us (8%)
  matrix products  29.1 us (8%)
  starting transfers between devices  14.6 us (4%)
  between operations  14.2 us (4%)
  other arithmetic  9.72 us (3%)
    all_to_all x3, blocking collectives, exchange(): return lax.all_to_all(value, axis, split_axis=0, concat_axis=0, tiled=True)  195 us
    pallas_call x1, Pallas kernels, rows_call(): pl.pallas_call(rows_kernel, grid_spec=pltpu.PrefetchScalarGridSpec(num_sc...  39.1 us
    pallas_call x1, Pallas kernels, grads_call(): pl.pallas_call(grads_kernel, grid_spec=pltpu.PrefetchScalarGridSpec(num_s...  28.4 us
    reduce_scatter x1, waiting for transfers between devices, shards(): attn = lax.psum_scatter(part, 'hidden', scatter_dimension=0, tiled=True)[0]  22.1 us
    dot_general x7, matrix products, mm(): return lax.dot_general(a, b, dims, preferred_element_type=f32)  21.3 us
    psum x1, blocking collectives, shards(): square = lax.psum(jnp.sum(stream * stream, axis=1), 'hidden') / D  15.6 us
    all_to_all x2, starting transfers between devices, exchange(): return lax.all_to_all(value, axis, split_axis=0, concat_axis=0, tiled=True)  13.7 us
  transfers between devices with their start and end apart: 11, of which 3 were waited for; matrix products, arithmetic and copies ran while one was open for 9% of the time, Pallas kernels for 8%

profile of v4, /device:TPU:6, one launch (start us, length us, event | category | flops | bytes accessed | tf_op | source)
XLA Modules:
  0.0 377.8 jit_solution(10117569194674001764)
XLA Ops:
  7.3 3.5 fusion.85
  10.8 2.3 convolution_convert_fusion.1
  13.1 2.2 fusion.18
  15.4 0.5 collective-permute-start.1
  16.3 0.4 copy-done.5
  17.1 0.3 bitcast_compare_fusion.2
  17.4 2.6 multiply_convert_fusion.1
  19.9 7.4 %all-to-all-start = ((bf16[16,64,1024]{2,1,0:T(8,128)(2,1)}), bf16[16,64,1024]{2,1,0:T(8,128)(2,1)}, u32[]{:S(2)}, u32[]{:S(2)}) async-start(bf16[16,64,1024]{2,1,0:T(8,128)(2,1)} %bitcast.111), calls=%async_computation.1 | async-start | bytes 4194304 | tf_op jit(solution)/shard_map/all_to_all | solution.py:250
  27.5 2.0 bitcast_compare_fusion
  29.5 0.8 dynamic_slice.21
  30.2 22.1 %reduce-scatter.4.cloned.1.call-done = bf16[1,384,256]{2,1,0:T(8,128)(2,1)} async-done(((bf16[8,384,256]{2,1,0:T(8,128)(2,1)}), bf16[1,384,256]{2,1,0:T(8,128)(2,1)}) %reduce-scatter.4.cloned.1.call-update) | async-done | bytes 196624 | tf_op jit(solution)/shard_map/reduce_scatter | solution.py:275
  52.4 1.2 multiply_reduce_fusion
  53.5 15.6 %psum.7 = f32[384]{0:T(512)S(1)} all-reduce(f32[384]{0:T(512)S(1)} %multiply_reduce_fusion), channel_id=1, replica_groups=mesh['group'=16,'hidden'=8] {'hidden'}, use_global_device_ids=true, to_apply=%region_5.6 | all-reduce | flops 384 | bytes 3072 | tf_op jit(solution)/shard_map/psum | solution.py:310
  69.1 2.8 convolution_convert_fusion
  71.9 28.4 %all_to_all.25 = bf16[16,240,256]{2,1,0:T(8,128)(2,1)} all-to-all(bf16[16,240,256]{2,1,0:T(8,128)(2,1)S(1)} %bitcast.113), channel_id=1, replica_groups=mesh['group'=16,'hidden'=8] {'group'}, dimensions={0} | all-to-all | bytes 3932160 | tf_op jit(solution)/shard_map/all_to_all | solution.py:250
  100.6 1.5 select_reduce_fusion.1
  102.2 1.4 bitcast_compare_fusion.1
  103.6 3.5 multiply_convert_fusion
  107.1 72.3 %all_to_all.26.refs_2_ = bf16[16,176,1024]{2,1,0:T(8,128)(2,1)} all-to-all(bf16[16,176,1024]{2,1,0:T(8,128)(2,1)S(1)} %bitcast.109), channel_id=1, replica_groups=mesh['group'=16,'hidden'=8] {'group'}, dimensions={0} | all-to-all | bytes 11534336 | tf_op jit(solution)/shard_map/all_to_all | solution.py:250
  179.4 0.7 select_reduce_fusion
  181.3 0.6 select_reduce_fusion.8
  181.9 0.7 select_reduce_fusion.4
  182.6 5.4 %all-gather.3.cloned.1.call-done = bf16[128,240,256]{2,1,0:T(8,128)(2,1)} async-done(((bf16[16,240,256]{2,1,0:T(8,128)(2,1)}), bf16[128,240,256]{2,1,0:T(8,128)(2,1)}) %all-gather.3.cloned.1.call-update) | async-done | bytes 15728656 | tf_op jit(solution)/shard_map/all_gather | solution.py:315
  188.0 1.7 collective-permute-done.4.refs_3_
  189.7 39.1 %expert_rows.1 = (bf16[8,16,240,256]{3,2,1,0:T(8,128)(2,1)}, bf16[16,240,128]{2,1,0:T(8,128)(2,1)}, bf16[16,240,256]{2,1,0:T(8,128)(2,1)}, bf16[16,240,1024]{2,1,0:T(8,128)(2,1)}) custom-call(s32[16]{0:T(128)} %get-tuple-element.53.order_ref, s32[16]{0:T(128)} %get-tuple-element.52.expert_ref, s32[16]{0:T(128)} %get-tuple-element.51.fresh_ref, ...), custom_call_target="tpu_custom_call" | custom-call | flops 18119393280 | bytes 83886080 | tf_op jit(solution)/shard_map/expert_rows/pallas_call | solution.py:119
  228.9 94.1 %all_to_all.27 = bf16[16,240,1024]{2,1,0:T(8,128)(2,1)} all-to-all(bf16[16,240,1024]{2,1,0:T(8,128)(2,1)} %get-tuple-element.30), channel_id=1, replica_groups=mesh['group'=16,'hidden'=8] {'group'}, dimensions={0} | all-to-all | bytes 15728640 | tf_op jit(solution)/shard_map/all_to_all | solution.py:250
  323.0 6.3 %all-to-all-start.4 = ((bf16[16,240,256]{2,1,0:T(8,128)(2,1)}), bf16[16,240,256]{2,1,0:T(8,128)(2,1)S(1)}, u32[]{:S(2)}, u32[]{:S(2)}) async-start(bf16[16,240,256]{2,1,0:T(8,128)(2,1)} %bitcast.112), calls=%async_computation.6 | async-start | bytes 3932160 | tf_op jit(solution)/shard_map/all_to_all | solution.py:250
  329.3 6.5 %bitcast_convert_fusion = bf16[384,1024]{1,0:T(8,128)(2,1)S(1)} fusion(bf16[16,240,1024]{2,1,0:T(8,128)(2,1)} %all_to_all.27, s32[16,384]{1,0:T(8,128)S(1)} %copy-done.3), kind=kOutput, calls=%fused_computation.25 | convolution fusion | flops 3021766656 | bytes 8675328 | tf_op jit(solution)/shard_map/dot_general | solution.py:34
  335.8 0.9 copy.76
  337.1 28.4 %weight_grads.1 = (bf16[8,96,2048]{2,1,0:T(8,128)(2,1)}, bf16[8,96,2048]{2,1,0:T(8,128)(2,1)}, bf16[8,96,2048]{2,1,0:T(8,128)(2,1)}) custom-call(s32[24]{0:T(128)} %get-tuple-element.33.chunk_ref, s32[24]{0:T(128)} %get-tuple-element.34.expert_ref, s32[24]{0:T(128)} %get-tuple-element.35.real_ref, s32[24]{0:T(128)} %get-tuple-element.36.last_ref, ...), custom_call_target="tpu_custom_call" | custom-call | flops 6039797760 | bytes 47185920 | tf_op jit(solution)/shard_map/weight_grads/pallas_call | solution.py:184
  365.5 2.5 fusion.25
  368.0 3.3 fusion.40
  (79 shorter events, 3.0 us)
Async XLA Ops:
  7.2 10.2 %copy-start = (bf16[384,2048]{1,0:T(8,128)(2,1)S(1)}, bf16[384,2048]{1,0:T(8,128)(2,1)}, u32[]{:S(2)}) copy-start(bf16[384,2048]{1,0:T(8,128)(2,1)} %param.25) | copy-start | bytes 4718596
  7.2 45.2 %reduce-scatter.4.cloned.1.call-start = ((), (), s32[]{:S(2)}) async-start(), calls=%async_computation.8 | async-start | bytes 1769472 | tf_op jit(solution)/shard_map/reduce_scatter | solution.py:275
  10.8 2.4 copy-start.11
  13.1 3.0 copy-start.8
  13.1 3.0 copy-start.9
  15.3 56.6 %collective-permute-start = (bf16[8,96,2048]{2,1,0:T(8,128)(2,1)}, bf16[8,96,2048]{2,1,0:T(8,128)(2,1)}, u32[]{:S(2)}, u32[]{:S(2)}) collective-permute-start(bf16[8,96,2048]{2,1,0:T(8,128)(2,1)} %bitcast.118), channel_id=1, source_target_pairs={{0,1},{1,0},{2,3},{3,2},{4,5},{5,4},{6,7},{7,6},{8,9},{9,8},{10,11... | collective-permute-start | bytes 9437192 | tf_op jit(solution)/shard_map/ppermute | solution.py:254
  15.4 56.5 %collective-permute-start.1 = (bf16[8,96,2048]{2,1,0:T(8,128)(2,1)}, bf16[8,96,2048]{2,1,0:T(8,128)(2,1)}, u32[]{:S(2)}, u32[]{:S(2)}) collective-permute-start(bf16[8,96,2048]{2,1,0:T(8,128)(2,1)} %bitcast.120), channel_id=1, source_target_pairs={{0,1},{1,0},{2,3},{3,2},{4,5},{5,4},{6,7},{7,6},{8,9},{9,8},{10,11... | collective-permute-start | bytes 9437192 | tf_op jit(solution)/shard_map/ppermute | solution.py:254
  15.9 56.0 %collective-permute-start.2 = (bf16[8,96,2048]{2,1,0:T(8,128)(2,1)}, bf16[8,96,2048]{2,1,0:T(8,128)(2,1)}, u32[]{:S(2)}, u32[]{:S(2)}) collective-permute-start(bf16[8,96,2048]{2,1,0:T(8,128)(2,1)} %refs_6_.1), channel_id=1, source_target_pairs={{0,1},{1,0},{2,3},{3,2},{4,5},{5,4},{6,7},{7,6},{8,9},{9,8},{10,11... | collective-permute-start | bytes 9437192 | tf_op jit(solution)/shard_map/ppermute | solution.py:254
  16.1 0.6 copy-start.5
  16.3 11.2 %copy-start.2 = (s32[16,384]{1,0:T(8,128)}, s32[16,384]{1,0:T(8,128)S(1)}, u32[]{:S(2)}) copy-start(s32[16,384]{1,0:T(8,128)S(1)} %fusion.44) | copy-start | bytes 73732
  19.9 51.9 %all-to-all-start = ((bf16[16,64,1024]{2,1,0:T(8,128)(2,1)}), bf16[16,64,1024]{2,1,0:T(8,128)(2,1)}, u32[]{:S(2)}, u32[]{:S(2)}) async-start(bf16[16,64,1024]{2,1,0:T(8,128)(2,1)} %bitcast.111), calls=%async_computation.1 | async-start | bytes 4194304 | tf_op jit(solution)/shard_map/all_to_all | solution.py:250
  27.4 160.7 %all-gather.3.cloned.1.call-start = ((), (), s32[]{:S(2)}) async-start(), calls=%async_computation.11 | async-start | bytes 17694720 | tf_op jit(solution)/shard_map/all_gather | solution.py:315
  100.4 222.7 %reduce-scatter.6.cloned.1.call-start = ((), (), s32[]{:S(2)}) async-start(), calls=%async_computation.9 | async-start | bytes 17694720 | tf_op jit(solution)/shard_map/reduce_scatter | solution.py:328
  100.4 6.7 %collective-permute-start.3 = (bf16[16,64,1024]{2,1,0:T(8,128)(2,1)}, bf16[16,64,1024]{2,1,0:T(8,128)(2,1)}, u32[]{:S(2)}, u32[]{:S(2)}) collective-permute-start(bf16[16,64,1024]{2,1,0:T(8,128)(2,1)} %all-to-all-done.refs_0_), channel_id=1, source_target_pairs={{0,1},{1,0},{2,3},{3,2},{4,5},{5,4},{6,7},{7,6},{8,9},{9,8},{10,11... | collective-permute-start | bytes 6291464 | tf_op jit(solution)/shard_map/ppermute | solution.py:254
  107.1 72.3 %copy-start.3 = (s32[16,384]{1,0:T(8,128)S(1)}, s32[16,384]{1,0:T(8,128)}, u32[]{:S(2)}) copy-start(s32[16,384]{1,0:T(8,128)} %copy-done.2) | copy-start | bytes 73732
  107.1 72.3 %copy-start.6 = (f32[384,16]{0,1:T(8,128)S(1)}, f32[384,16]{0,1:T(8,128)}, u32[]{:S(2)}) copy-start(f32[384,16]{0,1:T(8,128)} %copy-done.5) | copy-start | bytes 73732
  107.1 73.1 %copy-start.10 = (s32[16,16]{1,0:T(8,128)S(1)}, s32[16,16]{1,0:T(8,128)}, u32[]{:S(2)}) copy-start(s32[16,16]{1,0:T(8,128)} %param.24) | copy-start | bytes 3076
  179.4 10.3 %collective-permute-start.4 = (bf16[16,176,1024]{2,1,0:T(8,128)(2,1)}, bf16[16,176,1024]{2,1,0:T(8,128)(2,1)}, u32[]{:S(2)}, u32[]{:S(2)}) collective-permute-start(bf16[16,176,1024]{2,1,0:T(8,128)(2,1)} %all_to_all.26.refs_2_), channel_id=1, source_target_pairs={{0,1},{1,0},{2,3},{3,2},{4,5},{5,4},{6,7},{7,6},{8,9},{9,8},{10,11... | collective-permute-start | bytes 17301512 | tf_op jit(solution)/shard_map/ppermute | solution.py:254
  323.0 42.4 %all-to-all-start.4 = ((bf16[16,240,256]{2,1,0:T(8,128)(2,1)}), bf16[16,240,256]{2,1,0:T(8,128)(2,1)S(1)}, u32[]{:S(2)}, u32[]{:S(2)}) async-start(bf16[16,240,256]{2,1,0:T(8,128)(2,1)} %bitcast.112), calls=%async_computation.6 | async-start | bytes 3932160 | tf_op jit(solution)/shard_map/all_to_all | solution.py:250
  329.3 42.0 %reduce-scatter.8.cloned.1.call-start = ((), (), s32[]{:S(2)}) async-start(), calls=%async_computation.10 | async-start | bytes 983040 | tf_op jit(solution)/shard_map/reduce_scatter | solution.py:337
  365.5 2.6 copy-start.4
  365.5 2.5 copy-start.7
  365.5 5.8 %copy-start.1 = (bf16[384,2048]{1,0:T(8,128)(2,1)S(1)}, bf16[384,2048]{1,0:T(8,128)(2,1)}, u32[]{:S(2)}) copy-start(bf16[384,2048]{1,0:T(8,128)(2,1)} %param.25) | copy-start | bytes 4718596
Sparse Core Ops, SparseCore 0:
  15.4 36.8 reduce-scatter.3
  100.5 87.4 all-gather.2
  229.0 87.5 reduce-scatter.5
  336.9 24.6 reduce-scatter.7

commit v5 on v4

--- a/solution.py
+++ b/solution.py
@@ -19,7 +19,7 @@
 COLS = 256
 HALF = 1024
 STEPS = FETCH + EXP_GROUP
-SPLIT = (64, 176)
+SPLIT = (80, 160)
 
 epsilon = 1e-06
 bf16 = jnp.bfloat16
@@ -144,28 +144,38 @@
     act_ref, dgu_ref, gg_ref, gu_ref, gd_ref, acc_gu, acc_d = refs[2 * len(SPLIT) :]
     step = pl.program_id(0)
     core = core_ref[0]
-
-    @pl.when(real_ref[step] == 0)
-    def _():
-        acc_gu[...] = jnp.zeros_like(acc_gu)
-        acc_d[...] = jnp.zeros_like(acc_d)
-
-    @pl.when(real_ref[step] == 1)
-    def _():
+    kind, last = real_ref[step], last_ref[step]
+
+    def chunk(first):
         d_gu, act = dgu_ref[0].T, act_ref[0].T
         for block in range(D // COLS):
             place = slice(block * COLS, (block + 1) * COLS)
-            acc_gu[:, place] += mm(d_gu, x_ref[block, 0], NN)
+            part = mm(d_gu, x_ref[block, 0], NN)
+            acc_gu[:, place] = part if first else acc_gu[:, place] + part
         for half in range(2):
             for block in range(HALF // COLS):
                 place = slice(block * COLS, (block + 1) * COLS)
                 g = jnp.concatenate(
                     [g_refs[2 * i + half][0, :, place] for i in range(len(SPLIT))], axis=0
                 )
-                col = half * HALF + block * COLS
-                acc_d[:, col : col + COLS] += mm(act, g, NN)
-
-    @pl.when(last_ref[step] == 1)
+                into = slice(half * HALF + block * COLS, half * HALF + (block + 1) * COLS)
+                part = mm(act, g, NN)
+                acc_d[:, into] = part if first else acc_d[:, into] + part
+
+    @pl.when(kind == 1)
+    def _():
+        chunk(True)
+
+    @pl.when(kind == 2)
+    def _():
+        chunk(False)
+
+    @pl.when((last == 1) & (kind == 0))
+    def _():
+        for ref in (gg_ref, gu_ref, gd_ref):
+            ref[...] = jnp.zeros_like(ref)
+
+    @pl.when((last == 1) & (kind != 0))
     def _():
         gg_ref[0] = acc_gu[:UNITS, :].astype(bf16)
         gu_ref[0] = acc_gu[PAD : PAD + UNITS, :].astype(bf16)
@@ -220,7 +230,9 @@
         return jnp.sum(jnp.where(place, values[:, None], 0), axis=0)
 
     count = jnp.sum((owner[None, :] == owner[:, None]) & (key[None, :] > key[:, None]), axis=1)
-    real = (jnp.arange(STEPS) >= EXP_GROUP).astype(jnp.int32)
+    earlier = (experts[None, :] == experts[:, None]) & (ids[None, :] < ids[:, None])
+    again = jnp.any(earlier, axis=1).astype(jnp.int32)
+    real = jnp.concatenate([jnp.zeros((EXP_GROUP,), jnp.int32), 1 + again])
     last = (count == 0).astype(jnp.int32)
     return ordered(chunk), ordered(owner), ordered(real), ordered(last)
 
@@ -293,6 +305,16 @@
         weight = jnp.sum(jnp.where(hit, weight_t[:, None, :], 0.0), axis=2)
         return hit.astype(bf16).reshape(FETCH * size, tokens), weight.reshape(-1, 1)
 
+    row_slot = lax.broadcasted_iota(jnp.int32, (FETCH, FETCH * CAP), 1) // CAP
+    spread = (row_slot == lax.broadcasted_iota(jnp.int32, (FETCH, FETCH * CAP), 0)).astype(bf16)
+    row_cap = lax.broadcasted_iota(jnp.int32, (tokens, FETCH * CAP), 1) % CAP
+    hit_rows = mm(position.astype(bf16), spread, NN) == row_cap.astype(f32)
+    high = slot_weight.astype(bf16)
+    low = (slot_weight - high.astype(f32)).astype(bf16)
+    into = hit_rows.astype(bf16)
+    into_high = jnp.where(hit_rows, mm(high, spread, NN), 0.0).astype(bf16)
+    into_low = jnp.where(hit_rows, mm(low, spread, NN), 0.0).astype(bf16)
+
     cot_half = lax.dynamic_slice_in_dim(cotangent, core * HALF, HALF, 1)
 
     def grad_rows(start, size):
@@ -303,6 +325,14 @@
     g_first = exchange(after(grad_rows(0, SPLIT[0]), pick, row_weight))
     g_first_oth = swap(g_first)
 
+    second_rows = grad_rows(SPLIT[0], SPLIT[1])
+    own_col = lax.dynamic_slice_in_dim(fetch_list, group, 1, 1)[:, 0]
+    experts = own_col - group * EXP_GROUP
+    scalars = (*rows_order(experts), core_arr)
+    tables = grad_order(experts)
+    attn, second_rows, scalars, tables, into, into_high, into_low = lax.optimization_barrier(
+        (attn, second_rows, scalars, tables, into, into_high, into_low)
+    )
     first_col = hidden * COLS
     res_share = lax.dynamic_slice_in_dim(residual, first_col, COLS, 1)
     gain = lax.dynamic_slice_in_dim(norm_gain, first_col, COLS, 0)
@@ -313,16 +343,9 @@
     x_part = mm(pick, normed, NN).astype(bf16).reshape(FETCH, CAP, COLS)
     x_part = exchange(after(x_part, g_first, *weights))
     x_rows = lax.all_gather(x_part, "hidden", axis=0, tiled=False)
-    g_second = exchange(after(grad_rows(SPLIT[0], SPLIT[1]), x_part, g_first_oth))
+    g_second = exchange(after(second_rows, x_part, g_first_oth))
     g_parts = [g_first, g_first_oth, g_second, swap(g_second)]
 
-    own_col = lax.dynamic_slice_in_dim(fetch_list, group, 1, 1)[:, 0]
-    experts = own_col - group * EXP_GROUP
-    scalars = (*rows_order(experts), core_arr)
-    tables = grad_order(experts)
-    high = row_weight.astype(bf16)
-    low = (row_weight - high.astype(f32)).astype(bf16)
-    x_rows, high, low, *tables = lax.optimization_barrier((x_rows, high, low, *tables))
     out_rows, act, dgu, d_half = rows_call(scalars, x_rows, g_parts, weights)
 
     out_share = lax.psum_scatter(out_rows, "hidden", scatter_dimension=0, tiled=True)[0]
@@ -332,14 +355,14 @@
     )
     out_back = exchange(after(out_share, d_back))
 
-    d_tok = mm(pick, d_back.reshape(-1, HALF), TN).astype(bf16)
+    d_tok = mm(into, d_back.reshape(-1, HALF), NN).astype(bf16)
     d_tok = d_tok.reshape(tokens, 4, COLS).transpose(1, 0, 2)
     grad_normed = lax.psum_scatter(
         d_tok, "hidden", scatter_dimension=0, tiled=True, axis_index_groups=Z_GROUPS
     )[0]
 
     out_back = out_back.reshape(-1, COLS)
-    moe = mm(pick * high, out_back, TN) + mm(pick * low, out_back, TN)
+    moe = mm(into_high, out_back, NN) + mm(into_low, out_back, NN)
     layer_out = (stream + moe).astype(bf16)
     return (
         layer_out,

time: 380 us -> 378 us (level)
  matrix products: 29.1 us -> 39.4 us
  waiting for transfers between devices: 29.3 us -> 20 us
    reduce_scatter x1, waiting for transfers between devices: 22.1 us -> 5.19 us  [shards(): attn = lax.psum_scatter(part, 'hidden', scatter_dimension=0, tiled=True)[0]]
    ppermute x5, waiting for transfers between devices: 1.72 us -> 14 us  [swap(): return lax.ppermute(value, 'hidden', PAIRS)]
    dot_general x7 -> x10, matrix products: 21.3 us -> 31.5 us  [mm(): return lax.dot_general(a, b, dims, preferred_element_type=f32)]
    all_gather x1, waiting for transfers between devices: 5.44 us -> 0.72 us  [shards(): x_rows = lax.all_gather(x_part, 'hidden', axis=0, tiled=False)]
  transfers between devices with their start and end apart: 11 -> 11, of which waited for: 3 -> 4; matrix products, arithmetic and copies ran while one was open for 9% -> 11% of each run, Pallas kernels for 8% -> 7%
where the time goes in v5:
time: 378 us; the launch traced here: 374 us
  blocking collectives  208 us (55%)
  Pallas kernels  65.3 us (17%)
  matrix products  39.4 us (10%)
  waiting for transfers between devices  20 us (5%)
  starting transfers between devices  15.1 us (4%)
  between operations  14.1 us (4%)
  other arithmetic  7.63 us (2%)
  local copies, waits for them, and re-layouts  4.55 us (1%)
    all_to_all x3, blocking collectives, exchange(): return lax.all_to_all(value, axis, split_axis=0, concat_axis=0, tiled=True)  193 us
    pallas_call x1, Pallas kernels, rows_call(): pl.pallas_call(rows_kernel, grid_spec=pltpu.PrefetchScalarGridSpec(num_sc...  39 us
    dot_general x10, matrix products, mm(): return lax.dot_general(a, b, dims, preferred_element_type=f32)  31.5 us
    pallas_call x1, Pallas kernels, grads_call(): pl.pallas_call(grads_kernel, grid_spec=pltpu.PrefetchScalarGridSpec(num_s...  26.2 us
    psum x1, blocking collectives, shards(): square = lax.psum(jnp.sum(stream * stream, axis=1), 'hidden') / D  15.7 us
    all_to_all x2, starting transfers between devices, exchange(): return lax.all_to_all(value, axis, split_axis=0, concat_axis=0, tiled=True)  14.2 us
    ppermute x5, waiting for transfers between devices, swap(): return lax.ppermute(value, 'hidden', PAIRS)  14 us
  transfers between devices with their start and end apart: 11, of which 4 were waited for; matrix products, arithmetic and copies ran while one was open for 11% of the time, Pallas kernels for 7%

profile of v5, /device:TPU:6, one launch (start us, length us, event | category | flops | bytes accessed | tf_op | source)
XLA Modules:
  0.0 374.4 jit_solution(16588980636968013424)
XLA Ops:
  7.3 3.5 fusion.75
  10.8 2.3 convolution_convert_fusion.2
  13.1 2.2 fusion.10
  16.4 3.0 multiply_convert_fusion.1
  19.5 7.6 %all-to-all-start = ((bf16[16,80,1024]{2,1,0:T(8,128)(2,1)}), bf16[16,80,1024]{2,1,0:T(8,128)(2,1)}, u32[]{:S(2)}, u32[]{:S(2)}) async-start(bf16[16,80,1024]{2,1,0:T(8,128)(2,1)} %bitcast.97), calls=%async_computation.1 | async-start | bytes 5242880 | tf_op jit(solution)/shard_map/all_to_all | solution.py:262
  28.9 0.6 select_reduce_fusion.7
  29.5 0.7 select_reduce_fusion
  31.2 2.0 bitcast_compare_fusion
  33.1 0.8 dynamic_slice.23
  33.9 0.7 select_reduce_fusion.3
  34.6 3.0 fusion.80
  37.6 2.6 fusion.1
  40.2 2.5 fusion.2
  42.8 4.6 %multiply_convert_fusion = bf16[2560,1024]{1,0:T(8,128)(2,1)} fusion(pred[2560,384]{1,0:T(32,128)(4,1)S(1)} %bitcast_compare_fusion.1, f32[2560]{0:T(1024)S(1)} %mul.75, bf16[384,2048]{1,0:T(8,128)(2,1)S(1)} %copy-done, s32[]{:T(128)S(6)} %select_n.111), kind=kOutput, calls=%fused_computation.1 | convolution fusion | flops 2018508800 | bytes 7024644 | tf_op jit(solution)/shard_map/dot_general | solution.py:34
  47.4 5.2 %reduce-scatter.4.cloned.1.call-done = bf16[1,384,256]{2,1,0:T(8,128)(2,1)} async-done(((bf16[8,384,256]{2,1,0:T(8,128)(2,1)}), bf16[1,384,256]{2,1,0:T(8,128)(2,1)}) %reduce-scatter.4.cloned.1.call-update) | async-done | bytes 196624 | tf_op jit(solution)/shard_map/reduce_scatter | solution.py:287
  52.6 1.2 multiply_reduce_fusion
  53.7 15.7 %psum.7 = f32[384]{0:T(512)S(1)} all-reduce(f32[384]{0:T(512)S(1)} %multiply_reduce_fusion), channel_id=1, replica_groups=mesh['group'=16,'hidden'=8] {'hidden'}, use_global_device_ids=true, to_apply=%region_19.20 | all-reduce | flops 384 | bytes 3072 | tf_op jit(solution)/shard_map/psum | solution.py:340
  69.5 2.8 convolution_convert_fusion
  72.3 30.9 %all_to_all.25 = bf16[16,240,256]{2,1,0:T(8,128)(2,1)} all-to-all(bf16[16,240,256]{2,1,0:T(8,128)(2,1)S(1)} %bitcast.101), channel_id=1, replica_groups=mesh['group'=16,'hidden'=8] {'group'}, dimensions={0} | all-to-all | bytes 3932160 | tf_op jit(solution)/shard_map/all_to_all | solution.py:262
  103.4 5.2 %collective-permute-done.3.refs_1_ = bf16[16,80,1024]{2,1,0:T(8,128)(2,1)} collective-permute-done((bf16[16,80,1024]{2,1,0:T(8,128)(2,1)}, bf16[16,80,1024]{2,1,0:T(8,128)(2,1)}, u32[]{:S(2)}, u32[]{:S(2)}) %collective-permute-start.3) | collective-permute-done | bytes 2621472 | tf_op jit(solution)/shard_map/ppermute | solution.py:266
  108.6 66.4 %all_to_all.26.refs_2_ = bf16[16,160,1024]{2,1,0:T(8,128)(2,1)S(1)} all-to-all(bf16[16,160,1024]{2,1,0:T(8,128)(2,1)} %bitcast.95), channel_id=1, replica_groups=mesh['group'=16,'hidden'=8] {'group'}, dimensions={0} | all-to-all | bytes 10485760 | tf_op jit(solution)/shard_map/all_to_all | solution.py:262
  175.1 2.2 copy-done.2
  177.3 8.8 %collective-permute-done.4.refs_3_ = bf16[16,160,1024]{2,1,0:T(8,128)(2,1)} collective-permute-done((bf16[16,160,1024]{2,1,0:T(8,128)(2,1)S(1)}, bf16[16,160,1024]{2,1,0:T(8,128)(2,1)}, u32[]{:S(2)}, u32[]{:S(2)}) %collective-permute-start.4) | collective-permute-done | bytes 5242912 | tf_op jit(solution)/shard_map/ppermute | solution.py:266
  186.1 0.7 all-gather.3.cloned.1.call-done
  186.8 39.0 %expert_rows.1 = (bf16[8,16,240,256]{3,2,1,0:T(8,128)(2,1)}, bf16[16,240,128]{2,1,0:T(8,128)(2,1)}, bf16[16,240,256]{2,1,0:T(8,128)(2,1)}, bf16[16,240,1024]{2,1,0:T(8,128)(2,1)}) custom-call(s32[16]{0:T(128)} %get-tuple-element.33.order_ref, s32[16]{0:T(128)} %get-tuple-element.34.expert_ref, s32[16]{0:T(128)} %get-tuple-element.35.fresh_ref, ...), custom_call_target="tpu_custom_call" | custom-call | flops 18119393280 | bytes 83886080 | tf_op jit(solution)/shard_map/expert_rows/pallas_call | solution.py:119
  225.9 95.2 %all_to_all.27 = bf16[16,240,1024]{2,1,0:T(8,128)(2,1)} all-to-all(bf16[16,240,1024]{2,1,0:T(8,128)(2,1)} %get-tuple-element.41), channel_id=1, replica_groups=mesh['group'=16,'hidden'=8] {'group'}, dimensions={0} | all-to-all | bytes 15728640 | tf_op jit(solution)/shard_map/all_to_all | solution.py:262
  321.1 6.7 %all-to-all-start.4 = ((bf16[16,240,256]{2,1,0:T(8,128)(2,1)}), bf16[16,240,256]{2,1,0:T(8,128)(2,1)S(1)}, u32[]{:S(2)}, u32[]{:S(2)}) async-start(bf16[16,240,256]{2,1,0:T(8,128)(2,1)} %bitcast.98), calls=%async_computation.6 | async-start | bytes 3932160 | tf_op jit(solution)/shard_map/all_to_all | solution.py:262
  327.8 7.3 %convolution_convert_fusion.1 = bf16[384,1024]{1,0:T(8,128)(2,1)S(1)} fusion(bf16[384,3840]{1,0:T(8,128)(2,1)} %get-tuple-element.44, bf16[3840,1024]{1,0:T(8,128)(2,1)} %bitcast.94), kind=kOutput, calls=%fused_computation.24 | convolution fusion | flops 3020292096 | bytes 11599872 | tf_op jit(solution)/shard_map/dot_general | solution.py:34
  335.2 0.9 copy.76
  336.1 26.2 %weight_grads.1 = (bf16[8,96,2048]{2,1,0:T(8,128)(2,1)}, bf16[8,96,2048]{2,1,0:T(8,128)(2,1)}, bf16[8,96,2048]{2,1,0:T(8,128)(2,1)}) custom-call(s32[24]{0:T(128)} %get-tuple-element.45.chunk_ref, s32[24]{0:T(128)} %get-tuple-element.46.expert_ref, s32[24]{0:T(128)} %get-tuple-element.47.real_ref, s32[24]{0:T(128)} %get-tuple-element.48.last_ref, ...), custom_call_target="tpu_custom_call" | custom-call | flops 6039797760 | bytes 47185920 | tf_op jit(solution)/shard_map/weight_grads/pallas_call | solution.py:194
  362.4 2.9 fusion.81
  365.4 2.6 fusion.17
  (73 shorter events, 4.2 us)
Async XLA Ops:
  7.2 9.3 %copy-start = (bf16[384,2048]{1,0:T(8,128)(2,1)S(1)}, bf16[384,2048]{1,0:T(8,128)(2,1)}, u32[]{:S(2)}) copy-start(bf16[384,2048]{1,0:T(8,128)(2,1)} %param.25) | copy-start | bytes 4718596
  7.2 45.4 %reduce-scatter.4.cloned.1.call-start = ((), (), s32[]{:S(2)}) async-start(), calls=%async_computation.8 | async-start | bytes 1769472 | tf_op jit(solution)/shard_map/reduce_scatter | solution.py:287
  10.8 2.4 copy-start.8
  13.1 2.3 copy-start.5
  13.1 2.5 copy-start.6
  19.5 8.3 %copy-start.7 = (s32[16,16]{1,0:T(8,128)S(1)}, s32[16,16]{1,0:T(8,128)}, u32[]{:S(2)}) copy-start(s32[16,16]{1,0:T(8,128)} %param.24) | copy-start | bytes 3076
  19.5 52.8 %all-to-all-start = ((bf16[16,80,1024]{2,1,0:T(8,128)(2,1)}), bf16[16,80,1024]{2,1,0:T(8,128)(2,1)}, u32[]{:S(2)}, u32[]{:S(2)}) async-start(bf16[16,80,1024]{2,1,0:T(8,128)(2,1)} %bitcast.97), calls=%async_computation.1 | async-start | bytes 5242880 | tf_op jit(solution)/shard_map/all_to_all | solution.py:262
  27.0 159.8 %all-gather.3.cloned.1.call-start = ((), (), s32[]{:S(2)}) async-start(), calls=%async_computation.11 | async-start | bytes 17694720 | tf_op jit(solution)/shard_map/all_gather | solution.py:345
  27.1 45.2 %collective-permute-start = (bf16[8,96,2048]{2,1,0:T(8,128)(2,1)}, bf16[8,96,2048]{2,1,0:T(8,128)(2,1)}, u32[]{:S(2)}, u32[]{:S(2)}) collective-permute-start(bf16[8,96,2048]{2,1,0:T(8,128)(2,1)} %bitcast.113), channel_id=1, source_target_pairs={{0,1},{1,0},{2,3},{3,2},{4,5},{5,4},{6,7},{7,6},{8,9},{9,8},{10,11... | collective-permute-start | bytes 9437192 | tf_op jit(solution)/shard_map/ppermute | solution.py:266
  27.2 45.1 %collective-permute-start.1 = (bf16[8,96,2048]{2,1,0:T(8,128)(2,1)}, bf16[8,96,2048]{2,1,0:T(8,128)(2,1)}, u32[]{:S(2)}, u32[]{:S(2)}) collective-permute-start(bf16[8,96,2048]{2,1,0:T(8,128)(2,1)} %bitcast.115), channel_id=1, source_target_pairs={{0,1},{1,0},{2,3},{3,2},{4,5},{5,4},{6,7},{7,6},{8,9},{9,8},{10,11... | collective-permute-start | bytes 9437192 | tf_op jit(solution)/shard_map/ppermute | solution.py:266
  27.7 44.6 %collective-permute-start.2 = (bf16[8,96,2048]{2,1,0:T(8,128)(2,1)}, bf16[8,96,2048]{2,1,0:T(8,128)(2,1)}, u32[]{:S(2)}, u32[]{:S(2)}) collective-permute-start(bf16[8,96,2048]{2,1,0:T(8,128)(2,1)} %refs_6_.1), channel_id=1, source_target_pairs={{0,1},{1,0},{2,3},{3,2},{4,5},{5,4},{6,7},{7,6},{8,9},{9,8},{10,11... | collective-permute-start | bytes 9437192 | tf_op jit(solution)/shard_map/ppermute | solution.py:266
  103.2 217.9 %reduce-scatter.6.cloned.1.call-start = ((), (), s32[]{:S(2)}) async-start(), calls=%async_computation.9 | async-start | bytes 17694720 | tf_op jit(solution)/shard_map/reduce_scatter | solution.py:351
  103.3 5.3 %collective-permute-start.3 = (bf16[16,80,1024]{2,1,0:T(8,128)(2,1)}, bf16[16,80,1024]{2,1,0:T(8,128)(2,1)}, u32[]{:S(2)}, u32[]{:S(2)}) collective-permute-start(bf16[16,80,1024]{2,1,0:T(8,128)(2,1)} %all-to-all-done.refs_0_), channel_id=1, source_target_pairs={{0,1},{1,0},{2,3},{3,2},{4,5},{5,4},{6,7},{7,6},{8,9},{9,8},{10,11... | collective-permute-start | bytes 7864328 | tf_op jit(solution)/shard_map/ppermute | solution.py:266
  175.1 2.2 copy-start.2
  177.3 8.8 %collective-permute-start.4 = (bf16[16,160,1024]{2,1,0:T(8,128)(2,1)S(1)}, bf16[16,160,1024]{2,1,0:T(8,128)(2,1)}, u32[]{:S(2)}, u32[]{:S(2)}) collective-permute-start(bf16[16,160,1024]{2,1,0:T(8,128)(2,1)S(1)} %all_to_all.26.refs_2_), channel_id=1, source_target_pairs={{0,1},{1,0},{2,3},{3,2},{4,5},{5,4},{6,7},{7,6},{8,9},{9,8},{10,11... | collective-permute-start | bytes 15728648 | tf_op jit(solution)/shard_map/ppermute | solution.py:266
  321.1 41.3 %all-to-all-start.4 = ((bf16[16,240,256]{2,1,0:T(8,128)(2,1)}), bf16[16,240,256]{2,1,0:T(8,128)(2,1)S(1)}, u32[]{:S(2)}, u32[]{:S(2)}) async-start(bf16[16,240,256]{2,1,0:T(8,128)(2,1)} %bitcast.98), calls=%async_computation.6 | async-start | bytes 3932160 | tf_op jit(solution)/shard_map/all_to_all | solution.py:262
  327.8 40.1 %reduce-scatter.8.cloned.1.call-start = ((), (), s32[]{:S(2)}) async-start(), calls=%async_computation.10 | async-start | bytes 983040 | tf_op jit(solution)/shard_map/reduce_scatter | solution.py:360
  362.4 3.0 copy-start.3
  362.4 3.0 copy-start.4
  362.4 5.5 %copy-start.1 = (bf16[384,2048]{1,0:T(8,128)(2,1)S(1)}, bf16[384,2048]{1,0:T(8,128)(2,1)}, u32[]{:S(2)}) copy-start(bf16[384,2048]{1,0:T(8,128)(2,1)} %param.25) | copy-start | bytes 4718596
Sparse Core Ops, SparseCore 0:
  15.4 37.0 reduce-scatter.3
  103.4 83.4 all-gather.2
  226.0 84.9 reduce-scatter.5
  336.3 21.5 reduce-scatter.7

commit v6 on v5

--- a/solution.py
+++ b/solution.py
@@ -323,28 +323,33 @@
 
     pick, row_weight = one_hot(0, CAP)
     g_first = exchange(after(grad_rows(0, SPLIT[0]), pick, row_weight))
-    g_first_oth = swap(g_first)
 
     second_rows = grad_rows(SPLIT[0], SPLIT[1])
     own_col = lax.dynamic_slice_in_dim(fetch_list, group, 1, 1)[:, 0]
     experts = own_col - group * EXP_GROUP
     scalars = (*rows_order(experts), core_arr)
     tables = grad_order(experts)
-    attn, second_rows, scalars, tables, into, into_high, into_low = lax.optimization_barrier(
-        (attn, second_rows, scalars, tables, into, into_high, into_low)
+    attn, second_rows, scalars, tables, into, into_high, into_low, weights = (
+        lax.optimization_barrier(
+            (attn, second_rows, scalars, tables, into, into_high, into_low, weights)
+        )
     )
     first_col = hidden * COLS
     res_share = lax.dynamic_slice_in_dim(residual, first_col, COLS, 1)
     gain = lax.dynamic_slice_in_dim(norm_gain, first_col, COLS, 0)
     stream = res_share.astype(f32) + attn.astype(f32)
-    square = lax.psum(jnp.sum(stream * stream, axis=1), "hidden") / D
+    own_square = jnp.sum(stream * stream, axis=1)
+    square = own_square
+    for turn in range(1, 8):
+        square = square + lax.ppermute(own_square, "hidden", [(i, i ^ turn) for i in range(8)])
+    square = square / D
     normed = (stream * lax.rsqrt(square + epsilon)[:, None] * gain[None, :]).astype(bf16)
 
     x_part = mm(pick, normed, NN).astype(bf16).reshape(FETCH, CAP, COLS)
-    x_part = exchange(after(x_part, g_first, *weights))
+    x_part = exchange(after(x_part, g_first))
     x_rows = lax.all_gather(x_part, "hidden", axis=0, tiled=False)
-    g_second = exchange(after(second_rows, x_part, g_first_oth))
-    g_parts = [g_first, g_first_oth, g_second, swap(g_second)]
+    g_second = exchange(after(second_rows, x_part))
+    g_parts = [g_first, swap(after(g_first, g_second)), g_second, swap(g_second)]
 
     out_rows, act, dgu, d_half = rows_call(scalars, x_rows, g_parts, weights)
 

time: 378 us -> 371 us (0.981)
  blocking collectives: 208 us -> 194 us
  starting transfers between devices: 15.1 us -> 23.8 us
    psum x1 -> x0, blocking collectives: 15.7 us -> none  [shards(): square = lax.psum(jnp.sum(stream * stream, axis=1), 'hidden') / D]
    ppermute x0 -> x7, starting transfers between devices: none -> 8.65 us  [shards(): lax.ppermute(own_square, 'hidden', [(i, i ^ turn) for i in range(8)])]
  transfers between devices with their start and end apart: 11 -> 18, of which waited for: 4 -> 4; matrix products, arithmetic and copies ran while one was open for 11% -> 11% of each run, Pallas kernels for 7% -> 7%
where the time goes in v6:
time: 371 us; the launch traced here: 370 us
  blocking collectives  194 us (52%)
  Pallas kernels  65.7 us (18%)
  matrix products  38.9 us (10%)
  starting transfers between devices  23.8 us (6%)
  waiting for transfers between devices  22.1 us (6%)
  between operations  14.1 us (4%)
  other arithmetic  6.58 us (2%)
  local copies, waits for them, and re-layouts  4.54 us (1%)
    all_to_all x3, blocking collectives, exchange(): return lax.all_to_all(value, axis, split_axis=0, concat_axis=0, tiled=True)  194 us
    pallas_call x1, Pallas kernels, rows_call(): pl.pallas_call(rows_kernel, grid_spec=pltpu.PrefetchScalarGridSpec(num_sc...  38.5 us
    dot_general x10, matrix products, mm(): return lax.dot_general(a, b, dims, preferred_element_type=f32)  31 us
    pallas_call x1, Pallas kernels, grads_call(): pl.pallas_call(grads_kernel, grid_spec=pltpu.PrefetchScalarGridSpec(num_s...  27.2 us
    all_to_all x2, starting transfers between devices, exchange(): return lax.all_to_all(value, axis, split_axis=0, concat_axis=0, tiled=True)  13.8 us
    ppermute x5, waiting for transfers between devices, swap(): return lax.ppermute(value, 'hidden', PAIRS)  13.4 us
    ppermute x7, starting transfers between devices, shards(): lax.ppermute(own_square, 'hidden', [(i, i ^ turn) for i in range(8)])  8.65 us
    reduce_scatter x1, waiting for transfers between devices, shards(): attn = lax.psum_scatter(part, 'hidden', scatter_dimension=0, tiled=True)[0]  7.99 us
  transfers between devices with their start and end apart: 18, of which 4 were waited for; matrix products, arithmetic and copies ran while one was open for 11% of the time, Pallas kernels for 7%

profile of v6, /device:TPU:6, one launch (start us, length us, event | category | flops | bytes accessed | tf_op | source)
XLA Modules:
  0.0 369.9 jit_solution(17866527288759581729)
XLA Ops:
  7.3 3.5 fusion.75
  10.8 2.3 convolution_convert_fusion.2
  13.1 2.2 fusion.10
  16.4 3.0 multiply_convert_fusion.1
  19.5 7.6 %all-to-all-start = ((bf16[16,80,1024]{2,1,0:T(8,128)(2,1)}), bf16[16,80,1024]{2,1,0:T(8,128)(2,1)}, u32[]{:S(2)}, u32[]{:S(2)}) async-start(bf16[16,80,1024]{2,1,0:T(8,128)(2,1)} %bitcast.97), calls=%async_computation.1 | async-start | bytes 5242880 | tf_op jit(solution)/shard_map/all_to_all | solution.py:262
  29.6 0.7 select_reduce_fusion
  31.1 0.7 select_reduce_fusion.3
  31.8 3.0 fusion.80
  34.8 2.6 fusion.1
  37.4 2.5 fusion.2
  40.0 4.6 %multiply_convert_fusion = bf16[2560,1024]{1,0:T(8,128)(2,1)} fusion(pred[2560,384]{1,0:T(32,128)(4,1)S(1)} %bitcast_compare_fusion.1, f32[2560]{0:T(1024)S(1)} %mul.75, bf16[384,2048]{1,0:T(8,128)(2,1)S(1)} %copy-done, s32[]{:T(128)S(6)} %select_n.111), kind=kOutput, calls=%fused_computation.1 | convolution fusion | flops 2018508800 | bytes 7024644 | tf_op jit(solution)/shard_map/dot_general | solution.py:34
  44.6 8.0 %reduce-scatter.4.cloned.1.call-done = bf16[1,384,256]{2,1,0:T(8,128)(2,1)} async-done(((bf16[8,384,256]{2,1,0:T(8,128)(2,1)}), bf16[1,384,256]{2,1,0:T(8,128)(2,1)}) %reduce-scatter.4.cloned.1.call-update) | async-done | bytes 196624 | tf_op jit(solution)/shard_map/reduce_scatter | solution.py:287
  52.6 1.2 multiply_reduce_fusion
  53.8 3.0 collective-permute-start.9
  58.0 2.1 collective-permute-start.6
  60.1 1.0 collective-permute-start.5
  61.1 1.3 collective-permute-start.4
  62.4 0.8 dynamic_slice.23
  63.3 0.9 bitcast_compare_fusion
  64.7 2.3 convolution_convert_fusion
  67.1 33.2 %all_to_all.25 = bf16[16,240,256]{2,1,0:T(8,128)(2,1)} all-to-all(bf16[16,240,256]{2,1,0:T(8,128)(2,1)S(1)} %bitcast.101), channel_id=1, replica_groups=mesh['group'=16,'hidden'=8] {'group'}, dimensions={0} | all-to-all | bytes 3932160 | tf_op jit(solution)/shard_map/all_to_all | solution.py:262
  100.4 65.2 %all_to_all.26.refs_2_ = bf16[16,160,1024]{2,1,0:T(8,128)(2,1)S(1)} all-to-all(bf16[16,160,1024]{2,1,0:T(8,128)(2,1)} %bitcast.95), channel_id=1, replica_groups=mesh['group'=16,'hidden'=8] {'group'}, dimensions={0} | all-to-all | bytes 10485760 | tf_op jit(solution)/shard_map/all_to_all | solution.py:262
  165.5 2.2 copy-done.2
  168.3 13.2 %collective-permute-done.10.refs_1_ = bf16[16,80,1024]{2,1,0:T(8,128)(2,1)} collective-permute-done((bf16[16,80,1024]{2,1,0:T(8,128)(2,1)}, bf16[16,80,1024]{2,1,0:T(8,128)(2,1)}, u32[]{:S(2)}, u32[]{:S(2)}) %collective-permute-start.10) | collective-permute-done | bytes 2621472 | tf_op jit(solution)/shard_map/ppermute | solution.py:266
  181.7 38.5 %expert_rows.1 = (bf16[8,16,240,256]{3,2,1,0:T(8,128)(2,1)}, bf16[16,240,128]{2,1,0:T(8,128)(2,1)}, bf16[16,240,256]{2,1,0:T(8,128)(2,1)}, bf16[16,240,1024]{2,1,0:T(8,128)(2,1)}) custom-call(s32[16]{0:T(128)} %get-tuple-element.40.order_ref, s32[16]{0:T(128)} %get-tuple-element.41.expert_ref, s32[16]{0:T(128)} %get-tuple-element.42.fresh_ref, ...), custom_call_target="tpu_custom_call" | custom-call | flops 18119393280 | bytes 83886080 | tf_op jit(solution)/shard_map/expert_rows/pallas_call | solution.py:119
  220.2 95.8 %all_to_all.27 = bf16[16,240,1024]{2,1,0:T(8,128)(2,1)} all-to-all(bf16[16,240,1024]{2,1,0:T(8,128)(2,1)} %get-tuple-element.55), channel_id=1, replica_groups=mesh['group'=16,'hidden'=8] {'group'}, dimensions={0} | all-to-all | bytes 15728640 | tf_op jit(solution)/shard_map/all_to_all | solution.py:262
  316.1 6.3 %all-to-all-start.4 = ((bf16[16,240,256]{2,1,0:T(8,128)(2,1)}), bf16[16,240,256]{2,1,0:T(8,128)(2,1)S(1)}, u32[]{:S(2)}, u32[]{:S(2)}) async-start(bf16[16,240,256]{2,1,0:T(8,128)(2,1)} %bitcast.98), calls=%async_computation.6 | async-start | bytes 3932160 | tf_op jit(solution)/shard_map/all_to_all | solution.py:262
  322.4 7.3 %convolution_convert_fusion.1 = bf16[384,1024]{1,0:T(8,128)(2,1)S(1)} fusion(bf16[384,3840]{1,0:T(8,128)(2,1)} %get-tuple-element.58, bf16[3840,1024]{1,0:T(8,128)(2,1)} %bitcast.94), kind=kOutput, calls=%fused_computation.24 | convolution fusion | flops 3020292096 | bytes 11599872 | tf_op jit(solution)/shard_map/dot_general | solution.py:34
  329.7 0.9 copy.76
  330.7 27.2 %weight_grads.1 = (bf16[8,96,2048]{2,1,0:T(8,128)(2,1)}, bf16[8,96,2048]{2,1,0:T(8,128)(2,1)}, bf16[8,96,2048]{2,1,0:T(8,128)(2,1)}) custom-call(s32[24]{0:T(128)} %get-tuple-element.59.chunk_ref, s32[24]{0:T(128)} %get-tuple-element.60.expert_ref, s32[24]{0:T(128)} %get-tuple-element.61.real_ref, s32[24]{0:T(128)} %get-tuple-element.62.last_ref, ...), custom_call_target="tpu_custom_call" | custom-call | flops 6039797760 | bytes 47185920 | tf_op jit(solution)/shard_map/weight_grads/pallas_call | solution.py:194
  357.9 2.9 fusion.81
  360.8 2.6 fusion.17
  (86 shorter events, 7.4 us)
Async XLA Ops:
  7.2 9.3 %copy-start = (bf16[384,2048]{1,0:T(8,128)(2,1)S(1)}, bf16[384,2048]{1,0:T(8,128)(2,1)}, u32[]{:S(2)}) copy-start(bf16[384,2048]{1,0:T(8,128)(2,1)} %param.25) | copy-start | bytes 4718596
  7.2 45.4 %reduce-scatter.4.cloned.1.call-start = ((), (), s32[]{:S(2)}) async-start(), calls=%async_computation.8 | async-start | bytes 1769472 | tf_op jit(solution)/shard_map/reduce_scatter | solution.py:287
  10.8 2.4 copy-start.8
  13.1 2.3 copy-start.5
  13.1 2.5 copy-start.6
  19.5 8.3 %copy-start.7 = (s32[16,16]{1,0:T(8,128)S(1)}, s32[16,16]{1,0:T(8,128)}, u32[]{:S(2)}) copy-start(s32[16,16]{1,0:T(8,128)} %param.24) | copy-start | bytes 3076
  19.5 47.6 %all-to-all-start = ((bf16[16,80,1024]{2,1,0:T(8,128)(2,1)}), bf16[16,80,1024]{2,1,0:T(8,128)(2,1)}, u32[]{:S(2)}, u32[]{:S(2)}) async-start(bf16[16,80,1024]{2,1,0:T(8,128)(2,1)} %bitcast.97), calls=%async_computation.1 | async-start | bytes 5242880 | tf_op jit(solution)/shard_map/all_to_all | solution.py:262
  27.0 154.7 %all-gather.3.cloned.1.call-start = ((), (), s32[]{:S(2)}) async-start(), calls=%async_computation.11 | async-start | bytes 17694720 | tf_op jit(solution)/shard_map/all_gather | solution.py:350
  27.1 25.5 %collective-permute-start = (bf16[8,96,2048]{2,1,0:T(8,128)(2,1)}, bf16[8,96,2048]{2,1,0:T(8,128)(2,1)}, u32[]{:S(2)}, u32[]{:S(2)}) collective-permute-start(bf16[8,96,2048]{2,1,0:T(8,128)(2,1)} %bitcast.113), channel_id=1, source_target_pairs={{0,1},{1,0},{2,3},{3,2},{4,5},{5,4},{6,7},{7,6},{8,9},{9,8},{10,11... | collective-permute-start | bytes 9437192 | tf_op jit(solution)/shard_map/ppermute | solution.py:266
  27.2 25.4 %collective-permute-start.1 = (bf16[8,96,2048]{2,1,0:T(8,128)(2,1)}, bf16[8,96,2048]{2,1,0:T(8,128)(2,1)}, u32[]{:S(2)}, u32[]{:S(2)}) collective-permute-start(bf16[8,96,2048]{2,1,0:T(8,128)(2,1)} %bitcast.115), channel_id=1, source_target_pairs={{0,1},{1,0},{2,3},{3,2},{4,5},{5,4},{6,7},{7,6},{8,9},{9,8},{10,11... | collective-permute-start | bytes 9437192 | tf_op jit(solution)/shard_map/ppermute | solution.py:266
  27.7 24.9 %collective-permute-start.2 = (bf16[8,96,2048]{2,1,0:T(8,128)(2,1)}, bf16[8,96,2048]{2,1,0:T(8,128)(2,1)}, u32[]{:S(2)}, u32[]{:S(2)}) collective-permute-start(bf16[8,96,2048]{2,1,0:T(8,128)(2,1)} %refs_6_), channel_id=1, source_target_pairs={{0,1},{1,0},{2,3},{3,2},{4,5},{5,4},{6,7},{7,6},{8,9},{9,8},{10,11... | collective-permute-start | bytes 9437192 | tf_op jit(solution)/shard_map/ppermute | solution.py:266
  53.8 7.4 %collective-permute-start.9 = (f32[384]{0:T(512)S(1)}, f32[384]{0:T(512)S(1)}, u32[]{:S(2)}, u32[]{:S(2)}) collective-permute-start(f32[384]{0:T(512)S(1)} %multiply_reduce_fusion), channel_id=1, source_target_pairs={{0,7},{1,6},{2,5},{3,4},{4,3},{5,2},{6,1},{7,0},{8,15},{9,14},{10,... | collective-permute-start | bytes 4616 | tf_op jit(solution)/shard_map/ppermute | solution.py:344
  56.7 5.7 %collective-permute-start.8 = (f32[384]{0:T(512)S(1)}, f32[384]{0:T(512)S(1)}, u32[]{:S(2)}, u32[]{:S(2)}) collective-permute-start(f32[384]{0:T(512)S(1)} %multiply_reduce_fusion), channel_id=1, source_target_pairs={{0,6},{1,7},{2,4},{3,5},{4,2},{5,3},{6,0},{7,1},{8,14},{9,15},{10,... | collective-permute-start | bytes 4616 | tf_op jit(solution)/shard_map/ppermute | solution.py:344
  57.4 6.7 %collective-permute-start.7 = (f32[384]{0:T(512)S(1)}, f32[384]{0:T(512)S(1)}, u32[]{:S(2)}, u32[]{:S(2)}) collective-permute-start(f32[384]{0:T(512)S(1)} %multiply_reduce_fusion), channel_id=1, source_target_pairs={{0,5},{1,4},{2,7},{3,6},{4,1},{5,0},{6,3},{7,2},{8,13},{9,12},{10,... | collective-permute-start | bytes 4616 | tf_op jit(solution)/shard_map/ppermute | solution.py:344
  58.0 6.1 %collective-permute-start.6 = (f32[384]{0:T(512)S(1)}, f32[384]{0:T(512)S(1)}, u32[]{:S(2)}, u32[]{:S(2)}) collective-permute-start(f32[384]{0:T(512)S(1)} %multiply_reduce_fusion), channel_id=1, source_target_pairs={{0,4},{1,5},{2,6},{3,7},{4,0},{5,1},{6,2},{7,3},{8,12},{9,13},{10,... | collective-permute-start | bytes 4616 | tf_op jit(solution)/shard_map/ppermute | solution.py:344
  60.1 4.1 %collective-permute-start.5 = (f32[384]{0:T(512)S(1)}, f32[384]{0:T(512)S(1)}, u32[]{:S(2)}, u32[]{:S(2)}) collective-permute-start(f32[384]{0:T(512)S(1)} %multiply_reduce_fusion), channel_id=1, source_target_pairs={{0,3},{1,2},{2,1},{3,0},{4,7},{5,6},{6,5},{7,4},{8,11},{9,10},{10,... | collective-permute-start | bytes 4616 | tf_op jit(solution)/shard_map/ppermute | solution.py:344
  61.1 3.6 collective-permute-start.4
  62.4 2.3 collective-permute-start.3
  100.3 215.7 %reduce-scatter.6.cloned.1.call-start = ((), (), s32[]{:S(2)}) async-start(), calls=%async_computation.9 | async-start | bytes 17694720 | tf_op jit(solution)/shard_map/reduce_scatter | solution.py:356
  165.5 2.2 copy-start.2
  167.8 13.9 %collective-permute-start.11 = (bf16[16,160,1024]{2,1,0:T(8,128)(2,1)S(1)}, bf16[16,160,1024]{2,1,0:T(8,128)(2,1)}, u32[]{:S(2)}, u32[]{:S(2)}) collective-permute-start(bf16[16,160,1024]{2,1,0:T(8,128)(2,1)S(1)} %all_to_all.26.refs_2_), channel_id=1, source_target_pairs={{0,1},{1,0},{2,3},{3,2},{4,5},{5,4},{6,7},{7,6},{8,9},{9,8},{10,11... | collective-permute-start | bytes 15728648 | tf_op jit(solution)/shard_map/ppermute | solution.py:266
  167.8 13.7 %collective-permute-start.10 = (bf16[16,80,1024]{2,1,0:T(8,128)(2,1)}, bf16[16,80,1024]{2,1,0:T(8,128)(2,1)}, u32[]{:S(2)}, u32[]{:S(2)}) collective-permute-start(bf16[16,80,1024]{2,1,0:T(8,128)(2,1)} %all-to-all-done.refs_0_), channel_id=1, source_target_pairs={{0,1},{1,0},{2,3},{3,2},{4,5},{5,4},{6,7},{7,6},{8,9},{9,8},{10,11... | collective-permute-start | bytes 7864328 | tf_op jit(solution)/shard_map/ppermute | solution.py:266
  316.1 41.8 %all-to-all-start.4 = ((bf16[16,240,256]{2,1,0:T(8,128)(2,1)}), bf16[16,240,256]{2,1,0:T(8,128)(2,1)S(1)}, u32[]{:S(2)}, u32[]{:S(2)}) async-start(bf16[16,240,256]{2,1,0:T(8,128)(2,1)} %bitcast.98), calls=%async_computation.6 | async-start | bytes 3932160 | tf_op jit(solution)/shard_map/all_to_all | solution.py:262
  322.3 41.1 %reduce-scatter.8.cloned.1.call-start = ((), (), s32[]{:S(2)}) async-start(), calls=%async_computation.10 | async-start | bytes 983040 | tf_op jit(solution)/shard_map/reduce_scatter | solution.py:365
  357.9 3.0 copy-start.3
  357.9 3.0 copy-start.4
  357.9 5.5 %copy-start.1 = (bf16[384,2048]{1,0:T(8,128)(2,1)S(1)}, bf16[384,2048]{1,0:T(8,128)(2,1)}, u32[]{:S(2)}) copy-start(bf16[384,2048]{1,0:T(8,128)(2,1)} %param.25) | copy-start | bytes 4718596
Sparse Core Ops, SparseCore 0:
  15.4 37.1 reduce-scatter.3
  100.4 81.0 all-gather.2
  220.4 86.7 reduce-scatter.5
  330.8 22.0 reduce-scatter.7

commit v7 on v6

--- a/solution.py
+++ b/solution.py
@@ -84,24 +84,25 @@
         axis=0,
     )
     d_act = mm(g, wdp[...], NT)
-    hidden = []
+    acts, hidden = [], []
     for i in range(2):
         gate = pre[:, 2 * i * PAD : (2 * i + 1) * PAD]
         up = pre[:, (2 * i + 1) * PAD : (2 * i + 2) * PAD]
         d_part = d_act[:, i * PAD : (i + 1) * PAD]
         sig = jax.nn.sigmoid(gate)
         swish = gate * sig
-        if i == 0:
-            act = (swish * up).astype(bf16)
+        acts.append((swish * up).astype(bf16))
         hidden.append((d_part * up * sig * (1.0 + gate * (1.0 - sig))).astype(bf16))
         hidden.append((d_part * swish).astype(bf16))
-    act_ref[0] = act
+    act_ref[0] = acts[0]
     dgu_ref[0, :, :PAD] = hidden[0]
     dgu_ref[0, :, PAD:] = hidden[1]
-    for half, base in enumerate((core * 4, 4 - core * 4)):
-        for block in range(4):
-            col = half * HALF + block * COLS
-            out_ref[base + block, 0] = mm(act, wdp[:PAD, col : col + COLS], NN).astype(bf16)
+    act = jnp.concatenate(acts, axis=1)
+    for block in range(4):
+        half = core if block < 2 else 1 - core
+        col = half * HALF + (2 * (block % 2) + core) * COLS
+        col = pl.ds(pl.multiple_of(col, COLS), COLS)
+        out_ref[block, 0] = mm(act, wdp[:, col], NN).astype(bf16)
     both = jnp.concatenate(hidden, axis=1)
     for block in range(4):
         col = pl.ds(pl.multiple_of((2 * block + core) * COLS, COLS), COLS)
@@ -122,11 +123,16 @@
             num_scalar_prefetch=4,
             grid=(FETCH,),
             in_specs=[cols8, *halves, *[weight] * 6],
-            out_specs=[cols8, flat(CAP, PAD), flat(CAP, 2 * PAD), flat(CAP, HALF)],
+            out_specs=[
+                pl.BlockSpec((4, 1, CAP, COLS), lambda i, o, e, n, c: (0, o[i], 0, 0)),
+                flat(CAP, PAD),
+                flat(CAP, 2 * PAD),
+                flat(CAP, HALF),
+            ],
             scratch_shapes=[pltpu.VMEM((4 * PAD, D), bf16), pltpu.VMEM((2 * PAD, D), bf16)],
         ),
         out_shape=[
-            jax.ShapeDtypeStruct((8, FETCH, CAP, COLS), bf16),
+            jax.ShapeDtypeStruct((4, FETCH, CAP, COLS), bf16),
             jax.ShapeDtypeStruct((FETCH, CAP, PAD), bf16),
             jax.ShapeDtypeStruct((FETCH, CAP, 2 * PAD), bf16),
             jax.ShapeDtypeStruct((FETCH, CAP, HALF), bf16),
@@ -353,7 +359,9 @@
 
     out_rows, act, dgu, d_half = rows_call(scalars, x_rows, g_parts, weights)
 
-    out_share = lax.psum_scatter(out_rows, "hidden", scatter_dimension=0, tiled=True)[0]
+    out_share = lax.psum_scatter(
+        out_rows, "hidden", scatter_dimension=0, tiled=True, axis_index_groups=Z_GROUPS
+    )[0]
     d_back = exchange(d_half)
     grad_gate, grad_up, grad_down = grads_call(
         *tables, core_arr, x_rows, g_parts, after(act, d_back), dgu

time: 371 us -> 373 us (level)
  transfers between devices with their start and end apart: 18 -> 18, of which waited for: 4 -> 3; matrix products, arithmetic and copies ran while one was open for 11% -> 11% of each run, Pallas kernels for 7% -> 7%
where the time goes in v7:
time: 373 us; the launch traced here: 371 us
  blocking collectives  192 us (51%)
  Pallas kernels  66.5 us (18%)
  matrix products  38.9 us (10%)
  waiting for transfers between devices  24.2 us (6%)
  starting transfers between devices  23.3 us (6%)
  between operations  14.2 us (4%)
  other arithmetic  6.49 us (2%)
  local copies, waits for them, and re-layouts  4.62 us (1%)
    all_to_all x3, blocking collectives, exchange(): return lax.all_to_all(value, axis, split_axis=0, concat_axis=0, tiled=True)  192 us
    pallas_call x1, Pallas kernels, rows_call(): pl.pallas_call(rows_kernel, grid_spec=pltpu.PrefetchScalarGridSpec(num_sc...  39.7 us
    dot_general x10, matrix products, mm(): return lax.dot_general(a, b, dims, preferred_element_type=f32)  31 us
    pallas_call x1, Pallas kernels, grads_call(): pl.pallas_call(grads_kernel, grid_spec=pltpu.PrefetchScalarGridSpec(num_s...  26.9 us
    all_to_all x2, starting transfers between devices, exchange(): return lax.all_to_all(value, axis, split_axis=0, concat_axis=0, tiled=True)  13.8 us
    ppermute x5, waiting for transfers between devices, swap(): return lax.ppermute(value, 'hidden', PAIRS)  13.4 us
    reduce_scatter x1, waiting for transfers between devices, shards(): attn = lax.psum_scatter(part, 'hidden', scatter_dimension=0, tiled=True)[0]  10.7 us
    ppermute x7, starting transfers between devices, shards(): lax.ppermute(own_square, 'hidden', [(i, i ^ turn) for i in range(8)])  8.13 us
  transfers between devices with their start and end apart: 18, of which 3 were waited for; matrix products, arithmetic and copies ran while one was open for 11% of the time, Pallas kernels for 7%

profile of v7, /device:TPU:6, one launch (start us, length us, event | category | flops | bytes accessed | tf_op | source)
XLA Modules:
  0.0 370.6 jit_solution(5694920189239553328)
XLA Ops:
  7.3 3.5 fusion.75
  10.8 2.3 convolution_convert_fusion.2
  13.1 2.2 fusion.10
  16.4 3.0 multiply_convert_fusion.1
  19.5 7.6 %all-to-all-start = ((bf16[16,80,1024]{2,1,0:T(8,128)(2,1)}), bf16[16,80,1024]{2,1,0:T(8,128)(2,1)}, u32[]{:S(2)}, u32[]{:S(2)}) async-start(bf16[16,80,1024]{2,1,0:T(8,128)(2,1)} %bitcast.97), calls=%async_computation.1 | async-start | bytes 5242880 | tf_op jit(solution)/shard_map/all_to_all | solution.py:268
  28.9 0.6 select_reduce_fusion.7
  29.5 0.7 select_reduce_fusion
  31.1 0.7 select_reduce_fusion.3
  31.8 3.0 fusion.80
  34.7 2.6 fusion.1
  37.4 2.5 fusion.2
  39.9 4.6 %multiply_convert_fusion = bf16[2560,1024]{1,0:T(8,128)(2,1)} fusion(pred[2560,384]{1,0:T(32,128)(4,1)S(1)} %bitcast_compare_fusion.1, f32[2560]{0:T(1024)S(1)} %mul.75, bf16[384,2048]{1,0:T(8,128)(2,1)S(1)} %copy-done, s32[]{:T(128)S(6)} %select_n.111), kind=kOutput, calls=%fused_computation.1 | convolution fusion | flops 2018508800 | bytes 7024644 | tf_op jit(solution)/shard_map/dot_general | solution.py:34
  44.5 10.7 %reduce-scatter.4.cloned.1.call-done = bf16[1,384,256]{2,1,0:T(8,128)(2,1)} async-done(((bf16[8,384,256]{2,1,0:T(8,128)(2,1)}), bf16[1,384,256]{2,1,0:T(8,128)(2,1)}) %reduce-scatter.4.cloned.1.call-update) | async-done | bytes 196624 | tf_op jit(solution)/shard_map/reduce_scatter | solution.py:293
  55.2 1.2 multiply_reduce_fusion
  56.8 0.6 collective-permute-start.8
  58.0 4.6 %collective-permute-start.6 = (f32[384]{0:T(512)S(1)}, f32[384]{0:T(512)S(1)}, u32[]{:S(2)}, u32[]{:S(2)}) collective-permute-start(f32[384]{0:T(512)S(1)} %multiply_reduce_fusion), channel_id=1, source_target_pairs={{0,4},{1,5},{2,6},{3,7},{4,0},{5,1},{6,2},{7,3},{8,12},{9,13},{10,... | collective-permute-start | bytes 4616 | tf_op jit(solution)/shard_map/ppermute | solution.py:350
  62.7 1.8 collective-permute-start.3
  64.5 0.8 dynamic_slice.23
  65.4 0.9 bitcast_compare_fusion
  66.3 2.3 convolution_convert_fusion
  68.6 31.7 %all_to_all.25 = bf16[16,240,256]{2,1,0:T(8,128)(2,1)} all-to-all(bf16[16,240,256]{2,1,0:T(8,128)(2,1)S(1)} %bitcast.101), channel_id=1, replica_groups=mesh['group'=16,'hidden'=8] {'group'}, dimensions={0} | all-to-all | bytes 3932160 | tf_op jit(solution)/shard_map/all_to_all | solution.py:268
  100.4 65.2 %all_to_all.26.refs_2_ = bf16[16,160,1024]{2,1,0:T(8,128)(2,1)S(1)} all-to-all(bf16[16,160,1024]{2,1,0:T(8,128)(2,1)} %bitcast.95), channel_id=1, replica_groups=mesh['group'=16,'hidden'=8] {'group'}, dimensions={0} | all-to-all | bytes 10485760 | tf_op jit(solution)/shard_map/all_to_all | solution.py:268
  165.5 2.3 copy-done.2
  168.4 13.2 %collective-permute-done.10.refs_1_ = bf16[16,80,1024]{2,1,0:T(8,128)(2,1)} collective-permute-done((bf16[16,80,1024]{2,1,0:T(8,128)(2,1)}, bf16[16,80,1024]{2,1,0:T(8,128)(2,1)}, u32[]{:S(2)}, u32[]{:S(2)}) %collective-permute-start.10) | collective-permute-done | bytes 2621472 | tf_op jit(solution)/shard_map/ppermute | solution.py:272
  181.8 39.7 %expert_rows.1 = (bf16[4,16,240,256]{3,2,1,0:T(8,128)(2,1)}, bf16[16,240,128]{2,1,0:T(8,128)(2,1)}, bf16[16,240,256]{2,1,0:T(8,128)(2,1)}, bf16[16,240,1024]{2,1,0:T(8,128)(2,1)}) custom-call(s32[16]{0:T(128)} %get-tuple-element.40.order_ref, s32[16]{0:T(128)} %get-tuple-element.41.expert_ref, s32[16]{0:T(128)} %get-tuple-element.42.fresh_ref, ...), custom_call_target="tpu_custom_call" | custom-call | flops 18119393280 | bytes 83886080 | tf_op jit(solution)/shard_map/expert_rows/pallas_call | solution.py:120
  221.5 95.6 %all_to_all.27 = bf16[16,240,1024]{2,1,0:T(8,128)(2,1)} all-to-all(bf16[16,240,1024]{2,1,0:T(8,128)(2,1)} %get-tuple-element.55), channel_id=1, replica_groups=mesh['group'=16,'hidden'=8] {'group'}, dimensions={0} | all-to-all | bytes 15728640 | tf_op jit(solution)/shard_map/all_to_all | solution.py:268
  317.0 6.3 %all-to-all-start.4 = ((bf16[16,240,256]{2,1,0:T(8,128)(2,1)}), bf16[16,240,256]{2,1,0:T(8,128)(2,1)S(1)}, u32[]{:S(2)}, u32[]{:S(2)}) async-start(bf16[16,240,256]{2,1,0:T(8,128)(2,1)} %bitcast.98), calls=%async_computation.6 | async-start | bytes 3932160 | tf_op jit(solution)/shard_map/all_to_all | solution.py:268
  323.3 7.3 %convolution_convert_fusion.1 = bf16[384,1024]{1,0:T(8,128)(2,1)S(1)} fusion(bf16[384,3840]{1,0:T(8,128)(2,1)} %get-tuple-element.58, bf16[3840,1024]{1,0:T(8,128)(2,1)} %bitcast.94), kind=kOutput, calls=%fused_computation.24 | convolution fusion | flops 3020292096 | bytes 11599872 | tf_op jit(solution)/shard_map/dot_general | solution.py:34
  330.7 1.0 copy.76
  331.7 26.9 %weight_grads.1 = (bf16[8,96,2048]{2,1,0:T(8,128)(2,1)}, bf16[8,96,2048]{2,1,0:T(8,128)(2,1)}, bf16[8,96,2048]{2,1,0:T(8,128)(2,1)}) custom-call(s32[24]{0:T(128)} %get-tuple-element.59.chunk_ref, s32[24]{0:T(128)} %get-tuple-element.60.expert_ref, s32[24]{0:T(128)} %get-tuple-element.61.real_ref, s32[24]{0:T(128)} %get-tuple-element.62.last_ref, ...), custom_call_target="tpu_custom_call" | custom-call | flops 6039797760 | bytes 47185920 | tf_op jit(solution)/shard_map/weight_grads/pallas_call | solution.py:200
  358.6 2.9 fusion.81
  361.5 2.6 fusion.17
  (86 shorter events, 5.9 us)
Async XLA Ops:
  7.2 9.3 %copy-start = (bf16[384,2048]{1,0:T(8,128)(2,1)S(1)}, bf16[384,2048]{1,0:T(8,128)(2,1)}, u32[]{:S(2)}) copy-start(bf16[384,2048]{1,0:T(8,128)(2,1)} %param.25) | copy-start | bytes 4718596
  7.2 48.0 %reduce-scatter.4.cloned.1.call-start = ((), (), s32[]{:S(2)}) async-start(), calls=%async_computation.8 | async-start | bytes 1769472 | tf_op jit(solution)/shard_map/reduce_scatter | solution.py:293
  10.8 2.4 copy-start.8
  13.1 2.3 copy-start.5
  13.1 2.5 copy-start.6
  19.5 8.3 %copy-start.7 = (s32[16,16]{1,0:T(8,128)S(1)}, s32[16,16]{1,0:T(8,128)}, u32[]{:S(2)}) copy-start(s32[16,16]{1,0:T(8,128)} %param.24) | copy-start | bytes 3076
  19.5 49.1 %all-to-all-start = ((bf16[16,80,1024]{2,1,0:T(8,128)(2,1)}), bf16[16,80,1024]{2,1,0:T(8,128)(2,1)}, u32[]{:S(2)}, u32[]{:S(2)}) async-start(bf16[16,80,1024]{2,1,0:T(8,128)(2,1)} %bitcast.97), calls=%async_computation.1 | async-start | bytes 5242880 | tf_op jit(solution)/shard_map/all_to_all | solution.py:268
  27.0 154.8 %all-gather.3.cloned.1.call-start = ((), (), s32[]{:S(2)}) async-start(), calls=%async_computation.11 | async-start | bytes 17694720 | tf_op jit(solution)/shard_map/all_gather | solution.py:356
  27.1 28.1 %collective-permute-start = (bf16[8,96,2048]{2,1,0:T(8,128)(2,1)}, bf16[8,96,2048]{2,1,0:T(8,128)(2,1)}, u32[]{:S(2)}, u32[]{:S(2)}) collective-permute-start(bf16[8,96,2048]{2,1,0:T(8,128)(2,1)} %bitcast.113), channel_id=1, source_target_pairs={{0,1},{1,0},{2,3},{3,2},{4,5},{5,4},{6,7},{7,6},{8,9},{9,8},{10,11... | collective-permute-start | bytes 9437192 | tf_op jit(solution)/shard_map/ppermute | solution.py:272
  27.2 28.0 %collective-permute-start.1 = (bf16[8,96,2048]{2,1,0:T(8,128)(2,1)}, bf16[8,96,2048]{2,1,0:T(8,128)(2,1)}, u32[]{:S(2)}, u32[]{:S(2)}) collective-permute-start(bf16[8,96,2048]{2,1,0:T(8,128)(2,1)} %bitcast.115), channel_id=1, source_target_pairs={{0,1},{1,0},{2,3},{3,2},{4,5},{5,4},{6,7},{7,6},{8,9},{9,8},{10,11... | collective-permute-start | bytes 9437192 | tf_op jit(solution)/shard_map/ppermute | solution.py:272
  27.7 27.5 %collective-permute-start.2 = (bf16[8,96,2048]{2,1,0:T(8,128)(2,1)}, bf16[8,96,2048]{2,1,0:T(8,128)(2,1)}, u32[]{:S(2)}, u32[]{:S(2)}) collective-permute-start(bf16[8,96,2048]{2,1,0:T(8,128)(2,1)} %refs_6_), channel_id=1, source_target_pairs={{0,1},{1,0},{2,3},{3,2},{4,5},{5,4},{6,7},{7,6},{8,9},{9,8},{10,11... | collective-permute-start | bytes 9437192 | tf_op jit(solution)/shard_map/ppermute | solution.py:272
  56.3 6.3 %collective-permute-start.9 = (f32[384]{0:T(512)S(1)}, f32[384]{0:T(512)S(1)}, u32[]{:S(2)}, u32[]{:S(2)}) collective-permute-start(f32[384]{0:T(512)S(1)} %multiply_reduce_fusion), channel_id=1, source_target_pairs={{0,7},{1,6},{2,5},{3,4},{4,3},{5,2},{6,1},{7,0},{8,15},{9,14},{10,... | collective-permute-start | bytes 4616 | tf_op jit(solution)/shard_map/ppermute | solution.py:350
  56.8 5.9 %collective-permute-start.8 = (f32[384]{0:T(512)S(1)}, f32[384]{0:T(512)S(1)}, u32[]{:S(2)}, u32[]{:S(2)}) collective-permute-start(f32[384]{0:T(512)S(1)} %multiply_reduce_fusion), channel_id=1, source_target_pairs={{0,6},{1,7},{2,4},{3,5},{4,2},{5,3},{6,0},{7,1},{8,14},{9,15},{10,... | collective-permute-start | bytes 4616 | tf_op jit(solution)/shard_map/ppermute | solution.py:350
  57.4 8.8 %collective-permute-start.7 = (f32[384]{0:T(512)S(1)}, f32[384]{0:T(512)S(1)}, u32[]{:S(2)}, u32[]{:S(2)}) collective-permute-start(f32[384]{0:T(512)S(1)} %multiply_reduce_fusion), channel_id=1, source_target_pairs={{0,5},{1,4},{2,7},{3,6},{4,1},{5,0},{6,3},{7,2},{8,13},{9,12},{10,... | collective-permute-start | bytes 4616 | tf_op jit(solution)/shard_map/ppermute | solution.py:350
  58.0 8.2 %collective-permute-start.6 = (f32[384]{0:T(512)S(1)}, f32[384]{0:T(512)S(1)}, u32[]{:S(2)}, u32[]{:S(2)}) collective-permute-start(f32[384]{0:T(512)S(1)} %multiply_reduce_fusion), channel_id=1, source_target_pairs={{0,4},{1,5},{2,6},{3,7},{4,0},{5,1},{6,2},{7,3},{8,12},{9,13},{10,... | collective-permute-start | bytes 4616 | tf_op jit(solution)/shard_map/ppermute | solution.py:350
  62.6 3.6 collective-permute-start.5
  62.6 3.6 collective-permute-start.4
  62.7 3.6 collective-permute-start.3
  100.3 216.7 %reduce-scatter.6.cloned.1.call-start = ((), (), s32[]{:S(2)}) async-start(), calls=%async_computation.9 | async-start | bytes 9830400 | tf_op jit(solution)/shard_map/reduce_scatter | solution.py:362
  165.5 2.3 copy-start.2
  167.8 13.9 %collective-permute-start.11 = (bf16[16,160,1024]{2,1,0:T(8,128)(2,1)S(1)}, bf16[16,160,1024]{2,1,0:T(8,128)(2,1)}, u32[]{:S(2)}, u32[]{:S(2)}) collective-permute-start(bf16[16,160,1024]{2,1,0:T(8,128)(2,1)S(1)} %all_to_all.26.refs_2_), channel_id=1, source_target_pairs={{0,1},{1,0},{2,3},{3,2},{4,5},{5,4},{6,7},{7,6},{8,9},{9,8},{10,11... | collective-permute-start | bytes 15728648 | tf_op jit(solution)/shard_map/ppermute | solution.py:272
  167.8 13.7 %collective-permute-start.10 = (bf16[16,80,1024]{2,1,0:T(8,128)(2,1)}, bf16[16,80,1024]{2,1,0:T(8,128)(2,1)}, u32[]{:S(2)}, u32[]{:S(2)}) collective-permute-start(bf16[16,80,1024]{2,1,0:T(8,128)(2,1)} %all-to-all-done.refs_0_), channel_id=1, source_target_pairs={{0,1},{1,0},{2,3},{3,2},{4,5},{5,4},{6,7},{7,6},{8,9},{9,8},{10,11... | collective-permute-start | bytes 7864328 | tf_op jit(solution)/shard_map/ppermute | solution.py:272
  317.0 41.5 %all-to-all-start.4 = ((bf16[16,240,256]{2,1,0:T(8,128)(2,1)}), bf16[16,240,256]{2,1,0:T(8,128)(2,1)S(1)}, u32[]{:S(2)}, u32[]{:S(2)}) async-start(bf16[16,240,256]{2,1,0:T(8,128)(2,1)} %bitcast.98), calls=%async_computation.6 | async-start | bytes 3932160 | tf_op jit(solution)/shard_map/all_to_all | solution.py:268
  323.3 40.8 %reduce-scatter.8.cloned.1.call-start = ((), (), s32[]{:S(2)}) async-start(), calls=%async_computation.10 | async-start | bytes 983040 | tf_op jit(solution)/shard_map/reduce_scatter | solution.py:373
  358.6 3.0 copy-start.3
  358.6 3.0 copy-start.4
  358.6 5.5 %copy-start.1 = (bf16[384,2048]{1,0:T(8,128)(2,1)S(1)}, bf16[384,2048]{1,0:T(8,128)(2,1)}, u32[]{:S(2)}) copy-start(bf16[384,2048]{1,0:T(8,128)(2,1)} %param.25) | copy-start | bytes 4718596
Sparse Core Ops, SparseCore 0:
  15.4 39.6 reduce-scatter.3
  100.4 81.0 all-gather.2
  221.6 76.1 reduce-scatter.5
  331.8 22.1 reduce-scatter.7
